TPU v7x, 32 devices: a whole 2x2x4 slice. The times are simulated.
32 devices in a mesh: dp: 32 (over z, y, x, core).
Axes of the slice: x: 2, y: 2, z: 4, core: 2. Of those that a mesh axis runs over, the one named last changes fastest.
Arguments:
- inputs: bfloat16 [32, 1024, 768], P('dp'), may hold values from -6 to 6
- cotangent: bfloat16 [32, 1024, 768], P('dp'), may hold values from -6 to 6
- routes: int32 [32, 1024, 1], P('dp'), may hold values from 0 to 31; in each aligned block of 1024 rows (0 to 1023, 1024 to 2047, ..., all dimensions but the last counted through in order) at most 64 rows name the same one
- segments: int32 [32, 1024], P('dp'), may hold values from 0 to 7, never falling along the last dimension, each value on 1 to 512 neighbouring positions
- qkv_weight: float32 [768, 2304], P('dp'), may hold values from -0.21875 to 0.21875
- query_bias: float32 [768], P('dp'), may hold values from -1 to 1
- value_bias: float32 [768], P('dp'), may hold values from -0.5 to 0.5
- out_weight: float32 [768, 768], P('dp'), may hold values from -0.625 to 0.625
- out_bias: float32 [768], P('dp'), may hold values from -0.5 to 0.5
- attn_gain: float32 [768], P('dp'), may hold values from 0.5 to 1.5
- attn_shift: float32 [768], P('dp'), may hold values from -0.5 to 0.5
- moe_gain: float32 [768], P('dp'), may hold values from 0.5 to 1.5
- moe_shift: float32 [768], P('dp'), may hold values from -0.5 to 0.5
- router_weight: float32 [768, 32], P('dp'), may hold values from -0.15625 to 0.15625
- expert_in: float32 [32, 768, 3072], P('dp'), may hold values from -0.21875 to 0.21875
- expert_in_bias: float32 [32, 3072], P('dp'), may hold values from -0.5 to 0.5
- expert_out: float32 [32, 3072, 768], P('dp'), may hold values from -0.3125 to 0.3125
- expert_out_bias: float32 [32, 768], P('dp'), may hold values from -0.5 to 0.5
Outputs:
- output: bfloat16 [32, 1024, 768], P('dp')
- grad_inputs: float32 [32, 1024, 768], P('dp')
- grad_qkv_weight: float32 [768, 2304], P('dp')
- grad_query_bias: float32 [768], P('dp')
- grad_value_bias: float32 [768], P('dp')
- grad_out_weight: float32 [768, 768], P('dp')
- grad_out_bias: float32 [768], P('dp')
- grad_attn_gain: float32 [768], P('dp')
- grad_attn_shift: float32 [768], P('dp')
- grad_moe_gain: float32 [768], P('dp')
- grad_moe_shift: float32 [768], P('dp')
- grad_router_weight: float32 [768, 32], P('dp')
- grad_expert_in: float32 [32, 768, 3072], P('dp')
- grad_expert_in_bias: float32 [32, 3072], P('dp')
- grad_expert_out: float32 [32, 3072, 768], P('dp')
- grad_expert_out_bias: float32 [32, 768], P('dp')
Inputs may be any that keep to these rules, and one draw needn't show every extreme that they name: `routes`: each token names one expert; among the tokens of one device no expert is named more than 64 times, a bound that some block reaches. `segments`: document numbers never fall along a row; a document holds at most 512 tokens.
All inputs are finite; a program needn't handle non-finite values.
Results may differ from a plain program's by a relative error of at most 0.015.
Values may be sent and summed in bfloat16 or wider, within the bound.
No kernel may reach another device: no remote copies, remote signals or barrier semaphores. Data moves between devices by JAX's collectives and lax.ppermute only.
A program may use at most 384 MiB of HBM per device.

v0:
```python
import jax
import jax.numpy as jnp
from jax import lax
from jax.sharding import PartitionSpec as P

HEADS = 12
HEAD_DIM = 64


EPSILON = 1e-05
NEG_FILL = -1000000000.0
SQRT_HALF = 0.7071067811865476
INV_ROOT_TAU = 0.3989422804014327


def normalize(value, gain, shift):
    mean = jnp.mean(value, axis=1, keepdims=True)
    centred = value - mean
    spread = jnp.mean(centred * centred, axis=1, keepdims=True)
    inverse = lax.rsqrt(spread + EPSILON)
    scaled = centred * inverse
    return (scaled * gain + shift, scaled, inverse)


def normalize_back(grad, scaled, inverse, gain):
    grad_gain = jnp.sum(grad * scaled, axis=0)
    grad_shift = jnp.sum(grad, axis=0)
    inner = grad * gain
    grad_value = inverse * (
        inner
        - jnp.mean(inner, axis=1, keepdims=True)
        - scaled * jnp.mean(inner * scaled, axis=1, keepdims=True)
    )
    return (grad_value, grad_gain, grad_shift)


def gelu_slope(preact):
    return (
        0.5 * (1.0 + lax.erf(preact * SQRT_HALF))
        + preact * jnp.exp(-0.5 * preact * preact) * INV_ROOT_TAU
    )


def block_scores(queries, keys, segment, start):
    block = queries.shape[0]
    length = keys.shape[0]
    query_place = start + jnp.arange(block, dtype=jnp.int32)
    key_place = jnp.arange(length, dtype=jnp.int32)
    query_segment = segment[start : start + block]
    allowed = (query_segment[:, None] == segment[None, :]) & (
        key_place[None, :] <= query_place[:, None]
    )
    scores = jnp.einsum(
        "qhd,khd->hqk", queries, keys, preferred_element_type=jnp.float32
    ) * HEAD_DIM ** (-0.5)
    return jnp.where(allowed[None], scores, NEG_FILL)


def attend_sequence(item):
    queries, keys, values, segment = item
    length = queries.shape[0]
    block = min(512, length)
    results = []
    totals = []
    for start in range(0, length, block):
        scores = block_scores(queries[start : start + block], keys, segment, start)
        top = jnp.max(scores, axis=2, keepdims=True)
        expo = jnp.exp(scores - top)
        total = jnp.sum(expo, axis=2, keepdims=True)
        weights = (expo / total).astype(jnp.bfloat16)
        results.append(
            jnp.einsum("hqk,khd->qhd", weights, values, preferred_element_type=jnp.float32)
        )
        totals.append((top + jnp.log(total))[:, :, 0])
    return (jnp.concatenate(results, axis=0), jnp.concatenate(totals, axis=1))


def attend_back(item):
    queries, keys, values, segment, grad_mixed, log_total = item
    length = queries.shape[0]
    block = min(512, length)
    scale = HEAD_DIM ** (-0.5)
    grad_keys = jnp.zeros(keys.shape, jnp.float32)
    grad_values = jnp.zeros(values.shape, jnp.float32)
    grad_queries = []
    for start in range(0, length, block):
        query_block = queries[start : start + block]
        grad_block = grad_mixed[start : start + block]
        scores = block_scores(query_block, keys, segment, start)
        probs = jnp.exp(scores - log_total[:, start : start + block, None])
        grad_values = grad_values + jnp.einsum(
            "hqk,qhd->khd",
            probs.astype(jnp.bfloat16),
            grad_block,
            preferred_element_type=jnp.float32,
        )
        grad_probs = jnp.einsum(
            "qhd,khd->hqk", grad_block, values, preferred_element_type=jnp.float32
        )
        grad_scores = (
            probs * (grad_probs - jnp.sum(grad_probs * probs, axis=2, keepdims=True))
        ).astype(jnp.bfloat16)
        grad_queries.append(
            jnp.einsum("hqk,khd->qhd", grad_scores, keys, preferred_element_type=jnp.float32)
            * scale
        )
        grad_keys = (
            grad_keys
            + jnp.einsum(
                "hqk,qhd->khd", grad_scores, query_block, preferred_element_type=jnp.float32
            )
            * scale
        )
    return (jnp.concatenate(grad_queries, axis=0), grad_keys, grad_values)


def per_device(
    inputs,
    cotangent,
    routes,
    segments,
    qkv_weight,
    query_bias,
    value_bias,
    out_weight,
    out_bias,
    attn_gain,
    attn_shift,
    moe_gain,
    moe_shift,
    router_weight,
    expert_in,
    expert_in_bias,
    expert_out,
    expert_out_bias,
):
    seq_count, length, width = inputs.shape
    tokens = seq_count * length
    devices = lax.axis_size("dp")
    experts = router_weight.shape[1]
    capacity = 2 * tokens // devices
    gathered = (
        lax.all_gather(qkv_weight.astype(jnp.bfloat16), "dp", axis=0, tiled=True),
        lax.all_gather(out_weight.astype(jnp.bfloat16), "dp", axis=0, tiled=True),
        lax.all_gather(router_weight.astype(jnp.bfloat16), "dp", axis=0, tiled=True),
        lax.all_gather(query_bias.astype(jnp.bfloat16), "dp", axis=0, tiled=True),
        lax.all_gather(value_bias.astype(jnp.bfloat16), "dp", axis=0, tiled=True),
        lax.all_gather(out_bias.astype(jnp.bfloat16), "dp", axis=0, tiled=True),
        lax.all_gather(attn_gain.astype(jnp.bfloat16), "dp", axis=0, tiled=True),
        lax.all_gather(attn_shift.astype(jnp.bfloat16), "dp", axis=0, tiled=True),
        lax.all_gather(moe_gain.astype(jnp.bfloat16), "dp", axis=0, tiled=True),
        lax.all_gather(moe_shift.astype(jnp.bfloat16), "dp", axis=0, tiled=True),
    )
    proj_qkv, proj_out, proj_router = (gathered[0], gathered[1], gathered[2])
    bias_query = gathered[3].astype(jnp.float32)
    bias_value = gathered[4].astype(jnp.float32)
    bias_out = gathered[5].astype(jnp.float32)
    gain_attn = gathered[6].astype(jnp.float32)
    shift_attn = gathered[7].astype(jnp.float32)
    gain_moe = gathered[8].astype(jnp.float32)
    shift_moe = gathered[9].astype(jnp.float32)
    resid = inputs.astype(jnp.float32).reshape(tokens, width)
    normed, scaled_one, inverse_one = normalize(resid, gain_attn, shift_attn)
    normed_low = normed.astype(jnp.bfloat16)
    qkv_bias = jnp.concatenate([bias_query, jnp.zeros_like(bias_query), bias_value])
    packed = (jnp.dot(normed_low, proj_qkv, preferred_element_type=jnp.float32) + qkv_bias).astype(
        jnp.bfloat16
    )
    heads_shape = (seq_count, length, HEADS, HEAD_DIM)
    queries = packed[:, :width].reshape(heads_shape)
    keys = packed[:, width : 2 * width].reshape(heads_shape)
    values = packed[:, 2 * width :].reshape(heads_shape)
    mixed, log_totals = lax.map(attend_sequence, (queries, keys, values, segments))
    mixed_low = mixed.reshape(tokens, width).astype(jnp.bfloat16)
    hidden = resid + jnp.dot(mixed_low, proj_out, preferred_element_type=jnp.float32) + bias_out
    normed_two, scaled_two, inverse_two = normalize(hidden, gain_moe, shift_moe)
    moe_in = normed_two.astype(jnp.bfloat16)
    logits = jnp.dot(moe_in, proj_router, preferred_element_type=jnp.float32)
    route = routes.reshape(tokens)
    onehot = route[:, None] == jnp.arange(experts, dtype=jnp.int32)[None, :]
    onehot_int = onehot.astype(jnp.int32)
    slot = jnp.sum(jnp.cumsum(onehot_int, axis=0) * onehot_int, axis=1) - 1
    target = route * capacity + slot
    source_row = (
        jnp.zeros((experts * capacity,), jnp.int32)
        .at[target]
        .set(jnp.arange(tokens, dtype=jnp.int32))
    )
    occupied = jnp.zeros((experts * capacity,), jnp.bool_).at[target].set(True)
    outgoing = jnp.where(
        occupied[:, None], moe_in[source_row], jnp.zeros((), jnp.bfloat16)
    ).reshape(experts, capacity, width)
    weight_in = expert_in[0].astype(jnp.bfloat16)
    weight_back = expert_out[0].astype(jnp.bfloat16)
    bias_in = expert_in_bias[0]
    bias_back = expert_out_bias[0]
    received = lax.all_to_all(outgoing, "dp", split_axis=0, concat_axis=0, tiled=True)
    items = received.shape[1]
    preact = (
        jnp.dot(received.reshape(-1, width), weight_in, preferred_element_type=jnp.float32)
        + bias_in
    )
    active = jax.nn.gelu(preact, approximate=False).astype(jnp.bfloat16)
    result = (jnp.dot(active, weight_back, preferred_element_type=jnp.float32) + bias_back).astype(
        jnp.bfloat16
    )
    returned = lax.all_to_all(
        result.reshape(devices, items, width), "dp", split_axis=0, concat_axis=0, tiled=True
    )
    returned, received, preact = (returned, received, preact.reshape(devices, items, -1))
    token_back = returned.reshape(experts * capacity, width)[target].astype(jnp.float32)
    chosen = jnp.sum(jnp.where(onehot, logits, 0.0), axis=1)
    gate = jax.nn.sigmoid(chosen)
    output = hidden + gate[:, None] * token_back
    grad_out = cotangent.astype(jnp.float32).reshape(tokens, width)
    grad_gate = jnp.sum(grad_out * token_back, axis=1)
    grad_chosen = grad_gate * gate * (1.0 - gate)
    grad_logits = jnp.where(onehot, grad_chosen[:, None], 0.0)
    grad_logits_low = grad_logits.astype(jnp.bfloat16)
    grad_router = jnp.einsum(
        "td,te->de", moe_in, grad_logits_low, preferred_element_type=jnp.float32
    )
    grad_token_back = (grad_out * gate[:, None]).astype(jnp.bfloat16)
    back_slots = jnp.where(
        occupied[:, None], grad_token_back[source_row], jnp.zeros((), jnp.bfloat16)
    ).reshape(experts, capacity, width)
    arrived = lax.all_to_all(back_slots, "dp", split_axis=0, concat_axis=0, tiled=True).reshape(
        -1, width
    )
    preact_flat = preact.reshape(arrived.shape[0], -1)
    received_flat = received.reshape(-1, width)
    active_again = jax.nn.gelu(preact_flat, approximate=False).astype(jnp.bfloat16)
    grad_weight_back = jnp.einsum(
        "rf,rd->fd", active_again, arrived, preferred_element_type=jnp.float32
    )
    grad_bias_back = jnp.sum(arrived.astype(jnp.float32), axis=0)
    grad_preact = (
        jnp.einsum("rd,fd->rf", arrived, weight_back, preferred_element_type=jnp.float32)
        * gelu_slope(preact_flat)
    ).astype(jnp.bfloat16)
    grad_weight_in = jnp.einsum(
        "rd,rf->df", received_flat, grad_preact, preferred_element_type=jnp.float32
    )
    grad_bias_in = jnp.sum(grad_preact.astype(jnp.float32), axis=0)
    grad_rows = jnp.einsum(
        "rf,df->rd", grad_preact, weight_in, preferred_element_type=jnp.float32
    ).astype(jnp.bfloat16)
    grad_sent = lax.all_to_all(
        grad_rows.reshape(devices, capacity, width), "dp", split_axis=0, concat_axis=0, tiled=True
    )
    grad_moe_in = grad_sent.reshape(experts * capacity, width)[target].astype(
        jnp.float32
    ) + jnp.einsum("te,de->td", grad_logits_low, proj_router, preferred_element_type=jnp.float32)
    grad_two, grad_gain_moe, grad_shift_moe = normalize_back(
        grad_moe_in, scaled_two, inverse_two, gain_moe
    )
    grad_hidden = grad_out + grad_two
    grad_attn_low = grad_hidden.astype(jnp.bfloat16)
    grad_proj_out = jnp.einsum(
        "td,te->de", mixed_low, grad_attn_low, preferred_element_type=jnp.float32
    )
    grad_bias_out = jnp.sum(grad_attn_low.astype(jnp.float32), axis=0)
    grad_mixed = (
        jnp.einsum("te,de->td", grad_attn_low, proj_out, preferred_element_type=jnp.float32)
        .astype(jnp.bfloat16)
        .reshape(heads_shape)
    )
    grad_queries, grad_keys, grad_values = lax.map(
        attend_back, (queries, keys, values, segments, grad_mixed, log_totals)
    )
    grad_packed = jnp.concatenate(
        [
            grad_queries.reshape(tokens, width),
            grad_keys.reshape(tokens, width),
            grad_values.reshape(tokens, width),
        ],
        axis=1,
    ).astype(jnp.bfloat16)
    grad_bias_query = jnp.sum(grad_packed[:, :width].astype(jnp.float32), axis=0)
    grad_bias_value = jnp.sum(grad_packed[:, 2 * width :].astype(jnp.float32), axis=0)
    grad_proj_qkv = jnp.einsum(
        "td,te->de", normed_low, grad_packed, preferred_element_type=jnp.float32
    )
    grad_normed = jnp.einsum("te,de->td", grad_packed, proj_qkv, preferred_element_type=jnp.float32)
    grad_one, grad_gain_attn, grad_shift_attn = normalize_back(
        grad_normed, scaled_one, inverse_one, gain_attn
    )
    grad_inputs = (grad_hidden + grad_one).reshape(seq_count, length, width)
    summed = (
        lax.psum_scatter(grad_proj_qkv, "dp", scatter_dimension=0, tiled=True),
        lax.psum_scatter(grad_proj_out, "dp", scatter_dimension=0, tiled=True),
        lax.psum_scatter(grad_router, "dp", scatter_dimension=0, tiled=True),
        lax.psum_scatter(grad_bias_query, "dp", scatter_dimension=0, tiled=True),
        lax.psum_scatter(grad_bias_value, "dp", scatter_dimension=0, tiled=True),
        lax.psum_scatter(grad_bias_out, "dp", scatter_dimension=0, tiled=True),
        lax.psum_scatter(grad_gain_attn, "dp", scatter_dimension=0, tiled=True),
        lax.psum_scatter(grad_shift_attn, "dp", scatter_dimension=0, tiled=True),
        lax.psum_scatter(grad_gain_moe, "dp", scatter_dimension=0, tiled=True),
        lax.psum_scatter(grad_shift_moe, "dp", scatter_dimension=0, tiled=True),
    )
    (
        summed_qkv,
        summed_out,
        summed_router,
        summed_query,
        summed_value,
        summed_bias_out,
        summed_gain_attn,
        summed_shift_attn,
        summed_gain_moe,
        summed_shift_moe,
    ) = summed
    return (
        output.reshape(seq_count, length, width).astype(jnp.bfloat16),
        grad_inputs,
        summed_qkv,
        summed_query,
        summed_value,
        summed_out,
        summed_bias_out,
        summed_gain_attn,
        summed_shift_attn,
        summed_gain_moe,
        summed_shift_moe,
        summed_router,
        grad_weight_in[None],
        grad_bias_in[None],
        grad_weight_back[None],
        grad_bias_back[None],
    )


def solution(mesh):
    placed = (
        P("dp", None, None),
        P("dp", None, None),
        P("dp", None, None),
        P("dp", None),
        P("dp", None),
        P("dp"),
        P("dp"),
        P("dp", None),
        P("dp"),
        P("dp"),
        P("dp"),
        P("dp"),
        P("dp"),
        P("dp", None),
        P("dp", None, None),
        P("dp", None),
        P("dp", None, None),
        P("dp", None),
    )
    return jax.shard_map(
        per_device,
        mesh=mesh,
        in_specs=placed,
        out_specs=(
            P("dp", None, None),
            P("dp", None, None),
            P("dp", None),
            P("dp"),
            P("dp"),
            P("dp", None),
            P("dp"),
            P("dp"),
            P("dp"),
            P("dp"),
            P("dp"),
            P("dp", None),
            P("dp", None, None),
            P("dp", None),
            P("dp", None, None),
            P("dp", None),
        ),
        check_vma=False,
    )
```

profile of v0, /device:TPU:0, one launch (start us, length us, event | category | flops | bytes accessed | tf_op | source)
XLA Modules:
  0.0 1037.4 jit_solution(15060697834447433695)
XLA Ops:
  16.5 42.5 %all-reduce.16 = (bf16[768]{0:T(1024)(128)(2,1)S(1)}, bf16[768]{0:T(1024)(128)(2,1)S(1)}, bf16[768]{0:T(1024)(128)(2,1)S(1)}, bf16[768]{0:T(1024)(128)(2,1)S(1)}...) all-reduce(bf16[768]{0:T(1024)(128)(2,1)S(1)} %dynamic-update-slice, ...), channel_id=1, replica_groups=mesh['dp'=32] {'dp'}, use_global_device_ids=true, to_apply=%add.3 | all-reduce | flops 5376 | bytes 21504
  61.6 9.0 reduce-window.6
  106.2 12.2 %fusion.29 = (f32[12,512]{1,0:T(8,128)S(1)}, f32[12,512,1024]{2,1,0:T(8,128)}) fusion(pred[512,1024]{1,0:T(8,128)(4,1)} %get-tuple-element.148, bf16[512,12,64]{0,2,1:T(8,128)(2,1)} %bitcast.190, bf16[1024,12,64]{0,2,1:T(8,128)(2,1)S(1)} %bitcast.178), kind=kOutput, calls=%fused_computation.57 | convolution fusion | flops 824174592 | bytes 28073984 | tf_op jit(solution)/shard_map/while/body/eval_jaxpr/qhd,khd->hqk/dot_general | solution.py:53
  118.4 12.4 %fusion.17 = f32[12,512]{1,0:T(8,128)S(1)} fusion(f32[12,512]{1,0:T(8,128)S(1)} %get-tuple-element.151, f32[12,512,1024]{2,1,0:T(8,128)} %get-tuple-element.152, pred[512,1024]{1,0:T(8,128)(4,1)} %get-tuple-element.148), kind=kLoop, calls=%fused_computation.46 | loop fusion | flops 25159680 | bytes 25739264 | tf_op jit(solution)/shard_map/while/body/eval_jaxpr/reduce_sum | solution.py:69
  134.4 9.4 fusion.80
  143.9 12.3 %fusion.28 = (f32[12,512]{1,0:T(8,128)S(1)}, f32[12,512,1024]{2,1,0:T(8,128)}) fusion(pred[512,1024]{1,0:T(8,128)(4,1)} %get-tuple-element.147, bf16[512,12,64]{0,2,1:T(8,128)(2,1)} %bitcast.192, bf16[1024,12,64]{0,2,1:T(8,128)(2,1)S(1)} %bitcast.179), kind=kOutput, calls=%fused_computation.56 | convolution fusion | flops 824174592 | bytes 28073984 | tf_op jit(solution)/shard_map/while/body/eval_jaxpr/qhd,khd->hqk/dot_general | solution.py:53
  156.1 13.5 %fusion.16 = f32[12,512]{1,0:T(8,128)S(1)} fusion(f32[12,512]{1,0:T(8,128)S(1)} %get-tuple-element.153, f32[12,512,1024]{2,1,0:T(8,128)} %get-tuple-element.154, pred[512,1024]{1,0:T(8,128)(4,1)} %get-tuple-element.147), kind=kLoop, calls=%fused_computation.45 | loop fusion | flops 25159680 | bytes 25739264 | tf_op jit(solution)/shard_map/while/body/eval_jaxpr/reduce_sum | solution.py:69
  172.0 8.5 fusion.79
  189.2 9.4 gather_fusion
  207.5 70.7 %all-to-all-done = bf16[32,64,768]{2,1,0:T(8,128)(2,1)S(1)} async-done(((bf16[32,64,768]{2,1,0:T(8,128)(2,1)}), bf16[32,64,768]{2,1,0:T(8,128)(2,1)S(1)}, u32[]{:S(2)}, u32[]{:S(2)}) %all-to-all-start) | async-done | bytes 3145760 | tf_op jit(solution)/shard_map/all_to_all | solution.py:197
  278.2 64.8 %fusion.2 = (bf16[2048,3072]{1,0:T(8,128)(2,1)}, f32[2048,3072]{1,0:T(8,128)}) fusion(f32[3072]{0:T(1024)S(1)} %bitcast.226, bf16[2048,768]{1,0:T(8,128)(2,1)S(1)} %bitcast.198, f32[1,768,3072]{2,1,0:T(8,128)} %param.32), kind=kOutput, calls=%fused_computation.10 | convolution fusion | flops 10081271808 | bytes 50343936 | tf_op jit(solution)/shard_map/dot_general | solution.py:200
  343.0 14.0 %add_convert_fusion.1 = bf16[2048,768]{1,0:T(8,128)(2,1)} fusion(bf16[2048,3072]{1,0:T(8,128)(2,1)} %get-tuple-element.157, f32[768]{0:T(1024)S(1)} %copy-done.70, f32[1,3072,768]{2,1,0:T(8,128)S(1)} %copy-done.72), kind=kOutput, calls=%fused_computation.59 | convolution fusion | flops 9669181440 | bytes 25168896 | tf_op jit(solution)/shard_map/dot_general | solution.py:204
  363.6 84.9 %all_gather.39 = bf16[768,32]{1,0:T(8,128)(2,1)S(1)} all-gather(bf16[24,32]{1,0:T(8,128)(2,1)S(1)} %convert_element_type.188), channel_id=1, replica_groups=mesh['dp'=32] {'dp'}, dimensions={0}, use_global_device_ids=true | all-gather | bytes 50688 | tf_op jit(solution)/shard_map/all_gather | solution.py:145
  461.0 9.4 gather_fusion.2
  472.6 83.1 %all_to_all.20 = bf16[32,64,768]{2,1,0:T(8,128)(2,1)S(1)} all-to-all(bf16[32,64,768]{2,1,0:T(8,128)(2,1)S(1)} %broadcast_select_fusion), channel_id=1, replica_groups=mesh['dp'=32] {'dp'}, dimensions={0} | all-to-all | bytes 6291456 | tf_op jit(solution)/shard_map/all_to_all | solution.py:227
  555.7 25.6 %convert_reduce_fusion = (f32[3072]{0:T(1024)}, bf16[2048,3072]{1,0:T(8,128)(2,1)}) fusion(f32[2048,3072]{1,0:T(8,128)} %get-tuple-element.158, f32[3072]{0:T(1024)S(1)} %bitcast.227, bf16[2048,768]{1,0:T(8,128)(2,1)S(1)} %bitcast.186, f32[1,3072,768]{2,1,0:T(8,128)} %param.34), kind=kOutput, calls=%fused_computation.17 | convolution fusion | flops 9747821568 | bytes 50356224 | tf_op jit(solution)/shard_map/rd,fd->rf/dot_general | solution.py:238
  581.3 14.2 %fusion.47 = bf16[2048,768]{1,0:T(8,128)(2,1)} fusion(bf16[2048,3072]{1,0:T(8,128)(2,1)} %get-tuple-element.167, f32[1,768,3072]{2,1,0:T(8,128)S(1)} %bitcast.225), kind=kOutput, calls=%fused_computation.84 | convolution fusion | flops 9667608576 | bytes 25165824 | tf_op jit(solution)/shard_map/rf,df->rd/dot_general | solution.py:245
  602.1 69.4 %all-to-all-done.3 = bf16[32,64,768]{2,1,0:T(8,128)(2,1)S(1)} async-done(((bf16[32,64,768]{2,1,0:T(8,128)(2,1)}), bf16[32,64,768]{2,1,0:T(8,128)(2,1)S(1)}, u32[]{:S(2)}, u32[]{:S(2)}) %all-to-all-start.3) | async-done | bytes 3145760 | tf_op jit(solution)/shard_map/all_to_all | solution.py:248
  689.4 13.2 %fusion.20 = f32[12,64,1024]{2,1,0:T(8,128)} fusion(bf16[512,12,64]{0,2,1:T(8,128)(2,1)S(1)} %bitcast.204, f32[12,512]{1,0:T(8,128)S(1)} %log_add_fusion, f32[12,512,1024]{2,1,0:T(8,128)} %get-tuple-element.152, pred[512,1024]{1,0:T(8,128)(4,1)S(1)} %copy-done.17), kind=kOutput, calls=%fused_computation.49 | convolution fusion | flops 830472192 | bytes 29646848 | tf_op jit(solution)/shard_map/while/body/eval_jaxpr/hqk,qhd->khd/dot_general | solution.py:91
  702.6 17.7 %multiply_reduce_fusion = (f32[12,512]{1,0:T(8,128)S(1)}, f32[12,512,1024]{2,1,0:T(8,128)}) fusion(f32[12,512]{1,0:T(8,128)S(1)} %log_add_fusion, f32[12,512,1024]{2,1,0:T(8,128)} %get-tuple-element.152, pred[512,1024]{1,0:T(8,128)(4,1)S(1)} %copy-done.17, bf16[512,12,64]{0,2,1:T(8,128)(2,1)} %bitcast.205, bf16[1024,12,64]{0,2,1:T(8,128)(2,1)S(1)} %bitcast.184), kind=kOutput, calls=%fused_computation.19 | convolution fusion | flops 836757504 | bytes 53264384 | tf_op jit(solution)/shard_map/while/body/eval_jaxpr/qhd,khd->hqk/dot_general | solution.py:97
  720.4 21.6 %multiply_reduce_fusion.1 = (f32[12,512]{1,0:T(8,128)S(1)}, f32[12,512,1024]{2,1,0:T(8,128)}) fusion(f32[12,512]{1,0:T(8,128)S(1)} %log_add_fusion.1, f32[12,512,1024]{2,1,0:T(8,128)} %get-tuple-element.154, pred[512,1024]{1,0:T(8,128)(4,1)S(1)} %copy-done.16, bf16[512,12,64]{0,2,1:T(8,128)(2,1)S(1)} %bitcast.202, bf16[1024,12,64]{0,2,1:T(8,128)(2,1)S(1)} %bitcast.185), kind=kOutput, calls=%fused_computation.22 | convolution fusion | flops 836757504 | bytes 53264384 | tf_op jit(solution)/shard_map/while/body/eval_jaxpr/qhd,khd->hqk/dot_general | solution.py:97
  742.0 41.7 %multiply_convert_fusion = (bf16[12,512,1024]{2,1,0:T(8,128)(2,1)}, bf16[12,512,1024]{2,1,0:T(8,128)(2,1)}) fusion(f32[12,512,1024]{2,1,0:T(8,128)} %get-tuple-element.163, f32[12,512]{1,0:T(8,128)S(1)} %get-tuple-element.162, f32[12,512]{1,0:T(8,128)S(1)} %log_add_fusion, f32[12,512,1024]{2,1,0:T(8,128)} %get-tuple-element.152, ...), kind=kLoop, calls=%fused_computation.18 | loop fusion | flops 75497472 | bytes 126976000 | tf_op jit(solution)/shard_map/while/body/eval_jaxpr/convert_element_type | solution.py:102
  783.7 9.5 fusion.78
  793.3 7.0 fusion.120
  806.9 8.6 fusion.77
  815.9 13.0 %add_convert_fusion.2 = bf16[12,64,1024]{2,1,0:T(8,128)(2,1)S(1)} fusion(f32[12,64,1024]{2,1,0:T(8,128)S(1)} %copy-done.75, bf16[512,12,64]{0,2,1:T(8,128)(2,1)S(1)} %bitcast.203, f32[12,512]{1,0:T(8,128)S(1)} %log_add_fusion.1, f32[12,512,1024]{2,1,0:T(8,128)} %get-tuple-element.154, pred[512,1024]{1,0:T(8,128)(4,1)S(1)} %copy-done.16), kind=kOutput, calls=%fused_computation.103 | convolution fusion | flops 832045056 | bytes 31219712 | tf_op jit(solution)/shard_map/while/body/eval_jaxpr/hqk,qhd->khd/dot_general | solution.py:91
  830.1 7.0 fusion.70
  840.2 16.9 %convolution_bitcast_fusion = f32[1,3072,768]{2,1,0:T(8,128)} fusion(bf16[2048,3072]{1,0:T(8,128)(2,1)} %get-tuple-element.157, bf16[2048,768]{1,0:T(8,128)(2,1)} %bitcast.187), kind=kOutput, calls=%fused_computation.60 | convolution fusion | flops 9663676416 | bytes 25165824 | tf_op jit(solution)/shard_map/rf,rd->fd/dot_general | solution.py:233
  857.1 15.4 %convolution_bitcast_fusion.1 = f32[1,768,3072]{2,1,0:T(8,128)} fusion(bf16[2048,768]{1,0:T(8,128)(2,1)S(1)} %bitcast.199, bf16[2048,3072]{1,0:T(8,128)(2,1)} %get-tuple-element.167), kind=kOutput, calls=%fused_computation.61 | convolution fusion | flops 9663676416 | bytes 25165824 | tf_op jit(solution)/shard_map/rd,rf->df/dot_general | solution.py:241
  875.3 8.6 fusion.119
  891.0 38.7 %all-reduce.15 = (f32[768]{0:T(1024)S(1)}, f32[768]{0:T(1024)S(1)}, f32[768]{0:T(1024)S(1)}, f32[768]{0:T(1024)S(1)}, f32[768]{0:T(1024)S(1)}, /*index=5*/f32[768]{0:T(1024)S(1)}, f32[768]{0:T(1024)S(1)}) all-reduce(f32[768]{0:T(1024)S(1)} %convert_reduce_fusion.5, ...), channel_id=3, replica_groups=mesh['dp'=32] {'dp'}, use_global_device_ids=true, to_apply=%region_23.24.clone | all-reduce | flops 5376 | bytes 43008
  943.1 87.6 %reduce-scatter.6.cloned.1.call-done = f32[24,2304]{1,0:T(8,128)} async-done(((f32[768,2304]{1,0:T(8,128)}), f32[24,2304]{1,0:T(8,128)}) %reduce-scatter.6.cloned.1.call-update) | async-done | bytes 221200 | tf_op jit(solution)/shard_map/reduce_scatter | solution.py:290
  (299 shorter events, 150.4 us)
Async XLA Ops:
  7.2 78.0 %copy-start.61 = (s32[1,1024]{1,0:T(1,128)S(1)}, s32[1,1024]{1,0:T(1,128)}, u32[]{:S(2)}) copy-start(s32[1,1024]{1,0:T(1,128)} %param.21) | copy-start | bytes 12292
  7.2 80.0 %all-gather.3.cloned.1.call-start = ((), (), s32[]{:S(2)}) async-start(), calls=%async_computation.7 | async-start | bytes 3649536 | tf_op jit(solution)/shard_map/all_gather | solution.py:143
  8.9 173.3 %all-gather.5.cloned.1.call-start = ((), (), s32[]{:S(2)}) async-start(), calls=%async_computation.8 | async-start | bytes 1216512 | tf_op jit(solution)/shard_map/all_gather | solution.py:144
  59.0 34.6 %copy-start.50 = (f32[768]{0:T(1024)}, f32[768]{0:T(1024)S(1)}, u32[]{:S(2)}) copy-start(f32[768]{0:T(1024)S(1)} %convert_element_type.167) | copy-start | bytes 9220
  59.6 34.0 %copy-start.68 = (f32[768]{0:T(1024)}, f32[768]{0:T(1024)S(1)}, u32[]{:S(2)}) copy-start(f32[768]{0:T(1024)S(1)} %convert_element_type.169) | copy-start | bytes 9220
  84.4 97.8 %copy-start.2 = (bf16[1,1024,768]{1,2,0:T(8,128)(2,1)}, bf16[1,1024,768]{1,2,0:T(8,128)(2,1)S(1)}, u32[]{:S(2)}) copy-start(bf16[1,1024,768]{1,2,0:T(8,128)(2,1)S(1)} %copy.74) | copy-start | bytes 4718596
  98.5 45.4 %copy-start.4 = (bf16[1024,768]{0,1:T(8,128)(2,1)}, bf16[1024,768]{0,1:T(8,128)(2,1)S(1)}, u32[]{:S(2)}) copy-start(bf16[1024,768]{0,1:T(8,128)(2,1)S(1)} %copy.77) | copy-start | bytes 4718596
  106.2 24.7 %copy-start.10 = (bf16[1024,768]{0,1:T(8,128)(2,1)S(1)}, bf16[1024,768]{0,1:T(8,128)(2,1)}, u32[]{:S(2)}) copy-start(bf16[1024,768]{0,1:T(8,128)(2,1)} %copy.75) | copy-start | bytes 4718596
  118.4 16.0 %copy-start.1 = (f32[12,512,1024]{2,1,0:T(8,128)S(1)}, f32[12,512,1024]{2,1,0:T(8,128)}, u32[]{:S(2)}) copy-start(f32[12,512,1024]{2,1,0:T(8,128)} %get-tuple-element.152) | copy-start | bytes 75497472
  201.9 76.3 %copy-start.74 = (f32[1,3072]{1,0:T(1,128)S(1)}, f32[1,3072]{1,0:T(1,128)}, u32[]{:S(2)}) copy-start(f32[1,3072]{1,0:T(1,128)} %param.33) | copy-start | bytes 36868
  201.9 76.3 %all-to-all-start = ((bf16[32,64,768]{2,1,0:T(8,128)(2,1)}), bf16[32,64,768]{2,1,0:T(8,128)(2,1)S(1)}, u32[]{:S(2)}, u32[]{:S(2)}) async-start(bf16[32,64,768]{2,1,0:T(8,128)(2,1)} %broadcast_select_fusion.1), calls=%async_computation | async-start | bytes 6291456 | tf_op jit(solution)/shard_map/all_to_all | solution.py:197
  278.2 64.8 %copy-start.27 = (bf16[32,64,768]{2,1,0:T(8,128)(2,1)}, bf16[32,64,768]{2,1,0:T(8,128)(2,1)S(1)}, u32[]{:S(2)}) copy-start(bf16[32,64,768]{2,1,0:T(8,128)(2,1)S(1)} %all-to-all-done) | copy-start | bytes 9437188
  278.2 64.8 %copy-start.70 = (f32[768]{0:T(1024)S(1)}, f32[768]{0:T(1024)}, u32[]{:S(2)}) copy-start(f32[768]{0:T(1024)} %reduce.2) | copy-start | bytes 9220
  278.2 64.8 %copy-start.72 = (f32[1,3072,768]{2,1,0:T(8,128)S(1)}, f32[1,3072,768]{2,1,0:T(8,128)}, u32[]{:S(2)}) copy-start(f32[1,3072,768]{2,1,0:T(8,128)} %param.34) | copy-start | bytes 28311556
  357.0 91.5 %copy-start.64 = (s32[1024,1]{0,1:T(1,128)S(1)}, s32[1024,1]{0,1:T(1,128)}, u32[]{:S(2)}) copy-start(s32[1024,1]{0,1:T(1,128)} %copy-done.63) | copy-start | bytes 12292
  357.0 91.5 %copy-start.43 = (s32[1,1024,1]{1,2,0:T(1,128)S(1)}, s32[1,1024,1]{1,2,0:T(1,128)}, u32[]{:S(2)}) copy-start(s32[1,1024,1]{1,2,0:T(1,128)} %param.20) | copy-start | bytes 12292
  357.0 93.4 %all-to-all-start.1 = ((bf16[32,64,768]{2,1,0:T(8,128)(2,1)}), bf16[32,64,768]{2,1,0:T(8,128)(2,1)S(1)}, u32[]{:S(2)}, u32[]{:S(2)}) async-start(bf16[32,64,768]{2,1,0:T(8,128)(2,1)} %bitcast.201), calls=%async_computation.1 | async-start | bytes 6291456 | tf_op jit(solution)/shard_map/all_to_all | solution.py:207
  472.5 108.7 %slice-start.3 = ((s8[9437184]{0:T(1024)(128)(4,1)}), s8[4194304]{0:T(1024)(128)(4,1)S(1)}, s32[]{:S(2)}) async-start(s8[9437184]{0:T(1024)(128)(4,1)} %bitcast.224), calls=%async_computation.15 | async-start | bytes 8388608
  555.7 25.6 %copy-start.18 = (bf16[32,64,768]{2,1,0:T(8,128)(2,1)}, bf16[32,64,768]{2,1,0:T(8,128)(2,1)S(1)}, u32[]{:S(2)}) copy-start(bf16[32,64,768]{2,1,0:T(8,128)(2,1)S(1)} %all_to_all.20) | copy-start | bytes 9437188
  555.7 25.6 %slice-start.4 = ((s8[9437184]{0:T(1024)(128)(4,1)}), s8[4194304]{0:T(1024)(128)(4,1)S(1)}, s32[]{:S(2)}) async-start(s8[9437184]{0:T(1024)(128)(4,1)} %bitcast.224), calls=%async_computation.16 | async-start | bytes 8388608
  555.7 25.6 %slice-start.5 = ((s8[9437184]{0:T(1024)(128)(4,1)}), s8[1048576]{0:T(1024)(128)(4,1)S(1)}, s32[]{:S(2)}) async-start(s8[9437184]{0:T(1024)(128)(4,1)} %bitcast.224), calls=%async_computation.17 | async-start | bytes 2097152
  595.5 76.1 %all-to-all-start.3 = ((bf16[32,64,768]{2,1,0:T(8,128)(2,1)}), bf16[32,64,768]{2,1,0:T(8,128)(2,1)S(1)}, u32[]{:S(2)}, u32[]{:S(2)}) async-start(bf16[32,64,768]{2,1,0:T(8,128)(2,1)} %bitcast.200), calls=%async_computation.3 | async-start | bytes 6291456 | tf_op jit(solution)/shard_map/all_to_all | solution.py:248
  599.1 343.9 %reduce-scatter.10.cloned.1.call-start = ((), (), s32[]{:S(2)}) async-start(), calls=%async_computation.11 | async-start | bytes 405504
  602.0 341.0 %reduce-scatter.8.cloned.1.call-start = ((), (), s32[]{:S(2)}) async-start(), calls=%async_computation.10 | async-start | bytes 2433024 | tf_op jit(solution)/shard_map/reduce_scatter | solution.py:291
  688.4 31.9 %copy-start.29 = (bf16[512,768]{0,1:T(8,128)(2,1)}, bf16[512,768]{0,1:T(8,128)(2,1)S(1)}, u32[]{:S(2)}) copy-start(bf16[512,768]{0,1:T(8,128)(2,1)S(1)} %get-tuple-element.143) | copy-start | bytes 2359300
  702.6 17.7 %copy-start.16 = (pred[512,1024]{1,0:T(8,128)(4,1)S(1)}, pred[512,1024]{1,0:T(8,128)(4,1)}, u32[]{:S(2)}) copy-start(pred[512,1024]{1,0:T(8,128)(4,1)} %get-tuple-element.147) | copy-start | bytes 1572868
  742.0 41.7 %copy-start.5 = (bf16[1024,768]{0,1:T(8,128)(2,1)S(1)}, bf16[1024,768]{0,1:T(8,128)(2,1)}, u32[]{:S(2)}) copy-start(bf16[1024,768]{0,1:T(8,128)(2,1)} %copy-done.4) | copy-start | bytes 4718596
  783.7 16.6 %slice-start = ((s8[12582912]{0:T(1024)(128)(4,1)}), s8[4194304]{0:T(1024)(128)(4,1)S(1)}, s32[]{:S(2)}) async-start(s8[12582912]{0:T(1024)(128)(4,1)} %bitcast.174), calls=%async_computation.12 | async-start | bytes 8388608
  783.7 16.6 %slice-start.1 = ((s8[12582912]{0:T(1024)(128)(4,1)}), s8[4194304]{0:T(1024)(128)(4,1)S(1)}, s32[]{:S(2)}) async-start(s8[12582912]{0:T(1024)(128)(4,1)} %bitcast.174), calls=%async_computation.13 | async-start | bytes 8388608
  806.9 223.9 %reduce-scatter.6.cloned.1.call-start = ((), (), s32[]{:S(2)}) async-start(), calls=%async_computation.9 | async-start | bytes 7299072 | tf_op jit(solution)/shard_map/reduce_scatter | solution.py:290
  840.2 16.9 %copy-start.28 = (bf16[32,64,768]{2,1,0:T(8,128)(2,1)S(1)}, bf16[32,64,768]{2,1,0:T(8,128)(2,1)}, u32[]{:S(2)}) copy-start(bf16[32,64,768]{2,1,0:T(8,128)(2,1)} %copy-done.27) | copy-start | bytes 9437188
  857.1 18.1 %copy-start.24 = (bf16[1024,12,64]{0,2,1:T(8,128)(2,1)S(1)}, bf16[1024,12,64]{0,2,1:T(8,128)(2,1)}, u32[]{:S(2)}) copy-start(bf16[1024,12,64]{0,2,1:T(8,128)(2,1)} %copy-done.23) | copy-start | bytes 4718596
  (58 other events, 414.6 us)
Sparse Core Ops, SparseCore 0:
  11.5 62.9 all-gather.2
  77.9 52.4 all-gather.4
  605.5 97.8 reduce-scatter.9
  807.0 99.0 reduce-scatter.7
  912.2 118.4 reduce-scatter.5
where the time goes:
time: 1050 us; the launch traced here: 1040 us
  matrix products  326 us (31%)
  blocking collectives  249 us (24%)
  waiting for transfers between devices  228 us (22%)
  other arithmetic  118 us (11%)
  local copies, waits for them, and re-layouts  88.8 us (8%)
  between operations  15.1 us (1%)
  starting transfers between devices  12.8 us (1%)
    reduce_scatter x1, waiting for transfers between devices, per_device(): lax.psum_scatter(grad_proj_qkv, 'dp', scatter_dimension=0, tiled=True)  87.6 us
    all_gather x1, blocking collectives, per_device(): lax.all_gather(router_weight.astype(jnp.bfloat16), 'dp', axis=0, tiled=True)  84.9 us
    all_to_all x1, blocking collectives, per_device(): lax.all_to_all(back_slots, 'dp', split_axis=0, concat_axis=0, tiled=True)  83.1 us
    unnamed x2, blocking collectives  81.2 us
    all_to_all x1, waiting for transfers between devices, per_device(): lax.all_to_all(outgoing, 'dp', split_axis=0, concat_axis=0, tiled=True)  70.7 us
    all_to_all x1, waiting for transfers between devices, per_device(): lax.all_to_all(grad_rows.reshape(devices, capacity, width), 'dp', split_a...  69.4 us
    dot_general x1, matrix products, per_device(): jnp.dot(received.reshape(-1, width), weight_in, preferred_element_type=jn...  64.8 us
    convert_element_type x1, other arithmetic, attend_back(): grad_scores = (probs * (grad_probs - jnp.sum(grad_probs * probs, axis=2,...  41.7 us
  transfers between devices with their start and end apart: 8, of which 3 were waited for; matrix products, arithmetic and copies ran while one was open for 35% of the time, Pallas kernels for 0%

commit v1 on v0

v1 whole, which is shorter than its diff:
```python
import functools

import jax
import jax.numpy as jnp
from jax import lax
from jax.experimental import pallas as pl
from jax.experimental.pallas import tpu as pltpu
from jax.sharding import PartitionSpec as P

HEAD_DIM = 64
PAIR = 2 * HEAD_DIM
GROUPS = 3
QBLOCK = 256
MAX_DOC = 512
CHUNKS = 2
EPSILON = 1e-05
NEG_FILL = -1000000000.0
SQRT_HALF = 0.7071067811865476
INV_ROOT_TAU = 0.3989422804014327
F32 = jnp.float32
BF16 = jnp.bfloat16
VMEM_LIMIT = 56 * 1024 * 1024


def dot(a, b):
    return lax.dot_general(a, b, (((1,), (0,)), ((), ())), preferred_element_type=F32)


def dot_nt(a, b):
    return lax.dot_general(a, b, (((1,), (1,)), ((), ())), preferred_element_type=F32)


def dot_tn(a, b):
    return lax.dot_general(a, b, (((0,), (0,)), ((), ())), preferred_element_type=F32)


def params():
    return pltpu.CompilerParams(vmem_limit_bytes=VMEM_LIMIT)


def whole(shape):
    return pl.BlockSpec(shape, lambda *_: (0,) * len(shape))


def window(index):
    return max(0, index * QBLOCK - MAX_DOC), (index + 1) * QBLOCK


def iota(shape, axis):
    return lax.broadcasted_iota(jnp.int32, shape, axis)


def norm_stats(value):
    mean = jnp.mean(value, axis=1, keepdims=True)
    centred = value - mean
    spread = jnp.mean(centred * centred, axis=1, keepdims=True)
    inverse = lax.rsqrt(spread + EPSILON)
    return centred * inverse, inverse


def norm_back(grad, scaled, inverse, gain):
    inner = grad * gain
    return inverse * (
        inner
        - jnp.mean(inner, axis=1, keepdims=True)
        - scaled * jnp.mean(inner * scaled, axis=1, keepdims=True)
    )


def attend_kernel(x_ref, w_ref, b_ref, sc_ref, sr_ref, qkv_ref, mix_ref, lse_ref):
    tokens = x_ref.shape[0]
    wide = mix_ref.shape[1]
    pairs = wide // PAIR
    qkv_ref[...] = (dot(x_ref[...], w_ref[...]) + b_ref[...]).astype(BF16)
    lane = iota((QBLOCK, PAIR), 1)
    for i in range(tokens // QBLOCK):
        lo, hi = window(i)
        r0 = i * QBLOCK
        rows = slice(r0, r0 + QBLOCK)
        allowed = (sc_ref[rows, :] == sr_ref[:, lo:hi]) & (
            iota((QBLOCK, hi - lo), 1) + lo <= iota((QBLOCK, hi - lo), 0) + r0
        )
        total = jnp.zeros((QBLOCK, PAIR), F32)
        for p in range(pairs):
            q = qkv_ref[rows, p * PAIR : (p + 1) * PAIR] * jnp.asarray(HEAD_DIM**-0.5, BF16)
            k = qkv_ref[lo:hi, wide + p * PAIR : wide + (p + 1) * PAIR]
            v = qkv_ref[lo:hi, 2 * wide + p * PAIR : 2 * wide + (p + 1) * PAIR]
            outs = []
            for h in range(2):
                mine = (lane >= HEAD_DIM) if h else (lane < HEAD_DIM)
                qm = jnp.where(mine, q, jnp.zeros((), BF16))
                s = jnp.where(allowed, dot_nt(qm, k), NEG_FILL)
                top = jnp.max(s, axis=1, keepdims=True)
                e = jnp.exp(s - top)
                l = jnp.sum(e, axis=1, keepdims=True)
                outs.append(dot(e.astype(BF16), v) / l)
                total = jnp.where(lane == 2 * p + h, top + jnp.log(l), total)
            mix_ref[rows, p * PAIR : (p + 1) * PAIR] = jnp.where(
                lane < HEAD_DIM, outs[0], outs[1]
            ).astype(BF16)
        lse_ref[:, rows] = jnp.transpose(total)[: lse_ref.shape[0], :]


def attend(normed, weight, bias, seg_col, seg_row):
    tokens, width = normed.shape
    wide = weight.shape[1] // 3
    return pl.pallas_call(
        attend_kernel,
        out_shape=(
            jax.ShapeDtypeStruct((tokens, 3 * wide), BF16),
            jax.ShapeDtypeStruct((tokens, wide), BF16),
            jax.ShapeDtypeStruct((8, tokens), F32),
        ),
        compiler_params=params(),
        name="attend",
    )(normed, weight, bias, seg_col, seg_row)


def attend_back_kernel(
    qkv_ref, mix_ref, da_ref, wo_ref, lse_ref, sc_ref, sr_ref, out_ref, sum_ref, do_ref, dk_ref, dv_ref
):
    tokens = qkv_ref.shape[0]
    wide = mix_ref.shape[1]
    pairs = wide // PAIR
    do_ref[...] = dot_nt(da_ref[...], wo_ref[...]).astype(BF16)
    scale = jnp.asarray(HEAD_DIM**-0.5, BF16)
    lane = iota((QBLOCK, PAIR), 1)
    head_of = iota((8, wide), 1) // HEAD_DIM
    select = jnp.where(head_of == iota((8, wide), 0), 1.0, 0.0).astype(F32)
    delta = lax.dot_general(
        select,
        do_ref[...].astype(F32) * mix_ref[...].astype(F32),
        (((1,), (1,)), ((), ())),
        precision=lax.Precision.HIGHEST,
        preferred_element_type=F32,
    )
    for p in range(pairs):
        dk_ref[...] = jnp.zeros_like(dk_ref)
        dv_ref[...] = jnp.zeros_like(dv_ref)
        cq = slice(p * PAIR, (p + 1) * PAIR)
        ck = slice(wide + p * PAIR, wide + (p + 1) * PAIR)
        cv = slice(2 * wide + p * PAIR, 2 * wide + (p + 1) * PAIR)
        for i in range(tokens // QBLOCK):
            lo, hi = window(i)
            r0 = i * QBLOCK
            rows = slice(r0, r0 + QBLOCK)
            allowed = (sc_ref[lo:hi, :] == sr_ref[:, rows]) & (
                iota((hi - lo, QBLOCK), 0) + lo <= iota((hi - lo, QBLOCK), 1) + r0
            )
            q = qkv_ref[rows, cq] * scale
            k = qkv_ref[lo:hi, ck]
            v = qkv_ref[lo:hi, cv]
            g = do_ref[rows, cq]
            dq = jnp.zeros((QBLOCK, PAIR), F32)
            for h in range(2):
                mine = (lane >= HEAD_DIM) if h else (lane < HEAD_DIM)
                qm = jnp.where(mine, q, jnp.zeros((), BF16))
                gm = jnp.where(mine, g, jnp.zeros((), BF16))
                head = 2 * p + h
                s = jnp.where(allowed, dot_nt(k, qm), NEG_FILL)
                probs = jnp.exp(s - lse_ref[head : head + 1, rows])
                dv_ref[lo:hi, :] += dot(probs.astype(BF16), gm)
                ds = (probs * (dot_nt(v, gm) - delta[head : head + 1, rows])).astype(BF16)
                dk_ref[lo:hi, :] += dot(ds, qm)
                dq = jnp.where(mine, dot_tn(ds, k), dq)
            out_ref[rows, cq] = (dq * (HEAD_DIM**-0.5)).astype(BF16)
        out_ref[:, ck] = dk_ref[...].astype(BF16)
        out_ref[:, cv] = dv_ref[...].astype(BF16)
    sum_ref[...] = jnp.broadcast_to(
        jnp.sum(out_ref[...].astype(F32), axis=0, keepdims=True), sum_ref.shape
    )


def attend_back(qkv, mix, dattn, wo, lse, seg_col, seg_row):
    tokens, wide = mix.shape
    return pl.pallas_call(
        attend_back_kernel,
        out_shape=(
            jax.ShapeDtypeStruct((tokens, 3 * wide), BF16),
            jax.ShapeDtypeStruct((8, 3 * wide), F32),
        ),
        scratch_shapes=[
            pltpu.VMEM((tokens, wide), BF16),
            pltpu.VMEM((tokens, PAIR), F32),
            pltpu.VMEM((tokens, PAIR), F32),
        ],
        compiler_params=params(),
        name="attend_back",
    )(qkv, mix, dattn, wo, lse, seg_col, seg_row)


def project_kernel(x_ref, m0_ref, m1_ref, m2_ref, wo_ref, vec_ref, hid_ref, moe_ref):
    wide = m0_ref.shape[1]
    hidden = x_ref[...].astype(F32) + vec_ref[0:1, :]
    for g, ref in enumerate((m0_ref, m1_ref, m2_ref)):
        hidden = hidden + dot(ref[...], wo_ref[g * wide : (g + 1) * wide, :])
    hid_ref[...] = hidden
    scaled, _ = norm_stats(hidden)
    moe_ref[...] = (scaled * vec_ref[1:2, :] + vec_ref[2:3, :]).astype(BF16)


def project(x, mixes, wo, vecs):
    tokens, width = x.shape
    wide = mixes[0].shape[1]
    row = lambda n: pl.BlockSpec((QBLOCK, n), lambda i: (i, 0))
    return pl.pallas_call(
        project_kernel,
        grid=(tokens // QBLOCK,),
        in_specs=[row(width), row(wide), row(wide), row(wide), whole(wo.shape), whole(vecs.shape)],
        out_specs=(row(width), row(width)),
        out_shape=(
            jax.ShapeDtypeStruct((tokens, width), F32),
            jax.ShapeDtypeStruct((tokens, width), BF16),
        ),
        compiler_params=params(),
        name="project",
    )(x, *mixes, wo, vecs)


def pack_kernel(base, target_ref, rows_ref, out_ref):
    count = out_ref.shape[0]
    start = base + pl.program_id(0) * count
    hot = iota((count, rows_ref.shape[0]), 0) + start == target_ref[...]
    out_ref[...] = dot(jnp.where(hot, 1.0, 0.0).astype(BF16), rows_ref[...]).astype(BF16)


def pack(rows, target_row, base, count):
    tokens, width = rows.shape
    return pl.pallas_call(
        functools.partial(pack_kernel, base),
        grid=(count // 512,),
        in_specs=[whole((1, tokens)), whole(rows.shape)],
        out_specs=pl.BlockSpec((512, width), lambda i: (i, 0)),
        out_shape=jax.ShapeDtypeStruct((count, width), BF16),
        compiler_params=params(),
        name="pack",
    )(target_row, rows)


def unpack_rows(target, refs):
    base = 0
    picked = None
    for ref in refs:
        count = ref.shape[0]
        hot = iota((target.shape[0], count), 1) + base == target
        part = dot(jnp.where(hot, 1.0, 0.0).astype(BF16), ref[...])
        picked = part if picked is None else picked + part
        base += count
    return picked


def middle_kernel(*refs):
    slots = refs[:CHUNKS]
    tgt_ref, hid_ref, dy_ref, vec_ref, dhid_ref, da_ref, sum_ref = refs[CHUNKS:]
    dmoe = unpack_rows(tgt_ref[...], slots)
    scaled, inverse = norm_stats(hid_ref[...])
    dhid = dy_ref[...].astype(F32) + norm_back(dmoe, scaled, inverse, vec_ref[1:2, :])
    dhid_ref[...] = dhid
    low = dhid.astype(BF16)
    da_ref[...] = low

    @pl.when(pl.program_id(0) == 0)
    def _():
        sum_ref[...] = jnp.zeros_like(sum_ref)

    sum_ref[0:1, :] += jnp.sum(low.astype(F32), axis=0, keepdims=True)
    sum_ref[1:2, :] += jnp.sum(dmoe * scaled, axis=0, keepdims=True)
    sum_ref[2:3, :] += jnp.sum(dmoe, axis=0, keepdims=True)


def middle(slots, target_col, hidden, dy, vecs):
    tokens, width = hidden.shape
    row = lambda n: pl.BlockSpec((QBLOCK, n), lambda i: (i, 0))
    return pl.pallas_call(
        middle_kernel,
        grid=(tokens // QBLOCK,),
        in_specs=[whole(s.shape) for s in slots] + [row(1), row(width), row(width), whole(vecs.shape)],
        out_specs=(row(width), row(width), whole((8, width))),
        out_shape=(
            jax.ShapeDtypeStruct((tokens, width), F32),
            jax.ShapeDtypeStruct((tokens, width), BF16),
            jax.ShapeDtypeStruct((8, width), F32),
        ),
        compiler_params=params(),
        name="middle",
    )(*slots, target_col, hidden, dy, vecs)


def output_kernel(*refs):
    slots = refs[:CHUNKS]
    tgt_ref, route_ref, hid_ref, moe_ref, router_ref, out_ref = refs[CHUNKS:]
    logits = dot(moe_ref[...], router_ref[...])
    chosen = jnp.sum(
        jnp.where(iota(logits.shape, 1) == route_ref[...], logits, 0.0), axis=1, keepdims=True
    )
    gate = jax.nn.sigmoid(chosen)
    out_ref[...] = (hid_ref[...] + gate * unpack_rows(tgt_ref[...], slots)).astype(BF16)


def finish_output(slots, target_col, route_col, hidden, moe_in, router):
    tokens, width = hidden.shape
    row = lambda n: pl.BlockSpec((QBLOCK, n), lambda i: (i, 0))
    return pl.pallas_call(
        output_kernel,
        grid=(tokens // QBLOCK,),
        in_specs=[whole(s.shape) for s in slots]
        + [row(1), row(1), row(width), row(width), whole(router.shape)],
        out_specs=row(width),
        out_shape=jax.ShapeDtypeStruct((tokens, width), BF16),
        compiler_params=params(),
        name="finish_output",
    )(*slots, target_col, route_col, hidden, moe_in, router)


def last_kernel(d0_ref, d1_ref, d2_ref, w0_ref, w1_ref, w2_ref, x_ref, dhid_ref, vec_ref, out_ref, sum_ref):
    grad = dot_nt(d0_ref[...], w0_ref[...])
    grad = grad + dot_nt(d1_ref[...], w1_ref[...])
    grad = grad + dot_nt(d2_ref[...], w2_ref[...])
    scaled, inverse = norm_stats(x_ref[...].astype(F32))
    out_ref[...] = dhid_ref[...] + norm_back(grad, scaled, inverse, vec_ref[0:1, :])

    @pl.when(pl.program_id(0) == 0)
    def _():
        sum_ref[...] = jnp.zeros_like(sum_ref)

    sum_ref[0:1, :] += jnp.sum(grad * scaled, axis=0, keepdims=True)
    sum_ref[1:2, :] += jnp.sum(grad, axis=0, keepdims=True)


def last(dqkvs, weights, x, dhid, vecs):
    tokens, width = x.shape
    row = lambda n: pl.BlockSpec((QBLOCK, n), lambda i: (i, 0))
    return pl.pallas_call(
        last_kernel,
        grid=(tokens // QBLOCK,),
        in_specs=[row(d.shape[1]) for d in dqkvs]
        + [whole(w.shape) for w in weights]
        + [row(width), row(width), whole(vecs.shape)],
        out_specs=(row(width), whole((8, width))),
        out_shape=(
            jax.ShapeDtypeStruct((tokens, width), F32),
            jax.ShapeDtypeStruct((8, width), F32),
        ),
        compiler_params=params(),
        name="last",
    )(*dqkvs, *weights, x, dhid, vecs)


def expert_kernel(aliased, *refs):
    x_ref, dy_ref, wi_ref, bi_ref, wo_ref, vec_ref = refs[:6]
    refs = refs[6 + aliased :]
    ret_ref, dmoe_ref, act_ref, dpre_ref, arr_ref, xall_ref, gbi_ref, sum_ref = refs[:8]
    accr_ref, accg_ref = refs[8:]
    step = pl.program_id(0)

    def gate_of():
        x = x_ref[...].astype(F32)
        return jax.nn.sigmoid(jnp.sum(x * vec_ref[1:2, :], axis=1, keepdims=True))

    @pl.when(step == 0)
    def _():
        arr_ref[...] = (dy_ref[...].astype(F32) * gate_of()).astype(BF16)
        xall_ref[...] = x_ref[...]
        accr_ref[...] = jnp.broadcast_to(vec_ref[0:1, :], accr_ref.shape)
        accg_ref[...] = jnp.zeros_like(accg_ref)

    pre = dot(x_ref[...], wi_ref[...]) + bi_ref[...]
    dact = dot_nt(arr_ref[...], wo_ref[...])
    phi = 0.5 * (1.0 + lax.erf(pre * SQRT_HALF))
    act = (pre * phi).astype(BF16)
    act_ref[...] = act
    accr_ref[...] += dot(act, wo_ref[...])
    slope = phi + pre * jnp.exp(-0.5 * pre * pre) * INV_ROOT_TAU
    dpre = (dact * slope).astype(BF16)
    dpre_ref[...] = dpre
    accg_ref[...] += dot_nt(dpre, wi_ref[...])
    gbi_ref[...] = jnp.broadcast_to(
        jnp.sum(dpre.astype(F32), axis=0, keepdims=True), gbi_ref.shape
    )

    @pl.when(step == pl.num_programs(0) - 1)
    def _():
        gate = gate_of()
        ret = accr_ref[...].astype(BF16)
        ret_ref[...] = ret
        dgate = jnp.sum(dy_ref[...].astype(F32) * ret.astype(F32), axis=1, keepdims=True)
        dlogit = (dgate * gate * (1.0 - gate)).astype(BF16).astype(F32)
        dmoe_ref[...] = (
            accg_ref[...].astype(BF16).astype(F32) + dlogit * vec_ref[1:2, :]
        ).astype(BF16)
        sum_ref[...] = jnp.zeros_like(sum_ref)
        sum_ref[0:1, :] = jnp.sum(x_ref[...].astype(F32) * dlogit, axis=0, keepdims=True)
        sum_ref[1:2, :] = jnp.sum(arr_ref[...].astype(F32), axis=0, keepdims=True)


def expert_chunk(chunk, total, x, dy, w_in, b_in, w_out, vecs, kept):
    rows, width = x.shape
    hidden = w_in.shape[1]
    block = 512
    aliased = len(kept)
    any_spec = pl.BlockSpec(memory_space=pl.ANY)
    return pl.pallas_call(
        functools.partial(expert_kernel, aliased),
        grid=(hidden // block,),
        in_specs=[
            whole(x.shape),
            whole(dy.shape),
            pl.BlockSpec((width, block), lambda f: (0, f)),
            pl.BlockSpec((1, block), lambda f: (0, f)),
            pl.BlockSpec((block, width), lambda f: (f, 0)),
            whole(vecs.shape),
        ]
        + [any_spec] * aliased,
        out_specs=(
            whole((rows, width)),
            whole((rows, width)),
            pl.BlockSpec((rows, block), lambda f: (chunk, f)),
            pl.BlockSpec((rows, block), lambda f: (chunk, f)),
            pl.BlockSpec((rows, width), lambda f: (chunk, 0)),
            pl.BlockSpec((rows, width), lambda f: (chunk, 0)),
            pl.BlockSpec((8, block), lambda f: (0, f)),
            whole((8, width)),
        ),
        out_shape=(
            jax.ShapeDtypeStruct((rows, width), BF16),
            jax.ShapeDtypeStruct((rows, width), BF16),
            jax.ShapeDtypeStruct((total, hidden), BF16),
            jax.ShapeDtypeStruct((total, hidden), BF16),
            jax.ShapeDtypeStruct((total, width), BF16),
            jax.ShapeDtypeStruct((total, width), BF16),
            jax.ShapeDtypeStruct((8, hidden), F32),
            jax.ShapeDtypeStruct((8, width), F32),
        ),
        scratch_shapes=[pltpu.VMEM((rows, width), F32), pltpu.VMEM((rows, width), F32)],
        input_output_aliases={6 + i: 2 + i for i in range(aliased)},
        compiler_params=params(),
        name="expert",
    )(x, dy, w_in, b_in, w_out, vecs, *kept)


def levels_of(devices):
    side = int(round((devices // 8) ** 0.5))
    return (devices // (2 * side * side), side, side, 2)


def cyclic(devices, sizes, axis, shift):
    stride = 1
    for size in sizes[axis + 1 :]:
        stride *= size
    pairs = []
    for i in range(devices):
        at = (i // stride) % sizes[axis]
        pairs.append((i, i + ((at + shift) % sizes[axis] - at) * stride))
    return pairs


def coordinate(sizes, axis):
    stride = 1
    for size in sizes[axis + 1 :]:
        stride *= size
    return (lax.axis_index("dp") // stride) % sizes[axis]


def gather_level(block, devices, sizes, axis, position):
    size = sizes[axis]
    mine = coordinate(sizes, axis)
    shape = block.shape[:position] + (size,) + block.shape[position:]
    out = jnp.zeros(shape, block.dtype)
    for shift in range(size):
        part = block if shift == 0 else lax.ppermute(block, "dp", cyclic(devices, sizes, axis, shift))
        at = [0] * len(shape)
        at[position] = (mine - shift) % size
        out = lax.dynamic_update_slice(out, jnp.expand_dims(part, position), at)
    return out


def gather_rows(block, devices):
    sizes = levels_of(devices)
    rows, width = block.shape
    cut = (width // 256) * 128
    first, second = block[:, :cut], block[:, cut:]
    first = gather_level(first, devices, sizes, 0, 0)
    second = gather_level(second, devices, sizes, 0, 0)
    first = gather_level(first, devices, sizes, 1, 1)
    second = gather_level(second, devices, sizes, 2, 1)
    first = gather_level(first, devices, sizes, 2, 2)
    second = gather_level(second, devices, sizes, 1, 1)
    both = jnp.concatenate([first, second], axis=-1)
    both = gather_level(both, devices, sizes, 3, 3)
    return both.reshape(devices * rows, width)


def scatter_level(block, devices, sizes, axis, position):
    size = sizes[axis]
    mine = coordinate(sizes, axis)
    total = lax.dynamic_index_in_dim(block, mine, position, keepdims=False)
    for shift in range(1, size):
        part = lax.dynamic_index_in_dim(block, (mine + shift) % size, position, keepdims=False)
        got = lax.ppermute(part.astype(BF16), "dp", cyclic(devices, sizes, axis, shift))
        total = total + got.astype(F32)
    return total


def scatter_rows(grad, devices):
    sizes = levels_of(devices)
    rows, width = grad.shape
    grad = grad.reshape(sizes + (rows // devices, width))
    grad = scatter_level(grad, devices, sizes, 3, 3)
    cut = (width // 256) * 128
    first, second = grad[..., :cut], grad[..., cut:]
    first = scatter_level(first, devices, sizes, 2, 2)
    second = scatter_level(second, devices, sizes, 1, 1)
    first = scatter_level(first, devices, sizes, 1, 1)
    second = scatter_level(second, devices, sizes, 2, 1)
    first = scatter_level(first, devices, sizes, 0, 0)
    second = scatter_level(second, devices, sizes, 0, 0)
    return jnp.concatenate([first, second], axis=-1)


def exchange(slots, experts):
    rows, width = slots.shape
    out = lax.all_to_all(
        slots.reshape(experts, rows // experts, width), "dp", split_axis=0, concat_axis=0, tiled=True
    )
    return out.reshape(rows, width)


def per_device(
    inputs,
    cotangent,
    routes,
    segments,
    qkv_weight,
    query_bias,
    value_bias,
    out_weight,
    out_bias,
    attn_gain,
    attn_shift,
    moe_gain,
    moe_shift,
    router_weight,
    expert_in,
    expert_in_bias,
    expert_out,
    expert_out_bias,
):
    seq_count, tokens, width = inputs.shape
    devices = lax.axis_size("dp")
    experts = router_weight.shape[1]
    capacity = 2 * tokens // devices
    per_chunk = capacity // CHUNKS
    chunk_rows = experts * per_chunk
    wide = width // GROUPS
    rows = qkv_weight.shape[0]
    x = inputs.reshape(tokens, width)
    dy = cotangent.reshape(tokens, width)

    blocks = qkv_weight.reshape(rows, 3, GROUPS, wide).transpose(0, 2, 1, 3)
    blocks = blocks.reshape(rows, GROUPS, 3 * wide).astype(BF16)
    early = jnp.stack([attn_gain, attn_shift, query_bias, value_bias], axis=1).astype(BF16)
    early = jnp.pad(early, ((0, 0), (0, 128 - early.shape[1])))
    late = jnp.concatenate(
        [router_weight, out_bias[:, None], moe_gain[:, None], moe_shift[:, None]], axis=1
    ).astype(BF16)
    late = jnp.pad(late, ((0, 0), (0, -late.shape[1] % 128)))
    full_early = gather_rows(jnp.concatenate([blocks[:, 0], early], axis=1), devices)
    full_late = gather_rows(
        jnp.concatenate([blocks[:, 1], blocks[:, 2], out_weight.astype(BF16), late], axis=1), devices
    )
    weights = (full_early[:, : 3 * wide], full_late[:, : 3 * wide], full_late[:, 3 * wide : 6 * wide])
    proj_out = full_late[:, 6 * wide : 6 * wide + width]
    router = full_late[:, 6 * wide + width :]
    early_rows = full_early[:, 3 * wide : 3 * wide + 8].astype(F32).T
    late_rows = router.astype(F32).T
    vecs = jnp.pad(late_rows[experts : experts + 3], ((0, 5), (0, 0)))
    router_row = lax.dynamic_index_in_dim(late_rows, lax.axis_index("dp"), 0, keepdims=True)

    route = routes.reshape(tokens)
    onehot = route[:, None] == jnp.arange(experts, dtype=jnp.int32)[None, :]
    place = jnp.arange(tokens, dtype=jnp.int32)
    earlier = jnp.dot(
        (place[None, :] < place[:, None]).astype(BF16),
        onehot.astype(BF16),
        preferred_element_type=F32,
    )
    slot = jnp.sum(jnp.where(onehot, earlier, 0.0), axis=1).astype(jnp.int32)
    target = (slot // per_chunk) * chunk_rows + route * per_chunk + slot % per_chunk
    target_row, target_col = target[None, :], target[:, None]

    dys = [exchange(pack(dy, target_row, c * chunk_rows, chunk_rows), experts) for c in range(CHUNKS)]
    w_in = expert_in[0].astype(BF16)
    w_out = expert_out[0].astype(BF16)

    seg_row = segments.reshape(1, tokens)
    seg_col = segments.reshape(tokens, 1)
    scaled, _ = norm_stats(x.astype(F32))
    normed = (scaled * early_rows[0:1] + early_rows[1:2]).astype(BF16)
    qkvs, mixes, lses = [], [], []
    for g in range(GROUPS):
        cols = slice(g * wide, (g + 1) * wide)
        bias = jnp.concatenate(
            [early_rows[2:3, cols], jnp.zeros((1, wide), F32), early_rows[3:4, cols]], axis=1
        )
        qkv, mix, lse = attend(normed, weights[g], bias, seg_col, seg_row)
        qkvs.append(qkv)
        mixes.append(mix)
        lses.append(lse)
    hidden, moe_in = project(x, mixes, proj_out, vecs)

    expert_vecs = jnp.concatenate([expert_out_bias, router_row, jnp.zeros((6, width), F32)], axis=0)
    returned, dmoes, kept = [], [], ()
    dbias_in = dsums = 0.0
    received = [
        exchange(pack(moe_in, target_row, c * chunk_rows, chunk_rows), experts) for c in range(CHUNKS)
    ]
    for c in range(CHUNKS):
        ret, dmoe, *kept, dbias, sums = expert_chunk(
            c, CHUNKS * chunk_rows, received[c], dys[c], w_in, expert_in_bias, w_out, expert_vecs, kept
        )
        dmoes.append(exchange(dmoe, experts))
        returned.append(ret)
        dbias_in = dbias_in + dbias
        dsums = dsums + sums
    act, dpre, arrived, rows_in = kept
    grad_expert_out = dot_tn(act, arrived)
    grad_expert_in = dot_tn(rows_in, dpre)
    returned = [exchange(r, experts) for r in returned]

    dhid, dattn, mid_sums = middle(dmoes, target_col, hidden, dy, vecs)
    grad_out = scatter_rows(dot_tn(jnp.concatenate(mixes, axis=1), dattn), devices)
    dqkvs, qkv_sums, grad_qkv = [], [], []
    for g in range(GROUPS):
        dqkv, col_sums = attend_back(
            qkvs[g],
            mixes[g],
            dattn,
            proj_out[g * wide : (g + 1) * wide],
            lses[g],
            seg_col,
            seg_row,
        )
        dqkvs.append(dqkv)
        qkv_sums.append(col_sums[0:1])
        grad_qkv.append(scatter_rows(dot_tn(normed, dqkv), devices))
    grad_inputs, last_sums = last(dqkvs, weights, x, dhid, early_rows)
    output = finish_output(returned, target_col, route.reshape(tokens, 1), hidden, moe_in, router)

    grad_query = jnp.concatenate([s[:, :wide] for s in qkv_sums], axis=1)
    grad_value = jnp.concatenate([s[:, 2 * wide :] for s in qkv_sums], axis=1)
    small = jnp.concatenate(
        [grad_query, grad_value, mid_sums[0:3], last_sums[0:2], dsums[0:1]], axis=0
    )
    small = small.reshape(8, devices, rows).transpose(1, 0, 2).reshape(devices, 8 * rows)
    small = jnp.pad(small, ((0, 0), (0, -small.shape[1] % 128)))
    small = lax.all_to_all(small, "dp", split_axis=0, concat_axis=0, tiled=True)
    vectors = jnp.sum(small[:, : 7 * rows], axis=0).reshape(7, rows)
    grad_router = small[:, 7 * rows : 8 * rows].T
    grad_qkv = jnp.stack([g.reshape(rows, 3, wide) for g in grad_qkv], axis=2).reshape(rows, 3 * width)
    return (
        output.reshape(seq_count, tokens, width),
        grad_inputs.reshape(seq_count, tokens, width),
        grad_qkv,
        vectors[0],
        vectors[1],
        grad_out,
        vectors[2],
        vectors[5],
        vectors[6],
        vectors[3],
        vectors[4],
        grad_router,
        grad_expert_in[None],
        dbias_in[0:1],
        grad_expert_out[None],
        dsums[1:2],
    )


def solution(mesh):
    placed = (
        P("dp", None, None),
        P("dp", None, None),
        P("dp", None, None),
        P("dp", None),
        P("dp", None),
        P("dp"),
        P("dp"),
        P("dp", None),
        P("dp"),
        P("dp"),
        P("dp"),
        P("dp"),
        P("dp"),
        P("dp", None),
        P("dp", None, None),
        P("dp", None),
        P("dp", None, None),
        P("dp", None),
    )
    return jax.shard_map(
        per_device,
        mesh=mesh,
        in_specs=placed,
        out_specs=(
            P("dp", None, None),
            P("dp", None, None),
            P("dp", None),
            P("dp"),
            P("dp"),
            P("dp", None),
            P("dp"),
            P("dp"),
            P("dp"),
            P("dp"),
            P("dp"),
            P("dp", None),
            P("dp", None, None),
            P("dp", None),
            P("dp", None, None),
            P("dp", None),
        ),
        check_vma=False,
    )
```

time: 1050 us -> 595 us (0.57)
  matrix products: 326 us -> 42.1 us
  blocking collectives: 249 us -> 44 us
  Pallas kernels: 0 us -> 184 us
  starting transfers between devices: 12.8 us -> 129 us
  waiting for transfers between devices: 228 us -> 112 us
  other arithmetic: 118 us -> 36.4 us
  local copies, waits for them, and re-layouts: 88.8 us -> 37.1 us
  between operations: 15.1 us -> 3.02 us
    dot_general x27 -> x7, matrix products: 326 us -> 42.1 us  [the longest x6 41.5 us: dot_tn(): lax.dot_general(a, b, (((0,), (0,)), ((), ())), preferred_element_type=F32)]
    pallas_call x0 -> x16, Pallas kernels: none -> 184 us  [the longest x2 62.1 us: expert_chunk(): pl.pallas_call(functools.partial(expert_kernel, aliased), grid=(hidden //...]
    ppermute x0 -> x66, starting transfers between devices: none -> 91.8 us  [the longest x44 51.3 us: scatter_level(): lax.ppermute(part.astype(BF16), 'dp', cyclic(devices, sizes, axis, shift))]
    reduce_scatter x2 -> x0, waiting for transfers between devices: 87.7 us -> none  [the longest x1 87.6 us: per_device(): lax.psum_scatter(grad_proj_qkv, 'dp', scatter_dimension=0, tiled=True)]
    all_gather x1 -> x0, blocking collectives: 84.9 us -> none  [per_device(): lax.all_gather(router_weight.astype(jnp.bfloat16), 'dp', axis=0, tiled=True)]
    unnamed x2 -> x0, blocking collectives: 81.2 us -> none
    all_to_all x3 -> x8, waiting for transfers between devices: 140 us -> 64 us  [the longest x7 64 us: exchange(): lax.all_to_all(slots.reshape(experts, rows // experts, width), 'dp', spli...]
    ppermute x0 -> x66, waiting for transfers between devices: none -> 48.3 us  [the longest x22 34.7 us: gather_level(): lax.ppermute(block, 'dp', cyclic(devices, sizes, axis, shift))]
  transfers between devices with their start and end apart: 8 -> 74, of which waited for: 3 -> 25; matrix products, arithmetic and copies ran while one was open for 35% -> 19% of each run, Pallas kernels for 0% -> 26%
where the time goes in v1:
time: 595 us; the launch traced here: 588 us
  Pallas kernels  184 us (31%)
  starting transfers between devices  129 us (22%)
  waiting for transfers between devices  112 us (19%)
  blocking collectives  44 us (7%)
  matrix products  42.1 us (7%)
  local copies, waits for them, and re-layouts  37.1 us (6%)
  other arithmetic  36.4 us (6%)
    all_to_all x7, waiting for transfers between devices, exchange(): lax.all_to_all(slots.reshape(experts, rows // experts, width), 'dp', spli...  64 us
    pallas_call x2, Pallas kernels, expert_chunk(): pl.pallas_call(functools.partial(expert_kernel, aliased), grid=(hidden //...  62.1 us
    ppermute x44, starting transfers between devices, scatter_level(): lax.ppermute(part.astype(BF16), 'dp', cyclic(devices, sizes, axis, shift))  51.3 us
    all_to_all x1, blocking collectives, exchange(): lax.all_to_all(slots.reshape(experts, rows // experts, width), 'dp', spli...  44 us
    dot_general x6, matrix products, dot_tn(): lax.dot_general(a, b, (((0,), (0,)), ((), ())), preferred_element_type=F32)  41.5 us
    ppermute x22, starting transfers between devices, gather_level(): lax.ppermute(block, 'dp', cyclic(devices, sizes, axis, shift))  40.5 us
    pallas_call x3, Pallas kernels, attend_back(): pl.pallas_call(attend_back_kernel, out_shape=(jax.ShapeDtypeStruct((token...  39.1 us
    ppermute x22, waiting for transfers between devices, gather_level(): lax.ppermute(block, 'dp', cyclic(devices, sizes, axis, shift))  34.7 us
  transfers between devices with their start and end apart: 74, of which 25 were waited for; matrix products, arithmetic and copies ran while one was open for 19% of the time, Pallas kernels for 26%

profile of v1, /device:TPU:0, one launch (start us, length us, event | category | flops | bytes accessed | tf_op | source)
XLA Modules:
  0.0 588.1 jit_solution(9376740909365500631)
XLA Ops:
  11.3 4.3 pack.5
  15.6 5.7 all-to-all-start.1
  27.0 21.4 %collective-permute-done.2 = bf16[24,384]{1,0:T(8,128)(2,1)S(1)} collective-permute-done((bf16[24,384]{1,0:T(8,128)(2,1)S(1)}, bf16[24,384]{1,0:T(8,128)(2,1)S(1)}, u32[]{:S(2)}, u32[]{:S(2)}) %collective-permute-start.2) | collective-permute-done | bytes 18464 | tf_op jit(solution)/shard_map/ppermute | solution.py:470
  48.3 11.1 %collective-permute-start.6 = (bf16[24,512]{1,0:T(8,128)(2,1)S(1)}, bf16[24,512]{1,0:T(8,128)(2,1)S(1)}, u32[]{:S(2)}, u32[]{:S(2)}) collective-permute-start(bf16[24,512]{1,0:T(8,128)(2,1)S(1)} %get-tuple-element.147), channel_id=1, source_target_pairs={{0,16},{1,17},{2,18},{3,19},{4,20},{5,21},{6,22},{7,23},{8,24},{9,... | collective-permute-start | bytes 73736 | tf_op jit(solution)/shard_map/ppermute | solution.py:470
  77.0 4.9 collective-permute-done.4
  85.4 5.2 collective-permute-done.15
  93.9 4.3 pack.7
  99.3 4.3 all-to-all-start.4
  113.4 10.4 %attend.3 = (bf16[1024,768]{1,0:T(8,128)(2,1)}, bf16[1024,256]{1,0:T(8,128)(2,1)}, f32[8,1024]{1,0:T(8,128)}) custom-call(bf16[1024,768]{1,0:T(8,128)(2,1)} %fusion.6.x_ref, bf16[768,768]{1,0:T(8,128)(2,1)} %slice.238.w_ref.w0_ref, f32[1,768]{1,0:T(1,128)} %get-tuple-element.208.b_ref, s32[1024,1]{1,0:T(8,128)} %copy.221.sc_ref, s32[1,1024]{1,0:T(1,128)} %sr_ref.11), custom_call_target="tpu_custom_call" | custom-call | tf_op jit(solution)/shard_map/attend/pallas_call | solution.py:107
  133.3 10.7 %attend.5 = (bf16[1024,768]{1,0:T(8,128)(2,1)}, bf16[1024,256]{1,0:T(8,128)(2,1)}, f32[8,1024]{1,0:T(8,128)}) custom-call(bf16[1024,768]{1,0:T(8,128)(2,1)} %fusion.6.x_ref, bf16[768,768]{1,0:T(8,128)(2,1)} %get-tuple-element.155.w_ref.w2_ref, f32[1,768]{1,0:T(1,128)} %get-tuple-element.206.b_ref, s32[1024,1]{1,0:T(8,128)} %copy.221.sc_ref, s32[1,1024]{1,0:T(1,128)} %sr_ref.11), custom_call_target="tpu_custom_call" | custom-call | tf_op jit(solution)/shard_map/attend/pallas_call | solution.py:107
  143.9 10.4 %attend.4 = (bf16[1024,768]{1,0:T(8,128)(2,1)}, bf16[1024,256]{1,0:T(8,128)(2,1)}, f32[8,1024]{1,0:T(8,128)}) custom-call(bf16[1024,768]{1,0:T(8,128)(2,1)} %fusion.6.x_ref, bf16[768,768]{1,0:T(8,128)(2,1)} %get-tuple-element.156.w_ref.w1_ref, f32[1,768]{1,0:T(1,128)} %get-tuple-element.207.b_ref, s32[1024,1]{1,0:T(8,128)} %copy.221.sc_ref, s32[1,1024]{1,0:T(1,128)} %sr_ref.11), custom_call_target="tpu_custom_call" | custom-call | tf_op jit(solution)/shard_map/attend/pallas_call | solution.py:107
  154.4 6.0 %project.1 = (f32[1024,768]{1,0:T(8,128)}, bf16[1024,768]{1,0:T(8,128)(2,1)}) custom-call(bf16[1024,768]{1,0:T(8,128)(2,1)} %bitcast.388, bf16[1024,256]{1,0:T(8,128)(2,1)} %get-tuple-element.54.m0_ref.mix_ref, bf16[1024,256]{1,0:T(8,128)(2,1)} %get-tuple-element.55.m1_ref.mix_ref, bf16[1024,256]{1,0:T(8,128)(2,1)} %get-tuple-element.56.m2_ref.mix_ref, ...), custom_call_target="tpu_custom_call" | custom-call | tf_op jit(solution)/shard_map/project/pallas_call | solution.py:206
  160.4 4.3 pack.4
  164.7 6.2 %all-to-all-start = ((bf16[32,32,768]{2,1,0:T(8,128)(2,1)}), bf16[32,32,768]{2,1,0:T(8,128)(2,1)S(1)}, u32[]{:S(2)}, u32[]{:S(2)}) async-start(bf16[32,32,768]{2,1,0:T(8,128)(2,1)} %bitcast.399), calls=%async_computation | async-start | bytes 3145728 | tf_op jit(solution)/shard_map/all_to_all | solution.py:522
  170.9 4.3 pack.6
  175.2 33.3 %all-to-all-done = bf16[32,32,768]{2,1,0:T(8,128)(2,1)S(1)} async-done(((bf16[32,32,768]{2,1,0:T(8,128)(2,1)}), bf16[32,32,768]{2,1,0:T(8,128)(2,1)S(1)}, u32[]{:S(2)}, u32[]{:S(2)}) %all-to-all-start) | async-done | bytes 1572896 | tf_op jit(solution)/shard_map/all_to_all | solution.py:522
  212.4 6.3 %convert_bitcast_fusion.refs_4_ = bf16[3072,768]{1,0:T(8,128)(2,1)} fusion(f32[1,3072,768]{2,1,0:T(8,128)} %param.34), kind=kLoop, calls=%fused_computation.2 | loop fusion | flops 2359296 | bytes 14155776 | tf_op jit(solution)/shard_map/convert_element_type | solution.py:593
  218.7 6.6 %convert_bitcast_fusion.1.refs_2_ = bf16[768,3072]{1,0:T(8,128)(2,1)} fusion(f32[1,768,3072]{2,1,0:T(8,128)} %param.32), kind=kLoop, calls=%fused_computation.3 | loop fusion | flops 2359296 | bytes 14155776 | tf_op jit(solution)/shard_map/convert_element_type | solution.py:592
  226.3 31.0 %expert.2 = (bf16[1024,768]{1,0:T(8,128)(2,1)}, bf16[1024,768]{1,0:T(8,128)(2,1)}, bf16[2048,3072]{1,0:T(8,128)(2,1)}, bf16[2048,3072]{1,0:T(8,128)(2,1)}, bf16[...) custom-call(bf16[1024,768]{1,0:T(8,128)(2,1)} %bitcast.402, ...), custom_call_target="tpu_custom_call" | custom-call | tf_op jit(solution)/shard_map/expert/pallas_call | solution.py:402
  258.5 31.2 %expert.3 = (bf16[1024,768]{1,0:T(8,128)(2,1)}, bf16[1024,768]{1,0:T(8,128)(2,1)}, bf16[2048,3072]{1,0:T(8,128)(2,1)}, bf16[2048,3072]{1,0:T(8,128)(2,1)}, bf16[...) custom-call(bf16[1024,768]{1,0:T(8,128)(2,1)} %bitcast.393, ...), custom_call_target="tpu_custom_call", output_to_operand_aliasing={{2}: (6, {}), {3}: (7, {}), {4}: (8, {}), {5}: (9, {})} | custom-call | tf_op jit(solution)/shard_map/expert/pallas_call | solution.py:402
  289.6 44.0 %all_to_all.52 = bf16[32,32,768]{2,1,0:T(8,128)(2,1)} all-to-all(bf16[32,32,768]{2,1,0:T(8,128)(2,1)} %bitcast.410), channel_id=1, replica_groups=mesh['dp'=32] {'dp'}, dimensions={0} | all-to-all | bytes 3145728 | tf_op jit(solution)/shard_map/all_to_all | solution.py:522
  348.0 26.3 %all-to-all-done.6 = bf16[32,32,768]{2,1,0:T(8,128)(2,1)S(1)} async-done(((bf16[32,32,768]{2,1,0:T(8,128)(2,1)}), bf16[32,32,768]{2,1,0:T(8,128)(2,1)S(1)}, u32[]{:S(2)}, u32[]{:S(2)}) %all-to-all-start.6) | async-done | bytes 1572896 | tf_op jit(solution)/shard_map/all_to_all | solution.py:522
  378.4 16.3 %convolution_bitcast_fusion = f32[1,3072,768]{2,1,0:T(8,128)} fusion(bf16[2048,3072]{1,0:T(8,128)(2,1)} %get-tuple-element.90, bf16[2048,768]{1,0:T(8,128)(2,1)} %get-tuple-element.91), kind=kOutput, calls=%fused_computation | convolution fusion | flops 9663676416 | bytes 25165824 | tf_op jit(solution)/shard_map/dot_general | solution.py:34
  396.3 15.3 %convolution_bitcast_fusion.1 = f32[1,768,3072]{2,1,0:T(8,128)} fusion(bf16[2048,768]{1,0:T(8,128)(2,1)S(1)} %copy-done.8, bf16[2048,3072]{1,0:T(8,128)(2,1)} %get-tuple-element.87), kind=kOutput, calls=%fused_computation.1 | convolution fusion | flops 9663676416 | bytes 25165824 | tf_op jit(solution)/shard_map/dot_general | solution.py:34
  411.5 4.4 all-to-all-done.5
  420.4 10.1 %middle.1 = (f32[1024,768]{1,0:T(8,128)}, bf16[1024,768]{1,0:T(8,128)(2,1)}, f32[8,768]{1,0:T(8,128)}) custom-call(bf16[1024,768]{1,0:T(8,128)(2,1)} %bitcast.396, bf16[1024,768]{1,0:T(8,128)(2,1)} %bitcast.395, s32[1024,1]{1,0:T(8,128)} %fusion.27.refs_2_, f32[1024,768]{1,0:T(8,128)} %get-tuple-element.64.refs_4_.refs_3_, bf16[1024,768]{1,0:T(8,128)(2,1)} %bitcast.392, ...), custom_call_target="tpu_custom_call" | custom-call | tf_op jit(solution)/shard_map/middle/pallas_call | solution.py:274
  434.6 12.9 %attend_back.5 = (bf16[1024,768]{1,0:T(8,128)(2,1)}, f32[8,768]{1,0:T(8,128)}) custom-call(bf16[1024,768]{1,0:T(8,128)(2,1)} %get-tuple-element.74.qkv_ref, bf16[1024,256]{1,0:T(8,128)(2,1)} %get-tuple-element.56.m2_ref.mix_ref, bf16[1024,768]{1,0:T(8,128)(2,1)} %get-tuple-element.68.da_ref, bf16[256,768]{1,0:T(8,128)(2,1)} %get-tuple-element.148.wo_ref, ...), custom_call_target="tpu_custom_call" | custom-call | tf_op jit(solution)/shard_map/attend_back/pallas_call | solution.py:176
  447.5 13.1 %attend_back.4 = (bf16[1024,768]{1,0:T(8,128)(2,1)}, f32[8,768]{1,0:T(8,128)}) custom-call(bf16[1024,768]{1,0:T(8,128)(2,1)} %get-tuple-element.71.qkv_ref, bf16[1024,256]{1,0:T(8,128)(2,1)} %get-tuple-element.55.m1_ref.mix_ref, bf16[1024,768]{1,0:T(8,128)(2,1)} %get-tuple-element.68.da_ref, bf16[256,768]{1,0:T(8,128)(2,1)} %get-tuple-element.149.wo_ref, ...), custom_call_target="tpu_custom_call" | custom-call | tf_op jit(solution)/shard_map/attend_back/pallas_call | solution.py:176
  460.6 13.1 %attend_back.3 = (bf16[1024,768]{1,0:T(8,128)(2,1)}, f32[8,768]{1,0:T(8,128)}) custom-call(bf16[1024,768]{1,0:T(8,128)(2,1)} %get-tuple-element.65.qkv_ref, bf16[1024,256]{1,0:T(8,128)(2,1)} %get-tuple-element.54.m0_ref.mix_ref, bf16[1024,768]{1,0:T(8,128)(2,1)} %get-tuple-element.68.da_ref, bf16[256,768]{1,0:T(8,128)(2,1)} %get-tuple-element.150.wo_ref, ...), custom_call_target="tpu_custom_call" | custom-call | tf_op jit(solution)/shard_map/attend_back/pallas_call | solution.py:176
  473.7 10.2 %last.1 = (f32[1024,768]{1,0:T(8,128)}, f32[8,768]{1,0:T(8,128)}) custom-call(bf16[1024,768]{1,0:T(8,128)(2,1)} %get-tuple-element.70.d0_ref, bf16[1024,768]{1,0:T(8,128)(2,1)} %get-tuple-element.73.d1_ref, bf16[1024,768]{1,0:T(8,128)(2,1)} %get-tuple-element.76.d2_ref, bf16[768,768]{1,0:T(8,128)(2,1)} %slice.238.w_ref.w0_ref, ...), custom_call_target="tpu_custom_call" | custom-call | tf_op jit(solution)/shard_map/last/pallas_call | solution.py:333
  498.4 6.1 %all-to-all-start.8 = ((f32[32,1,256]{2,1,0:T(1,128)}), f32[32,1,256]{2,1,0:T(1,128)S(1)}, u32[]{:S(2)}, u32[]{:S(2)}) async-start(f32[32,1,256]{2,1,0:T(1,128)} %copy.250), calls=%async_computation.8 | async-start | bytes 65536 | tf_op jit(solution)/shard_map/all_to_all | solution.py:656
  506.3 8.2 %finish_output.1 = bf16[1024,768]{1,0:T(8,128)(2,1)} custom-call(bf16[1024,768]{1,0:T(8,128)(2,1)} %bitcast.401, bf16[1024,768]{1,0:T(8,128)(2,1)} %bitcast.400, s32[1024,1]{1,0:T(8,128)} %fusion.27.refs_2_, s32[1024,1]{1,0:T(8,128)} %copy.238.refs_3_, f32[1024,768]{1,0:T(8,128)} %get-tuple-element.64.refs_4_.refs_3_, ...), custom_call_target="tpu_custom_call" | custom-call | tf_op jit(solution)/shard_map/finish_output/pallas_call | solution.py:303
  (419 shorter events, 183.3 us)
Async XLA Ops:
  2.0 63.5 %collective-permute-start.11 = (bf16[24,1152]{1,0:T(8,128)(2,1)S(1)}, bf16[24,1152]{1,0:T(8,128)(2,1)S(1)}, u32[]{:S(2)}, u32[]{:S(2)}) collective-permute-start(bf16[24,1152]{1,0:T(8,128)(2,1)S(1)} %get-tuple-element.143), channel_id=1, source_target_pairs={{0,8},{1,9},{2,10},{3,11},{4,12},{5,13},{6,14},{7,15},{8,16},{9,17... | collective-permute-start | bytes 165896 | tf_op jit(solution)/shard_map/ppermute | solution.py:470
  5.1 63.9 %collective-permute-start.12 = (bf16[24,1152]{1,0:T(8,128)(2,1)S(1)}, bf16[24,1152]{1,0:T(8,128)(2,1)S(1)}, u32[]{:S(2)}, u32[]{:S(2)}) collective-permute-start(bf16[24,1152]{1,0:T(8,128)(2,1)S(1)} %get-tuple-element.143), channel_id=1, source_target_pairs={{0,16},{1,17},{2,18},{3,19},{4,20},{5,21},{6,22},{7,23},{8,24},{9,... | collective-permute-start | bytes 165896 | tf_op jit(solution)/shard_map/ppermute | solution.py:470
  7.7 62.7 %collective-permute-start.13 = (bf16[24,1152]{1,0:T(8,128)(2,1)S(1)}, bf16[24,1152]{1,0:T(8,128)(2,1)S(1)}, u32[]{:S(2)}, u32[]{:S(2)}) collective-permute-start(bf16[24,1152]{1,0:T(8,128)(2,1)S(1)} %get-tuple-element.143), channel_id=1, source_target_pairs={{0,24},{1,25},{2,26},{3,27},{4,28},{5,29},{6,30},{7,31},{8,0},{9,1... | collective-permute-start | bytes 165896 | tf_op jit(solution)/shard_map/ppermute | solution.py:470
  9.0 14.2 %collective-permute-start = (bf16[24,384]{1,0:T(8,128)(2,1)S(1)}, bf16[24,384]{1,0:T(8,128)(2,1)S(1)}, u32[]{:S(2)}, u32[]{:S(2)}) collective-permute-start(bf16[24,384]{1,0:T(8,128)(2,1)S(1)} %slice.234), channel_id=1, source_target_pairs={{0,8},{1,9},{2,10},{3,11},{4,12},{5,13},{6,14},{7,15},{8,16},{9,17... | collective-permute-start | bytes 55304 | tf_op jit(solution)/shard_map/ppermute | solution.py:470
  9.7 17.1 %collective-permute-start.1 = (bf16[24,384]{1,0:T(8,128)(2,1)S(1)}, bf16[24,384]{1,0:T(8,128)(2,1)S(1)}, u32[]{:S(2)}, u32[]{:S(2)}) collective-permute-start(bf16[24,384]{1,0:T(8,128)(2,1)S(1)} %slice.234), channel_id=1, source_target_pairs={{0,16},{1,17},{2,18},{3,19},{4,20},{5,21},{6,22},{7,23},{8,24},{9,... | collective-permute-start | bytes 55304 | tf_op jit(solution)/shard_map/ppermute | solution.py:470
  15.6 83.6 %all-to-all-start.1 = ((bf16[32,32,768]{2,1,0:T(8,128)(2,1)}), bf16[32,32,768]{2,1,0:T(8,128)(2,1)}, u32[]{:S(2)}, u32[]{:S(2)}) async-start(bf16[32,32,768]{2,1,0:T(8,128)(2,1)} %bitcast.394), calls=%async_computation.1 | async-start | bytes 3145728 | tf_op jit(solution)/shard_map/all_to_all | solution.py:522
  23.2 25.1 %collective-permute-start.2 = (bf16[24,384]{1,0:T(8,128)(2,1)S(1)}, bf16[24,384]{1,0:T(8,128)(2,1)S(1)}, u32[]{:S(2)}, u32[]{:S(2)}) collective-permute-start(bf16[24,384]{1,0:T(8,128)(2,1)S(1)} %slice.234), channel_id=1, source_target_pairs={{0,24},{1,25},{2,26},{3,27},{4,28},{5,29},{6,30},{7,31},{8,0},{9,1... | collective-permute-start | bytes 55304 | tf_op jit(solution)/shard_map/ppermute | solution.py:470
  26.9 32.6 %collective-permute-start.5 = (bf16[24,512]{1,0:T(8,128)(2,1)S(1)}, bf16[24,512]{1,0:T(8,128)(2,1)S(1)}, u32[]{:S(2)}, u32[]{:S(2)}) collective-permute-start(bf16[24,512]{1,0:T(8,128)(2,1)S(1)} %get-tuple-element.147), channel_id=1, source_target_pairs={{0,8},{1,9},{2,10},{3,11},{4,12},{5,13},{6,14},{7,15},{8,16},{9,17... | collective-permute-start | bytes 73736 | tf_op jit(solution)/shard_map/ppermute | solution.py:470
  48.3 14.6 %collective-permute-start.6 = (bf16[24,512]{1,0:T(8,128)(2,1)S(1)}, bf16[24,512]{1,0:T(8,128)(2,1)S(1)}, u32[]{:S(2)}, u32[]{:S(2)}) collective-permute-start(bf16[24,512]{1,0:T(8,128)(2,1)S(1)} %get-tuple-element.147), channel_id=1, source_target_pairs={{0,16},{1,17},{2,18},{3,19},{4,20},{5,21},{6,22},{7,23},{8,24},{9,... | collective-permute-start | bytes 73736 | tf_op jit(solution)/shard_map/ppermute | solution.py:470
  62.9 9.1 %collective-permute-start.16 = (bf16[24,1280]{1,0:T(8,128)(2,1)S(1)}, bf16[24,1280]{1,0:T(8,128)(2,1)S(1)}, u32[]{:S(2)}, u32[]{:S(2)}) collective-permute-start(bf16[24,1280]{1,0:T(8,128)(2,1)S(1)} %get-tuple-element.145), channel_id=1, source_target_pairs={{0,8},{1,9},{2,10},{3,11},{4,12},{5,13},{6,14},{7,15},{8,16},{9,17... | collective-permute-start | bytes 184328 | tf_op jit(solution)/shard_map/ppermute | solution.py:470
  72.0 9.9 %collective-permute-start.14 = (bf16[4,24,1152]{2,1,0:T(8,128)(2,1)S(1)}, bf16[4,24,1152]{2,1,0:T(8,128)(2,1)S(1)}, u32[]{:S(2)}, u32[]{:S(2)}) collective-permute-start(bf16[4,24,1152]{2,1,0:T(8,128)(2,1)S(1)} %bitcast_dynamic-update-slice_fusion.24), channel_id=1, source_target_pairs={{0,4},{1,5},{2,6},{3,7},{4,0},{5,1},{6,2},{7,3},{8,12},{9,13},{10,... | collective-permute-start | bytes 663560 | tf_op jit(solution)/shard_map/ppermute | solution.py:470
  72.6 10.8 %collective-permute-start.19 = (bf16[4,24,1280]{2,1,0:T(8,128)(2,1)S(1)}, bf16[4,24,1280]{2,1,0:T(8,128)(2,1)S(1)}, u32[]{:S(2)}, u32[]{:S(2)}) collective-permute-start(bf16[4,24,1280]{2,1,0:T(8,128)(2,1)S(1)} %bitcast_dynamic-update-slice_fusion.20), channel_id=1, source_target_pairs={{0,2},{1,3},{2,0},{3,1},{4,6},{5,7},{6,4},{7,5},{8,10},{9,11},{10,... | collective-permute-start | bytes 737288 | tf_op jit(solution)/shard_map/ppermute | solution.py:470
  76.1 8.3 %collective-permute-start.9 = (bf16[4,2,24,512]{3,2,1,0:T(8,128)(2,1)S(1)}, bf16[4,2,24,512]{3,2,1,0:T(8,128)(2,1)S(1)}, u32[]{:S(2)}, u32[]{:S(2)}) collective-permute-start(bf16[4,2,24,512]{3,2,1,0:T(8,128)(2,1)S(1)} %bitcast_dynamic-update-slice_fusion.16), channel_id=1, source_target_pairs={{0,4},{1,5},{2,6},{3,7},{4,0},{5,1},{6,2},{7,3},{8,12},{9,13},{10,... | collective-permute-start | bytes 589832 | tf_op jit(solution)/shard_map/ppermute | solution.py:470
  81.9 8.7 %collective-permute-start.15 = (bf16[4,2,24,1152]{3,2,1,0:T(8,128)(2,1)S(1)}, bf16[4,2,24,1152]{3,2,1,0:T(8,128)(2,1)S(1)}, u32[]{:S(2)}, u32[]{:S(2)}) collective-permute-start(bf16[4,2,24,1152]{3,2,1,0:T(8,128)(2,1)S(1)} %bitcast_dynamic-update-slice_fusion.11), channel_id=1, source_target_pairs={{0,2},{1,3},{2,0},{3,1},{4,6},{5,7},{6,4},{7,5},{8,10},{9,11},{10,... | collective-permute-start | bytes 1327112 | tf_op jit(solution)/shard_map/ppermute | solution.py:470
  83.5 8.9 %collective-permute-start.20 = (bf16[4,2,24,1280]{3,2,1,0:T(8,128)(2,1)S(1)}, bf16[4,2,24,1280]{3,2,1,0:T(8,128)(2,1)S(1)}, u32[]{:S(2)}, u32[]{:S(2)}) collective-permute-start(bf16[4,2,24,1280]{3,2,1,0:T(8,128)(2,1)S(1)} %bitcast_dynamic-update-slice_fusion.9), channel_id=1, source_target_pairs={{0,4},{1,5},{2,6},{3,7},{4,0},{5,1},{6,2},{7,3},{8,12},{9,13},{10,... | collective-permute-start | bytes 1474568 | tf_op jit(solution)/shard_map/ppermute | solution.py:470
  85.4 23.1 %collective-permute-start.10 = (bf16[4,2,2,24,896]{4,3,2,1,0:T(8,128)(2,1)}, bf16[4,2,2,24,896]{4,3,2,1,0:T(8,128)(2,1)}, u32[]{:S(2)}, u32[]{:S(2)}) collective-permute-start(bf16[4,2,2,24,896]{4,3,2,1,0:T(8,128)(2,1)} %pad_maximum_fusion.1), channel_id=1, source_target_pairs={{0,1},{1,0},{2,3},{3,2},{4,5},{5,4},{6,7},{7,6},{8,9},{9,8},{10,11... | collective-permute-start | bytes 2064392 | tf_op jit(solution)/shard_map/ppermute | solution.py:470
  93.8 30.0 %collective-permute-start.21 = (bf16[4,2,2,24,2432]{4,3,2,1,0:T(8,128)(2,1)}, bf16[4,2,2,24,2432]{4,3,2,1,0:T(8,128)(2,1)}, u32[]{:S(2)}, u32[]{:S(2)}) collective-permute-start(bf16[4,2,2,24,2432]{4,3,2,1,0:T(8,128)(2,1)} %pad_maximum_fusion), channel_id=1, source_target_pairs={{0,1},{1,0},{2,3},{3,2},{4,5},{5,4},{6,7},{7,6},{8,9},{9,8},{10,11... | collective-permute-start | bytes 5603336 | tf_op jit(solution)/shard_map/ppermute | solution.py:470
  99.3 65.4 %all-to-all-start.4 = ((bf16[32,32,768]{2,1,0:T(8,128)(2,1)}), bf16[32,32,768]{2,1,0:T(8,128)(2,1)}, u32[]{:S(2)}, u32[]{:S(2)}) async-start(bf16[32,32,768]{2,1,0:T(8,128)(2,1)} %bitcast.397), calls=%async_computation.4 | async-start | bytes 3145728 | tf_op jit(solution)/shard_map/all_to_all | solution.py:522
  164.7 43.8 %all-to-all-start = ((bf16[32,32,768]{2,1,0:T(8,128)(2,1)}), bf16[32,32,768]{2,1,0:T(8,128)(2,1)S(1)}, u32[]{:S(2)}, u32[]{:S(2)}) async-start(bf16[32,32,768]{2,1,0:T(8,128)(2,1)} %bitcast.399), calls=%async_computation | async-start | bytes 3145728 | tf_op jit(solution)/shard_map/all_to_all | solution.py:522
  208.5 48.8 %all-to-all-start.3 = ((bf16[32,32,768]{2,1,0:T(8,128)(2,1)}), bf16[32,32,768]{2,1,0:T(8,128)(2,1)S(1)}, u32[]{:S(2)}, u32[]{:S(2)}) async-start(bf16[32,32,768]{2,1,0:T(8,128)(2,1)} %bitcast.398), calls=%async_computation.3 | async-start | bytes 3145728 | tf_op jit(solution)/shard_map/all_to_all | solution.py:522
  333.7 40.6 %all-to-all-start.6 = ((bf16[32,32,768]{2,1,0:T(8,128)(2,1)}), bf16[32,32,768]{2,1,0:T(8,128)(2,1)S(1)}, u32[]{:S(2)}, u32[]{:S(2)}) async-start(bf16[32,32,768]{2,1,0:T(8,128)(2,1)} %bitcast.88), calls=%async_computation.6 | async-start | bytes 3145728 | tf_op jit(solution)/shard_map/all_to_all | solution.py:522
  374.3 41.7 %all-to-all-start.5 = ((bf16[32,32,768]{2,1,0:T(8,128)(2,1)}), bf16[32,32,768]{2,1,0:T(8,128)(2,1)S(1)}, u32[]{:S(2)}, u32[]{:S(2)}) async-start(bf16[32,32,768]{2,1,0:T(8,128)(2,1)} %bitcast.406), calls=%async_computation.5 | async-start | bytes 3145728 | tf_op jit(solution)/shard_map/all_to_all | solution.py:522
  416.0 82.5 %all-to-all-start.2 = ((bf16[32,32,768]{2,1,0:T(8,128)(2,1)}), bf16[32,32,768]{2,1,0:T(8,128)(2,1)S(1)}, u32[]{:S(2)}, u32[]{:S(2)}) async-start(bf16[32,32,768]{2,1,0:T(8,128)(2,1)} %bitcast.405), calls=%async_computation.2 | async-start | bytes 3145728 | tf_op jit(solution)/shard_map/all_to_all | solution.py:522
  434.4 81.5 %collective-permute-start.55 = (bf16[4,2,2,24,768]{4,3,0,2,1:T(8,128)(2,1)}, bf16[4,2,2,24,768]{4,3,0,2,1:T(8,128)(2,1)}, u32[]{:S(2)}, u32[]{:S(2)}) collective-permute-start(bf16[4,2,2,24,768]{4,3,0,2,1:T(8,128)(2,1)} %fusion.24), channel_id=1, source_target_pairs={{0,1},{1,0},{2,3},{3,2},{4,5},{5,4},{6,7},{7,6},{8,9},{9,8},{10,11... | collective-permute-start | bytes 1769480 | tf_op jit(solution)/shard_map/ppermute | solution.py:499
  492.3 28.6 %collective-permute-start.22 = (bf16[4,2,2,24,768]{4,3,2,1,0:T(8,128)(2,1)}, bf16[4,2,2,24,768]{4,3,2,1,0:T(8,128)(2,1)}, u32[]{:S(2)}, u32[]{:S(2)}) collective-permute-start(bf16[4,2,2,24,768]{4,3,2,1,0:T(8,128)(2,1)} %fusion.21), channel_id=1, source_target_pairs={{0,1},{1,0},{2,3},{3,2},{4,5},{5,4},{6,7},{7,6},{8,9},{9,8},{10,11... | collective-permute-start | bytes 1769480 | tf_op jit(solution)/shard_map/ppermute | solution.py:499
  494.9 28.0 %collective-permute-start.33 = (bf16[4,2,2,24,768]{4,3,2,1,0:T(8,128)(2,1)}, bf16[4,2,2,24,768]{4,3,2,1,0:T(8,128)(2,1)}, u32[]{:S(2)}, u32[]{:S(2)}) collective-permute-start(bf16[4,2,2,24,768]{4,3,2,1,0:T(8,128)(2,1)} %fusion.22), channel_id=1, source_target_pairs={{0,1},{1,0},{2,3},{3,2},{4,5},{5,4},{6,7},{7,6},{8,9},{9,8},{10,11... | collective-permute-start | bytes 1769480 | tf_op jit(solution)/shard_map/ppermute | solution.py:499
  498.4 16.1 %all-to-all-start.8 = ((f32[32,1,256]{2,1,0:T(1,128)}), f32[32,1,256]{2,1,0:T(1,128)S(1)}, u32[]{:S(2)}, u32[]{:S(2)}) async-start(f32[32,1,256]{2,1,0:T(1,128)} %copy.250), calls=%async_computation.8 | async-start | bytes 65536 | tf_op jit(solution)/shard_map/all_to_all | solution.py:656
  505.9 19.3 %collective-permute-start.44 = (bf16[4,2,2,24,768]{4,3,2,1,0:T(8,128)(2,1)S(1)}, bf16[4,2,2,24,768]{4,3,2,1,0:T(8,128)(2,1)S(1)}, u32[]{:S(2)}, u32[]{:S(2)}) collective-permute-start(bf16[4,2,2,24,768]{4,3,2,1,0:T(8,128)(2,1)S(1)} %fusion.23), channel_id=1, source_target_pairs={{0,1},{1,0},{2,3},{3,2},{4,5},{5,4},{6,7},{7,6},{8,9},{9,8},{10,11... | collective-permute-start | bytes 1769480 | tf_op jit(solution)/shard_map/ppermute | solution.py:499
  517.6 9.3 %collective-permute-start.56 = (bf16[4,2,24,384]{3,2,0,1:T(8,128)(2,1)S(1)}, bf16[4,2,24,384]{3,2,0,1:T(8,128)(2,1)S(1)}, u32[]{:S(2)}, u32[]{:S(2)}) collective-permute-start(bf16[4,2,24,384]{3,2,0,1:T(8,128)(2,1)S(1)} %fusion.38), channel_id=1, source_target_pairs={{0,2},{1,3},{2,0},{3,1},{4,6},{5,7},{6,4},{7,5},{8,10},{9,11},{10,... | collective-permute-start | bytes 442376 | tf_op jit(solution)/shard_map/ppermute | solution.py:499
  519.3 10.5 %collective-permute-start.61 = (bf16[4,2,24,384]{3,2,0,1:T(8,128)(2,1)S(1)}, bf16[4,2,24,384]{3,2,0,1:T(8,128)(2,1)S(1)}, u32[]{:S(2)}, u32[]{:S(2)}) collective-permute-start(bf16[4,2,24,384]{3,2,0,1:T(8,128)(2,1)S(1)} %fusion.39), channel_id=1, source_target_pairs={{0,4},{1,5},{2,6},{3,7},{4,0},{5,1},{6,2},{7,3},{8,12},{9,13},{10,... | collective-permute-start | bytes 442376 | tf_op jit(solution)/shard_map/ppermute | solution.py:499
  541.6 41.6 %collective-permute-start.58 = (bf16[24,384]{1,0:T(8,128)(2,1)S(1)}, bf16[24,384]{1,0:T(8,128)(2,1)S(1)}, u32[]{:S(2)}, u32[]{:S(2)}) collective-permute-start(bf16[24,384]{1,0:T(8,128)(2,1)S(1)} %get-tuple-element.165), channel_id=1, source_target_pairs={{0,8},{1,9},{2,10},{3,11},{4,12},{5,13},{6,14},{7,15},{8,16},{9,17... | collective-permute-start | bytes 55304 | tf_op jit(solution)/shard_map/ppermute | solution.py:499
  543.2 41.5 %collective-permute-start.59 = (bf16[24,384]{1,0:T(8,128)(2,1)S(1)}, bf16[24,384]{1,0:T(8,128)(2,1)S(1)}, u32[]{:S(2)}, u32[]{:S(2)}) collective-permute-start(bf16[24,384]{1,0:T(8,128)(2,1)S(1)} %get-tuple-element.167), channel_id=1, source_target_pairs={{0,16},{1,17},{2,18},{3,19},{4,20},{5,21},{6,22},{7,23},{8,24},{9,... | collective-permute-start | bytes 55304 | tf_op jit(solution)/shard_map/ppermute | solution.py:499
  (83 other events, 558.0 us)

commit v2 on v1

--- a/solution.py
+++ b/solution.py
@@ -6,6 +6,7 @@
 from jax.experimental import pallas as pl
 from jax.experimental.pallas import tpu as pltpu
 from jax.sharding import PartitionSpec as P
+
 
 HEAD_DIM = 64
 PAIR = 2 * HEAD_DIM
@@ -71,7 +72,10 @@
     tokens = x_ref.shape[0]
     wide = mix_ref.shape[1]
     pairs = wide // PAIR
-    qkv_ref[...] = (dot(x_ref[...], w_ref[...]) + b_ref[...]).astype(BF16)
+    packed = dot(x_ref[...], w_ref[...])
+    qkv_ref[:, :wide] = (packed[:, :wide] + b_ref[2:3, :]).astype(BF16)
+    qkv_ref[:, wide : 2 * wide] = packed[:, wide : 2 * wide].astype(BF16)
+    qkv_ref[:, 2 * wide :] = (packed[:, 2 * wide :] + b_ref[3:4, :]).astype(BF16)
     lane = iota((QBLOCK, PAIR), 1)
     for i in range(tokens // QBLOCK):
         lo, hi = window(i)
@@ -101,11 +105,20 @@
         lse_ref[:, rows] = jnp.transpose(total)[: lse_ref.shape[0], :]
 
 
-def attend(normed, weight, bias, seg_col, seg_row):
+def attend(group, normed, weight, block, early_rows, seg_col, seg_row):
     tokens, width = normed.shape
-    wide = weight.shape[1] // 3
+    wide = width // GROUPS
     return pl.pallas_call(
         attend_kernel,
+        grid=(1,),
+        in_specs=[
+            whole(normed.shape),
+            pl.BlockSpec((width, 3 * wide), lambda i: (0, block)),
+            pl.BlockSpec((8, wide), lambda i: (0, group)),
+            whole(seg_col.shape),
+            whole(seg_row.shape),
+        ],
+        out_specs=(whole((tokens, 3 * wide)), whole((tokens, wide)), whole((8, tokens))),
         out_shape=(
             jax.ShapeDtypeStruct((tokens, 3 * wide), BF16),
             jax.ShapeDtypeStruct((tokens, wide), BF16),
@@ -113,7 +126,7 @@
         ),
         compiler_params=params(),
         name="attend",
-    )(normed, weight, bias, seg_col, seg_row)
+    )(normed, weight, early_rows, seg_col, seg_row)
 
 
 def attend_back_kernel(
@@ -171,10 +184,22 @@
     )
 
 
-def attend_back(qkv, mix, dattn, wo, lse, seg_col, seg_row):
+def attend_back(group, qkv, mix, dattn, weight, block, lse, seg_col, seg_row):
     tokens, wide = mix.shape
+    width = dattn.shape[1]
     return pl.pallas_call(
         attend_back_kernel,
+        grid=(1,),
+        in_specs=[
+            whole(qkv.shape),
+            whole(mix.shape),
+            whole(dattn.shape),
+            pl.BlockSpec((wide, width), lambda i: (group, block)),
+            whole(lse.shape),
+            whole(seg_col.shape),
+            whole(seg_row.shape),
+        ],
+        out_specs=(whole((tokens, 3 * wide)), whole((8, 3 * wide))),
         out_shape=(
             jax.ShapeDtypeStruct((tokens, 3 * wide), BF16),
             jax.ShapeDtypeStruct((8, 3 * wide), F32),
@@ -186,7 +211,7 @@
         ],
         compiler_params=params(),
         name="attend_back",
-    )(qkv, mix, dattn, wo, lse, seg_col, seg_row)
+    )(qkv, mix, dattn, weight, lse, seg_col, seg_row)
 
 
 def project_kernel(x_ref, m0_ref, m1_ref, m2_ref, wo_ref, vec_ref, hid_ref, moe_ref):
@@ -199,14 +224,15 @@
     moe_ref[...] = (scaled * vec_ref[1:2, :] + vec_ref[2:3, :]).astype(BF16)
 
 
-def project(x, mixes, wo, vecs):
+def project(x, mixes, weight, block, vecs):
     tokens, width = x.shape
     wide = mixes[0].shape[1]
     row = lambda n: pl.BlockSpec((QBLOCK, n), lambda i: (i, 0))
     return pl.pallas_call(
         project_kernel,
         grid=(tokens // QBLOCK,),
-        in_specs=[row(width), row(wide), row(wide), row(wide), whole(wo.shape), whole(vecs.shape)],
+        in_specs=[row(width), row(wide), row(wide), row(wide)]
+        + [pl.BlockSpec((width, width), lambda i: (0, block)), whole(vecs.shape)],
         out_specs=(row(width), row(width)),
         out_shape=(
             jax.ShapeDtypeStruct((tokens, width), F32),
@@ -214,7 +240,7 @@
         ),
         compiler_params=params(),
         name="project",
-    )(x, *mixes, wo, vecs)
+    )(x, *mixes, weight, vecs)
 
 
 def pack_kernel(base, target_ref, rows_ref, out_ref):
@@ -224,10 +250,10 @@
     out_ref[...] = dot(jnp.where(hot, 1.0, 0.0).astype(BF16), rows_ref[...]).astype(BF16)
 
 
-def pack(rows, target_row, base, count):
+def pack(rows, target_row, chunk, count):
     tokens, width = rows.shape
     return pl.pallas_call(
-        functools.partial(pack_kernel, base),
+        functools.partial(pack_kernel, chunk * count),
         grid=(count // 512,),
         in_specs=[whole((1, tokens)), whole(rows.shape)],
         out_specs=pl.BlockSpec((512, width), lambda i: (i, 0)),
@@ -297,19 +323,20 @@
     out_ref[...] = (hid_ref[...] + gate * unpack_rows(tgt_ref[...], slots)).astype(BF16)
 
 
-def finish_output(slots, target_col, route_col, hidden, moe_in, router):
+def finish_output(slots, target_col, route_col, hidden, moe_in, weight, at, count):
     tokens, width = hidden.shape
     row = lambda n: pl.BlockSpec((QBLOCK, n), lambda i: (i, 0))
     return pl.pallas_call(
         output_kernel,
         grid=(tokens // QBLOCK,),
         in_specs=[whole(s.shape) for s in slots]
-        + [row(1), row(1), row(width), row(width), whole(router.shape)],
+        + [row(1), row(1), row(width), row(width)]
+        + [pl.BlockSpec((width, count), lambda i: (0, at // count))],
         out_specs=row(width),
         out_shape=jax.ShapeDtypeStruct((tokens, width), BF16),
         compiler_params=params(),
         name="finish_output",
-    )(*slots, target_col, route_col, hidden, moe_in, router)
+    )(*slots, target_col, route_col, hidden, moe_in, weight)
 
 
 def last_kernel(d0_ref, d1_ref, d2_ref, w0_ref, w1_ref, w2_ref, x_ref, dhid_ref, vec_ref, out_ref, sum_ref):
@@ -327,14 +354,14 @@
     sum_ref[1:2, :] += jnp.sum(grad, axis=0, keepdims=True)
 
 
-def last(dqkvs, weights, x, dhid, vecs):
+def last(dqkvs, weights, blocks, x, dhid, vecs):
     tokens, width = x.shape
     row = lambda n: pl.BlockSpec((QBLOCK, n), lambda i: (i, 0))
     return pl.pallas_call(
         last_kernel,
         grid=(tokens // QBLOCK,),
         in_specs=[row(d.shape[1]) for d in dqkvs]
-        + [whole(w.shape) for w in weights]
+        + [pl.BlockSpec((width, width), functools.partial(lambda b, i: (0, b), b)) for b in blocks]
         + [row(width), row(width), whole(vecs.shape)],
         out_specs=(row(width), whole((8, width))),
         out_shape=(
@@ -458,29 +485,38 @@
     stride = 1
     for size in sizes[axis + 1 :]:
         stride *= size
-    return (lax.axis_index("dp") // stride) % sizes[axis]
+    return lax.rem(lax.div(lax.axis_index("dp"), stride), sizes[axis])
+
+
+def shifted(block, devices, sizes, axis):
+    parts = [block]
+    for shift in range(1, sizes[axis]):
+        parts.append(lax.ppermute(block, "dp", cyclic(devices, sizes, axis, shift)))
+    return parts
+
+
+def in_order(parts, mine, position):
+    size = len(parts)
+    slots = []
+    for j in range(size):
+        back = lax.rem(mine + (size - j), size)
+        slot = parts[0]
+        for shift in range(1, size):
+            slot = jnp.where(back == shift, parts[shift], slot)
+        slots.append(slot)
+    return jnp.stack(slots, axis=position)
 
 
 def gather_level(block, devices, sizes, axis, position):
-    size = sizes[axis]
-    mine = coordinate(sizes, axis)
-    shape = block.shape[:position] + (size,) + block.shape[position:]
-    out = jnp.zeros(shape, block.dtype)
-    for shift in range(size):
-        part = block if shift == 0 else lax.ppermute(block, "dp", cyclic(devices, sizes, axis, shift))
-        at = [0] * len(shape)
-        at[position] = (mine - shift) % size
-        out = lax.dynamic_update_slice(out, jnp.expand_dims(part, position), at)
-    return out
+    return in_order(shifted(block, devices, sizes, axis), coordinate(sizes, axis), position)
 
 
 def gather_rows(block, devices):
     sizes = levels_of(devices)
     rows, width = block.shape
     cut = (width // 256) * 128
-    first, second = block[:, :cut], block[:, cut:]
-    first = gather_level(first, devices, sizes, 0, 0)
-    second = gather_level(second, devices, sizes, 0, 0)
+    block = gather_level(block, devices, sizes, 0, 0)
+    first, second = block[..., :cut], block[..., cut:]
     first = gather_level(first, devices, sizes, 1, 1)
     second = gather_level(second, devices, sizes, 2, 1)
     first = gather_level(first, devices, sizes, 2, 2)
@@ -490,38 +526,43 @@
     return both.reshape(devices * rows, width)
 
 
-def scatter_level(block, devices, sizes, axis, position):
+def scatter_level(blocks, devices, sizes, axis, position):
     size = sizes[axis]
     mine = coordinate(sizes, axis)
-    total = lax.dynamic_index_in_dim(block, mine, position, keepdims=False)
+    totals = [lax.dynamic_index_in_dim(block, mine, position, keepdims=False) for block in blocks]
     for shift in range(1, size):
-        part = lax.dynamic_index_in_dim(block, (mine + shift) % size, position, keepdims=False)
-        got = lax.ppermute(part.astype(BF16), "dp", cyclic(devices, sizes, axis, shift))
-        total = total + got.astype(F32)
-    return total
-
-
-def scatter_rows(grad, devices):
+        other = lax.rem(mine + shift, size)
+        parts = [
+            lax.dynamic_index_in_dim(block, other, position, keepdims=False).astype(BF16) for block in blocks
+        ]
+        part = jnp.concatenate(parts, axis=-1) if len(parts) > 1 else parts[0]
+        got = lax.ppermute(part, "dp", cyclic(devices, sizes, axis, shift))
+        base = 0
+        for n, total in enumerate(totals):
+            width = total.shape[-1]
+            totals[n] = total + got[..., base : base + width].astype(F32)
+            base += width
+    return totals
+
+
+def scatter_rows(first, second, devices):
     sizes = levels_of(devices)
-    rows, width = grad.shape
-    grad = grad.reshape(sizes + (rows // devices, width))
-    grad = scatter_level(grad, devices, sizes, 3, 3)
-    cut = (width // 256) * 128
-    first, second = grad[..., :cut], grad[..., cut:]
+    count = len(first)
+    both = [g.reshape(sizes + (g.shape[0] // devices, g.shape[1])) for g in first + second]
+    both = scatter_level(both, devices, sizes, 3, 3)
+    first, second = both[:count], both[count:]
     first = scatter_level(first, devices, sizes, 2, 2)
-    second = scatter_level(second, devices, sizes, 1, 1)
+    if second:
+        second = scatter_level(second, devices, sizes, 1, 1)
     first = scatter_level(first, devices, sizes, 1, 1)
-    second = scatter_level(second, devices, sizes, 2, 1)
-    first = scatter_level(first, devices, sizes, 0, 0)
-    second = scatter_level(second, devices, sizes, 0, 0)
-    return jnp.concatenate([first, second], axis=-1)
+    if second:
+        second = scatter_level(second, devices, sizes, 2, 1)
+    return scatter_level(first + second, devices, sizes, 0, 0)
 
 
 def exchange(slots, experts):
     rows, width = slots.shape
-    out = lax.all_to_all(
-        slots.reshape(experts, rows // experts, width), "dp", split_axis=0, concat_axis=0, tiled=True
-    )
+    out = lax.all_to_all(slots.reshape(experts, rows // experts, width), "dp", split_axis=0, concat_axis=0, tiled=True)
     return out.reshape(rows, width)
 
 
@@ -568,11 +609,12 @@
     full_late = gather_rows(
         jnp.concatenate([blocks[:, 1], blocks[:, 2], out_weight.astype(BF16), late], axis=1), devices
     )
-    weights = (full_early[:, : 3 * wide], full_late[:, : 3 * wide], full_late[:, 3 * wide : 6 * wide])
-    proj_out = full_late[:, 6 * wide : 6 * wide + width]
-    router = full_late[:, 6 * wide + width :]
+    weights = (full_early, full_late, full_late)
+    places = (0, 0, 1)
+    out_place = 2
+    router_at, router_wide = 6 * wide + width, late.shape[1]
     early_rows = full_early[:, 3 * wide : 3 * wide + 8].astype(F32).T
-    late_rows = router.astype(F32).T
+    late_rows = full_late[:, router_at:].astype(F32).T
     vecs = jnp.pad(late_rows[experts : experts + 3], ((0, 5), (0, 0)))
     router_row = lax.dynamic_index_in_dim(late_rows, lax.axis_index("dp"), 0, keepdims=True)
 
@@ -588,7 +630,7 @@
     target = (slot // per_chunk) * chunk_rows + route * per_chunk + slot % per_chunk
     target_row, target_col = target[None, :], target[:, None]
 
-    dys = [exchange(pack(dy, target_row, c * chunk_rows, chunk_rows), experts) for c in range(CHUNKS)]
+    dys = [exchange(pack(dy, target_row, c, chunk_rows), experts) for c in range(CHUNKS)]
     w_in = expert_in[0].astype(BF16)
     w_out = expert_out[0].astype(BF16)
 
@@ -598,22 +640,16 @@
     normed = (scaled * early_rows[0:1] + early_rows[1:2]).astype(BF16)
     qkvs, mixes, lses = [], [], []
     for g in range(GROUPS):
-        cols = slice(g * wide, (g + 1) * wide)
-        bias = jnp.concatenate(
-            [early_rows[2:3, cols], jnp.zeros((1, wide), F32), early_rows[3:4, cols]], axis=1
-        )
-        qkv, mix, lse = attend(normed, weights[g], bias, seg_col, seg_row)
+        qkv, mix, lse = attend(g, normed, weights[g], places[g], early_rows, seg_col, seg_row)
         qkvs.append(qkv)
         mixes.append(mix)
         lses.append(lse)
-    hidden, moe_in = project(x, mixes, proj_out, vecs)
+    hidden, moe_in = project(x, mixes, full_late, out_place, vecs)
 
     expert_vecs = jnp.concatenate([expert_out_bias, router_row, jnp.zeros((6, width), F32)], axis=0)
     returned, dmoes, kept = [], [], ()
     dbias_in = dsums = 0.0
-    received = [
-        exchange(pack(moe_in, target_row, c * chunk_rows, chunk_rows), experts) for c in range(CHUNKS)
-    ]
+    received = [exchange(pack(moe_in, target_row, c, chunk_rows), experts) for c in range(CHUNKS)]
     for c in range(CHUNKS):
         ret, dmoe, *kept, dbias, sums = expert_chunk(
             c, CHUNKS * chunk_rows, received[c], dys[c], w_in, expert_in_bias, w_out, expert_vecs, kept
@@ -628,23 +664,18 @@
     returned = [exchange(r, experts) for r in returned]
 
     dhid, dattn, mid_sums = middle(dmoes, target_col, hidden, dy, vecs)
-    grad_out = scatter_rows(dot_tn(jnp.concatenate(mixes, axis=1), dattn), devices)
-    dqkvs, qkv_sums, grad_qkv = [], [], []
-    for g in range(GROUPS):
-        dqkv, col_sums = attend_back(
-            qkvs[g],
-            mixes[g],
-            dattn,
-            proj_out[g * wide : (g + 1) * wide],
-            lses[g],
-            seg_col,
-            seg_row,
-        )
-        dqkvs.append(dqkv)
-        qkv_sums.append(col_sums[0:1])
-        grad_qkv.append(scatter_rows(dot_tn(normed, dqkv), devices))
-    grad_inputs, last_sums = last(dqkvs, weights, x, dhid, early_rows)
-    output = finish_output(returned, target_col, route.reshape(tokens, 1), hidden, moe_in, router)
+    part_out = dot_tn(jnp.concatenate(mixes, axis=1), dattn)
+    dqkvs, qkv_sums, parts = [None] * GROUPS, [None] * GROUPS, [None] * GROUPS
+    for g in reversed(range(GROUPS)):
+        dqkvs[g], col_sums = attend_back(g, qkvs[g], mixes[g], dattn, full_late, out_place, lses[g], seg_col, seg_row)
+        qkv_sums[g] = col_sums[0:1]
+        parts[g] = dot_tn(normed, dqkvs[g])
+    grad_out, *upper = scatter_rows([part_out], parts[1:], devices)
+    grad_qkv = scatter_rows(parts[:1], [], devices) + upper
+    grad_inputs, last_sums = last(dqkvs, weights, places, x, dhid, early_rows)
+    output = finish_output(
+        returned, target_col, route.reshape(tokens, 1), hidden, moe_in, full_late, router_at, router_wide
+    )
 
     grad_query = jnp.concatenate([s[:, :wide] for s in qkv_sums], axis=1)
     grad_value = jnp.concatenate([s[:, 2 * wide :] for s in qkv_sums], axis=1)

time: 595 us -> 565 us (0.950)
  starting transfers between devices: 129 us -> 76.9 us
  waiting for transfers between devices: 112 us -> 140 us
  local copies, waits for them, and re-layouts: 37.1 us -> 28.4 us
  other arithmetic: 36.4 us -> 42.5 us
    ppermute x66 -> x30, starting transfers between devices: 91.8 us -> 39.5 us  [the longest x16 20.4 us: shifted(): parts.append(lax.ppermute(block, 'dp', cyclic(devices, sizes, axis, shift)))]
    ppermute x66 -> x30, waiting for transfers between devices: 48.3 us -> 78.5 us  [the longest x16 57 us: shifted(): parts.append(lax.ppermute(block, 'dp', cyclic(devices, sizes, axis, shift)))]
    unnamed x86 -> x94, local copies, waits for them, and re-layouts: 3.48 us -> 10.2 us
    slice x9 -> x1, local copies, waits for them, and re-layouts: 7.67 us -> 1.32 us  [scatter_level(): totals[n] = total + got[..., base:base + width].astype(F32)]
  transfers between devices with their start and end apart: 74 -> 38, of which waited for: 25 -> 13; matrix products, arithmetic and copies ran while one was open for 19% -> 17% of each run, Pallas kernels for 26% -> 27%
where the time goes in v2:
time: 565 us; the launch traced here: 559 us
  Pallas kernels  185 us (33%)
  waiting for transfers between devices  140 us (25%)
  starting transfers between devices  76.9 us (14%)
  blocking collectives  44 us (8%)
  other arithmetic  42.5 us (8%)
  matrix products  39.4 us (7%)
  local copies, waits for them, and re-layouts  28.4 us (5%)
    pallas_call x2, Pallas kernels, expert_chunk(): pl.pallas_call(functools.partial(expert_kernel, aliased), grid=(hidden //...  62.4 us
    all_to_all x7, waiting for transfers between devices, exchange(): lax.all_to_all(slots.reshape(experts, rows // experts, width), 'dp', spli...  61.9 us
    ppermute x16, waiting for transfers between devices, shifted(): parts.append(lax.ppermute(block, 'dp', cyclic(devices, sizes, axis, shift)))  57 us
    all_to_all x1, blocking collectives, exchange(): lax.all_to_all(slots.reshape(experts, rows // experts, width), 'dp', spli...  44 us
    pallas_call x3, Pallas kernels, attend_back(): pl.pallas_call(attend_back_kernel, grid=(1,), in_specs=[whole(qkv.shape),...  38.9 us
    dot_general x6, matrix products, dot_tn(): lax.dot_general(a, b, (((0,), (0,)), ((), ())), preferred_element_type=F32)  38.8 us
    pallas_call x3, Pallas kernels, attend(): pl.pallas_call(attend_kernel, grid=(1,), in_specs=[whole(normed.shape), p...  31.8 us
    all_to_all x7, starting transfers between devices, exchange(): lax.all_to_all(slots.reshape(experts, rows // experts, width), 'dp', spli...  31.6 us
  transfers between devices with their start and end apart: 38, of which 13 were waited for; matrix products, arithmetic and copies ran while one was open for 17% of the time, Pallas kernels for 27%

profile of v2, /device:TPU:0, one launch (start us, length us, event | category | flops | bytes accessed | tf_op | source)
XLA Modules:
  0.0 558.5 jit_solution(11924658509492478861)
XLA Ops:
  21.1 5.1 all-to-all-start.1
  32.2 36.6 %collective-permute-done.9 = bf16[24,2432]{1,0:T(8,128)(2,1)S(1)} collective-permute-done((bf16[24,2432]{1,0:T(8,128)(2,1)S(1)}, bf16[24,2432]{1,0:T(8,128)(2,1)S(1)}, u32[]{:S(2)}, u32[]{:S(2)}) %collective-permute-start.9) | collective-permute-done | bytes 116768 | tf_op jit(solution)/shard_map/ppermute | solution.py:494
  73.4 7.3 %collective-permute-done.4 = bf16[4,2,24,384]{3,2,0,1:T(8,128)(2,1)S(1)} collective-permute-done((bf16[4,2,24,384]{3,2,0,1:T(8,128)(2,1)S(1)}, bf16[4,2,24,384]{3,2,0,1:T(8,128)(2,1)S(1)}, u32[]{:S(2)}, u32[]{:S(2)}) %collective-permute-start.4) | collective-permute-done | bytes 147488 | tf_op jit(solution)/shard_map/ppermute | solution.py:494
  84.1 7.3 %collective-permute-done.12 = bf16[4,2,24,1152]{3,2,0,1:T(8,128)(2,1)S(1)} collective-permute-done((bf16[4,2,24,1152]{3,2,0,1:T(8,128)(2,1)S(1)}, bf16[4,2,24,1152]{3,2,0,1:T(8,128)(2,1)S(1)}, u32[]{:S(2)}, u32[]{:S(2)}) %collective-permute-start.12) | collective-permute-done | bytes 442400 | tf_op jit(solution)/shard_map/ppermute | solution.py:494
  91.6 5.7 %collective-permute-done.14 = bf16[4,2,24,1280]{3,2,0,1:T(8,128)(2,1)S(1)} collective-permute-done((bf16[4,2,24,1280]{3,2,0,1:T(8,128)(2,1)S(1)}, bf16[4,2,24,1280]{3,2,0,1:T(8,128)(2,1)S(1)}, u32[]{:S(2)}, u32[]{:S(2)}) %collective-permute-start.14) | collective-permute-done | bytes 491552 | tf_op jit(solution)/shard_map/ppermute | solution.py:494
  100.2 4.3 pack.7
  113.8 10.6 %attend.3 = (bf16[1024,768]{1,0:T(8,128)(2,1)}, bf16[1024,256]{1,0:T(8,128)(2,1)}, f32[8,1024]{1,0:T(8,128)}) custom-call(bf16[1024,768]{1,0:T(8,128)(2,1)} %fusion.6.x_ref, bf16[768,896]{1,0:T(8,128)(2,1)} %bitcast.286, f32[8,768]{1,0:T(8,128)} %copy-done.35, s32[1024,1]{1,0:T(8,128)} %copy.173.sc_ref, s32[1,1024]{1,0:T(1,128)} %sr_ref.11), custom_call_target="tpu_custom_call" | custom-call | tf_op jit(solution)/shard_map/attend/pallas_call | solution.py:111
  129.1 10.5 %attend.5 = (bf16[1024,768]{1,0:T(8,128)(2,1)}, bf16[1024,256]{1,0:T(8,128)(2,1)}, f32[8,1024]{1,0:T(8,128)}) custom-call(bf16[1024,768]{1,0:T(8,128)(2,1)} %fusion.6.x_ref, bf16[768,2432]{1,0:T(8,128)(2,1)} %bitcast.270, f32[8,768]{1,0:T(8,128)} %copy-done.35, s32[1024,1]{1,0:T(8,128)} %copy.173.sc_ref, s32[1,1024]{1,0:T(1,128)} %sr_ref.11), custom_call_target="tpu_custom_call" | custom-call | tf_op jit(solution)/shard_map/attend/pallas_call | solution.py:111
  139.6 10.7 %attend.4 = (bf16[1024,768]{1,0:T(8,128)(2,1)}, bf16[1024,256]{1,0:T(8,128)(2,1)}, f32[8,1024]{1,0:T(8,128)}) custom-call(bf16[1024,768]{1,0:T(8,128)(2,1)} %fusion.6.x_ref, bf16[768,2432]{1,0:T(8,128)(2,1)} %bitcast.271, f32[8,768]{1,0:T(8,128)} %copy-done.35, s32[1024,1]{1,0:T(8,128)} %copy.173.sc_ref, s32[1,1024]{1,0:T(1,128)} %sr_ref.11), custom_call_target="tpu_custom_call" | custom-call | tf_op jit(solution)/shard_map/attend/pallas_call | solution.py:111
  152.2 5.9 %project.1 = (f32[1024,768]{1,0:T(8,128)}, bf16[1024,768]{1,0:T(8,128)(2,1)}) custom-call(bf16[1024,768]{1,0:T(8,128)(2,1)} %bitcast.280, bf16[1024,256]{1,0:T(8,128)(2,1)} %get-tuple-element.54.m0_ref.mix_ref, bf16[1024,256]{1,0:T(8,128)(2,1)} %get-tuple-element.55.m1_ref.mix_ref, bf16[1024,256]{1,0:T(8,128)(2,1)} %get-tuple-element.56.m2_ref.mix_ref, ...), custom_call_target="tpu_custom_call" | custom-call | tf_op jit(solution)/shard_map/project/pallas_call | solution.py:231
  162.5 5.9 %all-to-all-start = ((bf16[32,32,768]{2,1,0:T(8,128)(2,1)}), bf16[32,32,768]{2,1,0:T(8,128)(2,1)S(1)}, u32[]{:S(2)}, u32[]{:S(2)}) async-start(bf16[32,32,768]{2,1,0:T(8,128)(2,1)} %bitcast.296), calls=%async_computation | async-start | bytes 3145728 | tf_op jit(solution)/shard_map/all_to_all | solution.py:565
  168.4 4.3 pack.6
  172.8 33.3 %all-to-all-done = bf16[32,32,768]{2,1,0:T(8,128)(2,1)S(1)} async-done(((bf16[32,32,768]{2,1,0:T(8,128)(2,1)}), bf16[32,32,768]{2,1,0:T(8,128)(2,1)S(1)}, u32[]{:S(2)}, u32[]{:S(2)}) %all-to-all-start) | async-done | bytes 1572896 | tf_op jit(solution)/shard_map/all_to_all | solution.py:565
  210.0 6.3 %convert_bitcast_fusion.refs_4_ = bf16[3072,768]{1,0:T(8,128)(2,1)} fusion(f32[1,3072,768]{2,1,0:T(8,128)} %param.34), kind=kLoop, calls=%fused_computation.2 | loop fusion | flops 2359296 | bytes 14155776 | tf_op jit(solution)/shard_map/convert_element_type | solution.py:635
  216.3 6.6 %convert_bitcast_fusion.1.refs_2_ = bf16[768,3072]{1,0:T(8,128)(2,1)} fusion(f32[1,768,3072]{2,1,0:T(8,128)} %param.32), kind=kLoop, calls=%fused_computation.3 | loop fusion | flops 2359296 | bytes 14155776 | tf_op jit(solution)/shard_map/convert_element_type | solution.py:634
  223.9 31.0 %expert.2 = (bf16[1024,768]{1,0:T(8,128)(2,1)}, bf16[1024,768]{1,0:T(8,128)(2,1)}, bf16[2048,3072]{1,0:T(8,128)(2,1)}, bf16[2048,3072]{1,0:T(8,128)(2,1)}, bf16[...) custom-call(bf16[1024,768]{1,0:T(8,128)(2,1)} %bitcast.298, ...), custom_call_target="tpu_custom_call" | custom-call | tf_op jit(solution)/shard_map/expert/pallas_call | solution.py:429
  256.1 31.4 %expert.3 = (bf16[1024,768]{1,0:T(8,128)(2,1)}, bf16[1024,768]{1,0:T(8,128)(2,1)}, bf16[2048,3072]{1,0:T(8,128)(2,1)}, bf16[2048,3072]{1,0:T(8,128)(2,1)}, bf16[...) custom-call(bf16[1024,768]{1,0:T(8,128)(2,1)} %bitcast.288, ...), custom_call_target="tpu_custom_call", output_to_operand_aliasing={{2}: (6, {}), {3}: (7, {}), {4}: (8, {}), {5}: (9, {})} | custom-call | tf_op jit(solution)/shard_map/expert/pallas_call | solution.py:429
  287.5 44.0 %all_to_all.52 = bf16[32,32,768]{2,1,0:T(8,128)(2,1)} all-to-all(bf16[32,32,768]{2,1,0:T(8,128)(2,1)} %bitcast.305), channel_id=1, replica_groups=mesh['dp'=32] {'dp'}, dimensions={0} | all-to-all | bytes 3145728 | tf_op jit(solution)/shard_map/all_to_all | solution.py:565
  343.6 28.6 %all-to-all-done.6 = bf16[32,32,768]{2,1,0:T(8,128)(2,1)S(1)} async-done(((bf16[32,32,768]{2,1,0:T(8,128)(2,1)}), bf16[32,32,768]{2,1,0:T(8,128)(2,1)S(1)}, u32[]{:S(2)}, u32[]{:S(2)}) %all-to-all-start.6) | async-done | bytes 1572896 | tf_op jit(solution)/shard_map/all_to_all | solution.py:565
  376.2 16.3 %convolution_bitcast_fusion = f32[1,3072,768]{2,1,0:T(8,128)} fusion(bf16[2048,3072]{1,0:T(8,128)(2,1)} %get-tuple-element.90, bf16[2048,768]{1,0:T(8,128)(2,1)} %get-tuple-element.91), kind=kOutput, calls=%fused_computation | convolution fusion | flops 9663676416 | bytes 25165824 | tf_op jit(solution)/shard_map/dot_general | solution.py:35
  393.1 15.3 %convolution_bitcast_fusion.1 = f32[1,768,3072]{2,1,0:T(8,128)} fusion(bf16[2048,768]{1,0:T(8,128)(2,1)S(1)} %copy-done.18, bf16[2048,3072]{1,0:T(8,128)(2,1)} %get-tuple-element.87), kind=kOutput, calls=%fused_computation.1 | convolution fusion | flops 9663676416 | bytes 25165824 | tf_op jit(solution)/shard_map/dot_general | solution.py:35
  408.4 10.0 %middle.1 = (f32[1024,768]{1,0:T(8,128)}, bf16[1024,768]{1,0:T(8,128)(2,1)}, f32[8,768]{1,0:T(8,128)}) custom-call(bf16[1024,768]{1,0:T(8,128)(2,1)} %bitcast.294, bf16[1024,768]{1,0:T(8,128)(2,1)} %bitcast.293, s32[1024,1]{1,0:T(8,128)} %fusion.27.refs_2_, f32[1024,768]{1,0:T(8,128)} %get-tuple-element.64.refs_4_.refs_3_, bf16[1024,768]{1,0:T(8,128)(2,1)} %bitcast.284, ...), custom_call_target="tpu_custom_call" | custom-call | tf_op jit(solution)/shard_map/middle/pallas_call | solution.py:300
  418.4 12.9 %attend_back.5 = (bf16[1024,768]{1,0:T(8,128)(2,1)}, f32[8,768]{1,0:T(8,128)}) custom-call(bf16[1024,768]{1,0:T(8,128)(2,1)} %get-tuple-element.74.qkv_ref, bf16[1024,256]{1,0:T(8,128)(2,1)} %get-tuple-element.56.m2_ref.mix_ref, bf16[1024,768]{1,0:T(8,128)(2,1)} %get-tuple-element.68.da_ref, bf16[768,2432]{1,0:T(8,128)(2,1)} %bitcast.274, ...), custom_call_target="tpu_custom_call" | custom-call | tf_op jit(solution)/shard_map/attend_back/pallas_call | solution.py:190
  431.2 13.1 %attend_back.4 = (bf16[1024,768]{1,0:T(8,128)(2,1)}, f32[8,768]{1,0:T(8,128)}) custom-call(bf16[1024,768]{1,0:T(8,128)(2,1)} %get-tuple-element.71.qkv_ref, bf16[1024,256]{1,0:T(8,128)(2,1)} %get-tuple-element.55.m1_ref.mix_ref, bf16[1024,768]{1,0:T(8,128)(2,1)} %get-tuple-element.68.da_ref, bf16[768,2432]{1,0:T(8,128)(2,1)} %bitcast.275, ...), custom_call_target="tpu_custom_call" | custom-call | tf_op jit(solution)/shard_map/attend_back/pallas_call | solution.py:190
  445.1 5.9 %all-to-all-start.2 = ((bf16[32,32,768]{2,1,0:T(8,128)(2,1)}), bf16[32,32,768]{2,1,0:T(8,128)(2,1)S(1)}, u32[]{:S(2)}, u32[]{:S(2)}) async-start(bf16[32,32,768]{2,1,0:T(8,128)(2,1)} %bitcast.300), calls=%async_computation.2 | async-start | bytes 3145728 | tf_op jit(solution)/shard_map/all_to_all | solution.py:565
  451.8 12.9 %attend_back.3 = (bf16[1024,768]{1,0:T(8,128)(2,1)}, f32[8,768]{1,0:T(8,128)}) custom-call(bf16[1024,768]{1,0:T(8,128)(2,1)} %get-tuple-element.65.qkv_ref, bf16[1024,256]{1,0:T(8,128)(2,1)} %get-tuple-element.54.m0_ref.mix_ref, bf16[1024,768]{1,0:T(8,128)(2,1)} %get-tuple-element.68.da_ref, bf16[768,2432]{1,0:T(8,128)(2,1)} %bitcast.276, ...), custom_call_target="tpu_custom_call" | custom-call | tf_op jit(solution)/shard_map/attend_back/pallas_call | solution.py:190
  464.7 10.4 %last.1 = (f32[1024,768]{1,0:T(8,128)}, f32[8,768]{1,0:T(8,128)}) custom-call(bf16[1024,768]{1,0:T(8,128)(2,1)} %get-tuple-element.70.d0_ref, bf16[1024,768]{1,0:T(8,128)(2,1)} %get-tuple-element.73.d1_ref, bf16[1024,768]{1,0:T(8,128)(2,1)} %get-tuple-element.76.d2_ref, bf16[768,896]{1,0:T(8,128)(2,1)} %bitcast.287, bf16[768,2432]{1,0:T(8,128)(2,1)} %bitcast.277, ...), custom_call_target="tpu_custom_call" | custom-call | tf_op jit(solution)/shard_map/last/pallas_call | solution.py:360
  491.7 5.8 %all-to-all-start.8 = ((f32[32,1,256]{2,1,0:T(1,128)}), f32[32,1,256]{2,1,0:T(1,128)S(1)}, u32[]{:S(2)}, u32[]{:S(2)}) async-start(f32[32,1,256]{2,1,0:T(1,128)} %copy.202), calls=%async_computation.8 | async-start | bytes 65536 | tf_op jit(solution)/shard_map/all_to_all | solution.py:687
  499.1 8.2 %finish_output.1 = bf16[1024,768]{1,0:T(8,128)(2,1)} custom-call(bf16[1024,768]{1,0:T(8,128)(2,1)} %bitcast.292, bf16[1024,768]{1,0:T(8,128)(2,1)} %bitcast.290, s32[1024,1]{1,0:T(8,128)} %fusion.27.refs_2_, s32[1024,1]{1,0:T(8,128)} %copy.187.refs_3_, f32[1024,768]{1,0:T(8,128)} %get-tuple-element.64.refs_4_.refs_3_, ...), custom_call_target="tpu_custom_call" | custom-call | tf_op jit(solution)/shard_map/finish_output/pallas_call | solution.py:329
  512.0 6.8 %collective-permute-done.17 = bf16[4,2,24,768]{3,2,1,0:T(8,128)(2,1)S(1)} collective-permute-done((bf16[4,2,24,768]{3,2,1,0:T(8,128)(2,1)S(1)}, bf16[4,2,24,768]{3,2,1,0:T(8,128)(2,1)S(1)}, u32[]{:S(2)}, u32[]{:S(2)}) %collective-permute-start.17) | collective-permute-done | bytes 294944 | tf_op jit(solution)/shard_map/ppermute | solution.py:539
  535.1 4.5 collective-permute-done.23
  541.4 5.2 collective-permute-done.24
  (296 shorter events, 133.6 us)
Async XLA Ops:
  5.9 26.3 %collective-permute-start.10 = (bf16[24,2432]{1,0:T(8,128)(2,1)S(1)}, bf16[24,2432]{1,0:T(8,128)(2,1)S(1)}, u32[]{:S(2)}, u32[]{:S(2)}) collective-permute-start(bf16[24,2432]{1,0:T(8,128)(2,1)S(1)} %pad_maximum_fusion.14), channel_id=1, source_target_pairs={{0,8},{1,9},{2,10},{3,11},{4,12},{5,13},{6,14},{7,15},{8,16},{9,17... | collective-permute-start | bytes 350216 | tf_op jit(solution)/shard_map/ppermute | solution.py:494
  9.0 23.2 %collective-permute-start.8 = (bf16[24,2432]{1,0:T(8,128)(2,1)S(1)}, bf16[24,2432]{1,0:T(8,128)(2,1)S(1)}, u32[]{:S(2)}, u32[]{:S(2)}) collective-permute-start(bf16[24,2432]{1,0:T(8,128)(2,1)S(1)} %pad_maximum_fusion.14), channel_id=1, source_target_pairs={{0,24},{1,25},{2,26},{3,27},{4,28},{5,29},{6,30},{7,31},{8,0},{9,1... | collective-permute-start | bytes 350216 | tf_op jit(solution)/shard_map/ppermute | solution.py:494
  12.5 13.7 %collective-permute-start = (bf16[24,896]{1,0:T(8,128)(2,1)S(1)}, bf16[24,896]{1,0:T(8,128)(2,1)S(1)}, u32[]{:S(2)}, u32[]{:S(2)}) collective-permute-start(bf16[24,896]{1,0:T(8,128)(2,1)S(1)} %fusion.51), channel_id=1, source_target_pairs={{0,24},{1,25},{2,26},{3,27},{4,28},{5,29},{6,30},{7,31},{8,0},{9,1... | collective-permute-start | bytes 129032 | tf_op jit(solution)/shard_map/ppermute | solution.py:494
  14.6 14.4 %collective-permute-start.1 = (bf16[24,896]{1,0:T(8,128)(2,1)S(1)}, bf16[24,896]{1,0:T(8,128)(2,1)S(1)}, u32[]{:S(2)}, u32[]{:S(2)}) collective-permute-start(bf16[24,896]{1,0:T(8,128)(2,1)S(1)} %fusion.51), channel_id=1, source_target_pairs={{0,16},{1,17},{2,18},{3,19},{4,20},{5,21},{6,22},{7,23},{8,24},{9,... | collective-permute-start | bytes 129032 | tf_op jit(solution)/shard_map/ppermute | solution.py:494
  14.6 14.4 %collective-permute-start.2 = (bf16[24,896]{1,0:T(8,128)(2,1)S(1)}, bf16[24,896]{1,0:T(8,128)(2,1)S(1)}, u32[]{:S(2)}, u32[]{:S(2)}) collective-permute-start(bf16[24,896]{1,0:T(8,128)(2,1)S(1)} %fusion.51), channel_id=1, source_target_pairs={{0,8},{1,9},{2,10},{3,11},{4,12},{5,13},{6,14},{7,15},{8,16},{9,17... | collective-permute-start | bytes 129032 | tf_op jit(solution)/shard_map/ppermute | solution.py:494
  21.1 84.5 %all-to-all-start.1 = ((bf16[32,32,768]{2,1,0:T(8,128)(2,1)}), bf16[32,32,768]{2,1,0:T(8,128)(2,1)S(1)}, u32[]{:S(2)}, u32[]{:S(2)}) async-start(bf16[32,32,768]{2,1,0:T(8,128)(2,1)} %bitcast.289), calls=%async_computation.1 | async-start | bytes 3145728 | tf_op jit(solution)/shard_map/all_to_all | solution.py:565
  26.2 42.5 %collective-permute-start.9 = (bf16[24,2432]{1,0:T(8,128)(2,1)S(1)}, bf16[24,2432]{1,0:T(8,128)(2,1)S(1)}, u32[]{:S(2)}, u32[]{:S(2)}) collective-permute-start(bf16[24,2432]{1,0:T(8,128)(2,1)S(1)} %pad_maximum_fusion.14), channel_id=1, source_target_pairs={{0,16},{1,17},{2,18},{3,19},{4,20},{5,21},{6,22},{7,23},{8,24},{9,... | collective-permute-start | bytes 350216 | tf_op jit(solution)/shard_map/ppermute | solution.py:494
  29.1 42.9 %collective-permute-start.3 = (bf16[4,24,384]{2,1,0:T(8,128)(2,1)S(1)}, bf16[4,24,384]{2,1,0:T(8,128)(2,1)S(1)}, u32[]{:S(2)}, u32[]{:S(2)}) collective-permute-start(bf16[4,24,384]{2,1,0:T(8,128)(2,1)S(1)} %pad_maximum_fusion.21), channel_id=1, source_target_pairs={{0,4},{1,5},{2,6},{3,7},{4,0},{5,1},{6,2},{7,3},{8,12},{9,13},{10,... | collective-permute-start | bytes 221192 | tf_op jit(solution)/shard_map/ppermute | solution.py:494
  30.6 41.9 %collective-permute-start.5 = (bf16[4,24,512]{2,1,0:T(8,128)(2,1)S(1)}, bf16[4,24,512]{2,1,0:T(8,128)(2,1)S(1)}, u32[]{:S(2)}, u32[]{:S(2)}) collective-permute-start(bf16[4,24,512]{2,1,0:T(8,128)(2,1)S(1)} %pad_maximum_fusion.18), channel_id=1, source_target_pairs={{0,2},{1,3},{2,0},{3,1},{4,6},{5,7},{6,4},{7,5},{8,10},{9,11},{10,... | collective-permute-start | bytes 294920 | tf_op jit(solution)/shard_map/ppermute | solution.py:494
  69.0 11.8 %collective-permute-start.11 = (bf16[4,24,1152]{2,1,0:T(8,128)(2,1)S(1)}, bf16[4,24,1152]{2,1,0:T(8,128)(2,1)S(1)}, u32[]{:S(2)}, u32[]{:S(2)}) collective-permute-start(bf16[4,24,1152]{2,1,0:T(8,128)(2,1)S(1)} %pad_maximum_fusion.11), channel_id=1, source_target_pairs={{0,4},{1,5},{2,6},{3,7},{4,0},{5,1},{6,2},{7,3},{8,12},{9,13},{10,... | collective-permute-start | bytes 663560 | tf_op jit(solution)/shard_map/ppermute | solution.py:494
  70.4 13.1 %collective-permute-start.13 = (bf16[4,24,1280]{2,1,0:T(8,128)(2,1)S(1)}, bf16[4,24,1280]{2,1,0:T(8,128)(2,1)S(1)}, u32[]{:S(2)}, u32[]{:S(2)}) collective-permute-start(bf16[4,24,1280]{2,1,0:T(8,128)(2,1)S(1)} %pad_maximum_fusion.8), channel_id=1, source_target_pairs={{0,2},{1,3},{2,0},{3,1},{4,6},{5,7},{6,4},{7,5},{8,10},{9,11},{10,... | collective-permute-start | bytes 737288 | tf_op jit(solution)/shard_map/ppermute | solution.py:494
  72.0 8.7 %collective-permute-start.4 = (bf16[4,2,24,384]{3,2,0,1:T(8,128)(2,1)S(1)}, bf16[4,2,24,384]{3,2,0,1:T(8,128)(2,1)S(1)}, u32[]{:S(2)}, u32[]{:S(2)}) collective-permute-start(bf16[4,2,24,384]{3,2,0,1:T(8,128)(2,1)S(1)} %pad_maximum_fusion.13), channel_id=1, source_target_pairs={{0,2},{1,3},{2,0},{3,1},{4,6},{5,7},{6,4},{7,5},{8,10},{9,11},{10,... | collective-permute-start | bytes 442376 | tf_op jit(solution)/shard_map/ppermute | solution.py:494
  72.7 9.9 %collective-permute-start.6 = (bf16[4,2,24,512]{3,2,0,1:T(8,128)(2,1)S(1)}, bf16[4,2,24,512]{3,2,0,1:T(8,128)(2,1)S(1)}, u32[]{:S(2)}, u32[]{:S(2)}) collective-permute-start(bf16[4,2,24,512]{3,2,0,1:T(8,128)(2,1)S(1)} %pad_maximum_fusion.12), channel_id=1, source_target_pairs={{0,4},{1,5},{2,6},{3,7},{4,0},{5,1},{6,2},{7,3},{8,12},{9,13},{10,... | collective-permute-start | bytes 589832 | tf_op jit(solution)/shard_map/ppermute | solution.py:494
  80.9 10.5 %collective-permute-start.12 = (bf16[4,2,24,1152]{3,2,0,1:T(8,128)(2,1)S(1)}, bf16[4,2,24,1152]{3,2,0,1:T(8,128)(2,1)S(1)}, u32[]{:S(2)}, u32[]{:S(2)}) collective-permute-start(bf16[4,2,24,1152]{3,2,0,1:T(8,128)(2,1)S(1)} %pad_maximum_fusion.5), channel_id=1, source_target_pairs={{0,2},{1,3},{2,0},{3,1},{4,6},{5,7},{6,4},{7,5},{8,10},{9,11},{10,... | collective-permute-start | bytes 1327112 | tf_op jit(solution)/shard_map/ppermute | solution.py:494
  83.5 26.6 %collective-permute-start.7 = (bf16[4,2,2,24,896]{4,3,0,2,1:T(8,128)(2,1)}, bf16[4,2,2,24,896]{4,3,0,2,1:T(8,128)(2,1)}, u32[]{:S(2)}, u32[]{:S(2)}) collective-permute-start(bf16[4,2,2,24,896]{4,3,0,2,1:T(8,128)(2,1)} %maximum_maximum_fusion.1), channel_id=1, source_target_pairs={{0,1},{1,0},{2,3},{3,2},{4,5},{5,4},{6,7},{7,6},{8,9},{9,8},{10,11... | collective-permute-start | bytes 2064392 | tf_op jit(solution)/shard_map/ppermute | solution.py:494
  83.7 13.7 %collective-permute-start.14 = (bf16[4,2,24,1280]{3,2,0,1:T(8,128)(2,1)S(1)}, bf16[4,2,24,1280]{3,2,0,1:T(8,128)(2,1)S(1)}, u32[]{:S(2)}, u32[]{:S(2)}) collective-permute-start(bf16[4,2,24,1280]{3,2,0,1:T(8,128)(2,1)S(1)} %pad_maximum_fusion.4), channel_id=1, source_target_pairs={{0,4},{1,5},{2,6},{3,7},{4,0},{5,1},{6,2},{7,3},{8,12},{9,13},{10,... | collective-permute-start | bytes 1474568 | tf_op jit(solution)/shard_map/ppermute | solution.py:494
  99.0 25.4 %collective-permute-start.15 = (bf16[4,2,2,24,2432]{4,3,0,2,1:T(8,128)(2,1)}, bf16[4,2,2,24,2432]{4,3,0,2,1:T(8,128)(2,1)}, u32[]{:S(2)}, u32[]{:S(2)}) collective-permute-start(bf16[4,2,2,24,2432]{4,3,0,2,1:T(8,128)(2,1)} %maximum_maximum_fusion), channel_id=1, source_target_pairs={{0,1},{1,0},{2,3},{3,2},{4,5},{5,4},{6,7},{7,6},{8,9},{9,8},{10,11... | collective-permute-start | bytes 5603336 | tf_op jit(solution)/shard_map/ppermute | solution.py:494
  105.6 56.9 %all-to-all-start.4 = ((bf16[32,32,768]{2,1,0:T(8,128)(2,1)}), bf16[32,32,768]{2,1,0:T(8,128)(2,1)}, u32[]{:S(2)}, u32[]{:S(2)}) async-start(bf16[32,32,768]{2,1,0:T(8,128)(2,1)} %bitcast.291), calls=%async_computation.4 | async-start | bytes 3145728 | tf_op jit(solution)/shard_map/all_to_all | solution.py:565
  162.5 43.6 %all-to-all-start = ((bf16[32,32,768]{2,1,0:T(8,128)(2,1)}), bf16[32,32,768]{2,1,0:T(8,128)(2,1)S(1)}, u32[]{:S(2)}, u32[]{:S(2)}) async-start(bf16[32,32,768]{2,1,0:T(8,128)(2,1)} %bitcast.296), calls=%async_computation | async-start | bytes 3145728 | tf_op jit(solution)/shard_map/all_to_all | solution.py:565
  206.1 48.8 %all-to-all-start.3 = ((bf16[32,32,768]{2,1,0:T(8,128)(2,1)}), bf16[32,32,768]{2,1,0:T(8,128)(2,1)S(1)}, u32[]{:S(2)}, u32[]{:S(2)}) async-start(bf16[32,32,768]{2,1,0:T(8,128)(2,1)} %bitcast.295), calls=%async_computation.3 | async-start | bytes 3145728 | tf_op jit(solution)/shard_map/all_to_all | solution.py:565
  331.5 40.6 %all-to-all-start.6 = ((bf16[32,32,768]{2,1,0:T(8,128)(2,1)}), bf16[32,32,768]{2,1,0:T(8,128)(2,1)S(1)}, u32[]{:S(2)}, u32[]{:S(2)}) async-start(bf16[32,32,768]{2,1,0:T(8,128)(2,1)} %bitcast.68), calls=%async_computation.6 | async-start | bytes 3145728 | tf_op jit(solution)/shard_map/all_to_all | solution.py:565
  372.1 72.9 %all-to-all-start.5 = ((bf16[32,32,768]{2,1,0:T(8,128)(2,1)}), bf16[32,32,768]{2,1,0:T(8,128)(2,1)S(1)}, u32[]{:S(2)}, u32[]{:S(2)}) async-start(bf16[32,32,768]{2,1,0:T(8,128)(2,1)} %bitcast.301), calls=%async_computation.5 | async-start | bytes 3145728 | tf_op jit(solution)/shard_map/all_to_all | solution.py:565
  445.1 46.7 %all-to-all-start.2 = ((bf16[32,32,768]{2,1,0:T(8,128)(2,1)}), bf16[32,32,768]{2,1,0:T(8,128)(2,1)S(1)}, u32[]{:S(2)}, u32[]{:S(2)}) async-start(bf16[32,32,768]{2,1,0:T(8,128)(2,1)} %bitcast.300), calls=%async_computation.2 | async-start | bytes 3145728 | tf_op jit(solution)/shard_map/all_to_all | solution.py:565
  481.9 26.2 %collective-permute-start.16 = (bf16[4,2,2,24,768]{4,3,2,1,0:T(8,128)(2,1)S(1)}, bf16[4,2,2,24,768]{4,3,2,1,0:T(8,128)(2,1)S(1)}, u32[]{:S(2)}, u32[]{:S(2)}) collective-permute-start(bf16[4,2,2,24,768]{4,3,2,1,0:T(8,128)(2,1)S(1)} %fusion.21), channel_id=1, source_target_pairs={{0,1},{1,0},{2,3},{3,2},{4,5},{5,4},{6,7},{7,6},{8,9},{9,8},{10,11... | collective-permute-start | bytes 1769480 | tf_op jit(solution)/shard_map/ppermute | solution.py:539
  491.5 29.1 %collective-permute-start.22 = (bf16[4,2,2,24,2304]{4,3,2,1,0:T(8,128)(2,1)}, bf16[4,2,2,24,2304]{4,3,2,1,0:T(8,128)(2,1)}, u32[]{:S(2)}, u32[]{:S(2)}) collective-permute-start(bf16[4,2,2,24,2304]{4,3,2,1,0:T(8,128)(2,1)} %pad_maximum_fusion.1), channel_id=1, source_target_pairs={{0,1},{1,0},{2,3},{3,2},{4,5},{5,4},{6,7},{7,6},{8,9},{9,8},{10,11... | collective-permute-start | bytes 5308424 | tf_op jit(solution)/shard_map/ppermute | solution.py:539
  491.7 15.6 %all-to-all-start.8 = ((f32[32,1,256]{2,1,0:T(1,128)}), f32[32,1,256]{2,1,0:T(1,128)S(1)}, u32[]{:S(2)}, u32[]{:S(2)}) async-start(f32[32,1,256]{2,1,0:T(1,128)} %copy.202), calls=%async_computation.8 | async-start | bytes 65536 | tf_op jit(solution)/shard_map/all_to_all | solution.py:687
  509.5 9.2 %collective-permute-start.17 = (bf16[4,2,24,768]{3,2,1,0:T(8,128)(2,1)S(1)}, bf16[4,2,24,768]{3,2,1,0:T(8,128)(2,1)S(1)}, u32[]{:S(2)}, u32[]{:S(2)}) collective-permute-start(bf16[4,2,24,768]{3,2,1,0:T(8,128)(2,1)S(1)} %fusion.32), channel_id=1, source_target_pairs={{0,2},{1,3},{2,0},{3,1},{4,6},{5,7},{6,4},{7,5},{8,10},{9,11},{10,... | collective-permute-start | bytes 884744 | tf_op jit(solution)/shard_map/ppermute | solution.py:539
  518.9 9.1 %collective-permute-start.18 = (bf16[4,24,768]{2,1,0:T(8,128)(2,1)S(1)}, bf16[4,24,768]{2,1,0:T(8,128)(2,1)S(1)}, u32[]{:S(2)}, u32[]{:S(2)}) collective-permute-start(bf16[4,24,768]{2,1,0:T(8,128)(2,1)S(1)} %fusion.36), channel_id=1, source_target_pairs={{0,4},{1,5},{2,6},{3,7},{4,0},{5,1},{6,2},{7,3},{8,12},{9,13},{10,... | collective-permute-start | bytes 442376 | tf_op jit(solution)/shard_map/ppermute | solution.py:539
  523.8 15.9 %collective-permute-start.23 = (bf16[4,2,24,1536]{3,2,0,1:T(8,128)(2,1)S(1)}, bf16[4,2,24,1536]{3,2,0,1:T(8,128)(2,1)S(1)}, u32[]{:S(2)}, u32[]{:S(2)}) collective-permute-start(bf16[4,2,24,1536]{3,2,0,1:T(8,128)(2,1)S(1)} %pad_maximum_fusion.3), channel_id=1, source_target_pairs={{0,4},{1,5},{2,6},{3,7},{4,0},{5,1},{6,2},{7,3},{8,12},{9,13},{10,... | collective-permute-start | bytes 1769480 | tf_op jit(solution)/shard_map/ppermute | solution.py:539
  528.1 22.8 %collective-permute-start.19 = (bf16[24,768]{1,0:T(8,128)(2,1)S(1)}, bf16[24,768]{1,0:T(8,128)(2,1)S(1)}, u32[]{:S(2)}, u32[]{:S(2)}) collective-permute-start(bf16[24,768]{1,0:T(8,128)(2,1)S(1)} %get-tuple-element.169), channel_id=1, source_target_pairs={{0,8},{1,9},{2,10},{3,11},{4,12},{5,13},{6,14},{7,15},{8,16},{9,17... | collective-permute-start | bytes 110600 | tf_op jit(solution)/shard_map/ppermute | solution.py:539
  529.6 22.7 %collective-permute-start.20 = (bf16[24,768]{1,0:T(8,128)(2,1)S(1)}, bf16[24,768]{1,0:T(8,128)(2,1)S(1)}, u32[]{:S(2)}, u32[]{:S(2)}) collective-permute-start(bf16[24,768]{1,0:T(8,128)(2,1)S(1)} %get-tuple-element.171), channel_id=1, source_target_pairs={{0,16},{1,17},{2,18},{3,19},{4,20},{5,21},{6,22},{7,23},{8,24},{9,... | collective-permute-start | bytes 110600 | tf_op jit(solution)/shard_map/ppermute | solution.py:539
  532.1 20.3 %collective-permute-start.21 = (bf16[24,768]{1,0:T(8,128)(2,1)S(1)}, bf16[24,768]{1,0:T(8,128)(2,1)S(1)}, u32[]{:S(2)}, u32[]{:S(2)}) collective-permute-start(bf16[24,768]{1,0:T(8,128)(2,1)S(1)} %get-tuple-element.170), channel_id=1, source_target_pairs={{0,24},{1,25},{2,26},{3,27},{4,28},{5,29},{6,30},{7,31},{8,0},{9,1... | collective-permute-start | bytes 110600 | tf_op jit(solution)/shard_map/ppermute | solution.py:539
  (51 other events, 336.8 us)

commit v3 on v2

--- a/solution.py
+++ b/solution.py
@@ -129,8 +129,53 @@
     )(normed, weight, early_rows, seg_col, seg_row)
 
 
+def halves(grad, part_ref, own_ref):
+    half = part_ref.shape[0]
+    part_ref[...] = grad[:half].astype(BF16)
+    own_ref[...] = grad[half:]
+
+
+def outer_kernel(turned_ref, grad_ref, part_ref, own_ref):
+    halves(dot(turned_ref[...], grad_ref[...]), part_ref, own_ref)
+
+
+def outer(turned, grad, blocks):
+    rows, _ = turned.shape
+    width = grad.shape[1]
+    return pl.pallas_call(
+        outer_kernel,
+        grid=(1,),
+        in_specs=[whole(turned.shape), whole(grad.shape)],
+        out_specs=(
+            pl.BlockSpec((rows // 2, width), lambda i: (0, blocks - 1)),
+            whole((rows // 2, width)),
+        ),
+        out_shape=(
+            jax.ShapeDtypeStruct((rows // 2, blocks * width), BF16),
+            jax.ShapeDtypeStruct((rows // 2, width), F32),
+        ),
+        compiler_params=params(),
+        name="outer",
+    )(turned, grad)
+
+
 def attend_back_kernel(
-    qkv_ref, mix_ref, da_ref, wo_ref, lse_ref, sc_ref, sr_ref, out_ref, sum_ref, do_ref, dk_ref, dv_ref
+    qkv_ref,
+    mix_ref,
+    da_ref,
+    wo_ref,
+    lse_ref,
+    sc_ref,
+    sr_ref,
+    turned_ref,
+    _,
+    out_ref,
+    sum_ref,
+    part_ref,
+    own_ref,
+    do_ref,
+    dk_ref,
+    dv_ref,
 ):
     tokens = qkv_ref.shape[0]
     wide = mix_ref.shape[1]
@@ -182,9 +227,10 @@
     sum_ref[...] = jnp.broadcast_to(
         jnp.sum(out_ref[...].astype(F32), axis=0, keepdims=True), sum_ref.shape
     )
-
-
-def attend_back(group, qkv, mix, dattn, weight, block, lse, seg_col, seg_row):
+    halves(dot(turned_ref[...], out_ref[...]), part_ref, own_ref)
+
+
+def attend_back(group, qkv, mix, dattn, weight, block, lse, seg_col, seg_row, turned, parts):
     tokens, wide = mix.shape
     width = dattn.shape[1]
     return pl.pallas_call(
@@ -198,11 +244,21 @@
             whole(lse.shape),
             whole(seg_col.shape),
             whole(seg_row.shape),
+            whole(turned.shape),
+            pl.BlockSpec(memory_space=pl.ANY),
         ],
-        out_specs=(whole((tokens, 3 * wide)), whole((8, 3 * wide))),
+        out_specs=(
+            whole((tokens, 3 * wide)),
+            whole((8, 3 * wide)),
+            pl.BlockSpec((width // 2, 3 * wide), lambda i: (0, group)),
+            whole((width // 2, 3 * wide)),
+        ),
+        input_output_aliases={8: 2},
         out_shape=(
             jax.ShapeDtypeStruct((tokens, 3 * wide), BF16),
             jax.ShapeDtypeStruct((8, 3 * wide), F32),
+            jax.ShapeDtypeStruct(parts.shape, BF16),
+            jax.ShapeDtypeStruct((width // 2, 3 * wide), F32),
         ),
         scratch_shapes=[
             pltpu.VMEM((tokens, wide), BF16),
@@ -211,7 +267,7 @@
         ],
         compiler_params=params(),
         name="attend_back",
-    )(qkv, mix, dattn, weight, lse, seg_col, seg_row)
+    )(qkv, mix, dattn, weight, lse, seg_col, seg_row, turned, parts)
 
 
 def project_kernel(x_ref, m0_ref, m1_ref, m2_ref, wo_ref, vec_ref, hid_ref, moe_ref):
@@ -243,24 +299,29 @@
     )(x, *mixes, weight, vecs)
 
 
-def pack_kernel(base, target_ref, rows_ref, out_ref):
+def pack_kernel(base, target_ref, rows_ref, *refs):
+    out_ref = refs[-1]
     count = out_ref.shape[0]
     start = base + pl.program_id(0) * count
     hot = iota((count, rows_ref.shape[0]), 0) + start == target_ref[...]
     out_ref[...] = dot(jnp.where(hot, 1.0, 0.0).astype(BF16), rows_ref[...]).astype(BF16)
 
 
-def pack(rows, target_row, chunk, count):
+def pack(rows, target_row, base, count, total, kept=()):
     tokens, width = rows.shape
+    block = 512
+    first = base % total // block
     return pl.pallas_call(
-        functools.partial(pack_kernel, chunk * count),
-        grid=(count // 512,),
-        in_specs=[whole((1, tokens)), whole(rows.shape)],
-        out_specs=pl.BlockSpec((512, width), lambda i: (i, 0)),
-        out_shape=jax.ShapeDtypeStruct((count, width), BF16),
+        functools.partial(pack_kernel, base),
+        grid=(count // block,),
+        in_specs=[whole((1, tokens)), whole(rows.shape)]
+        + [pl.BlockSpec(memory_space=pl.ANY)] * len(kept),
+        out_specs=pl.BlockSpec((block, width), lambda i: (first + i, 0)),
+        out_shape=jax.ShapeDtypeStruct((total, width), BF16),
+        input_output_aliases={2: 0} if kept else {},
         compiler_params=params(),
         name="pack",
-    )(target_row, rows)
+    )(target_row, rows, *kept)
 
 
 def unpack_rows(target, refs):
@@ -312,15 +373,13 @@
     )(*slots, target_col, hidden, dy, vecs)
 
 
-def output_kernel(*refs):
-    slots = refs[:CHUNKS]
-    tgt_ref, route_ref, hid_ref, moe_ref, router_ref, out_ref = refs[CHUNKS:]
+def output_kernel(slots_ref, tgt_ref, route_ref, hid_ref, moe_ref, router_ref, out_ref):
     logits = dot(moe_ref[...], router_ref[...])
     chosen = jnp.sum(
         jnp.where(iota(logits.shape, 1) == route_ref[...], logits, 0.0), axis=1, keepdims=True
     )
     gate = jax.nn.sigmoid(chosen)
-    out_ref[...] = (hid_ref[...] + gate * unpack_rows(tgt_ref[...], slots)).astype(BF16)
+    out_ref[...] = (hid_ref[...] + gate * unpack_rows(tgt_ref[...], [slots_ref])).astype(BF16)
 
 
 def finish_output(slots, target_col, route_col, hidden, moe_in, weight, at, count):
@@ -329,14 +388,13 @@
     return pl.pallas_call(
         output_kernel,
         grid=(tokens // QBLOCK,),
-        in_specs=[whole(s.shape) for s in slots]
-        + [row(1), row(1), row(width), row(width)]
+        in_specs=[whole(slots.shape), row(1), row(1), row(width), row(width)]
         + [pl.BlockSpec((width, count), lambda i: (0, at // count))],
         out_specs=row(width),
         out_shape=jax.ShapeDtypeStruct((tokens, width), BF16),
         compiler_params=params(),
         name="finish_output",
-    )(*slots, target_col, route_col, hidden, moe_in, weight)
+    )(slots, target_col, route_col, hidden, moe_in, weight)
 
 
 def last_kernel(d0_ref, d1_ref, d2_ref, w0_ref, w1_ref, w2_ref, x_ref, dhid_ref, vec_ref, out_ref, sum_ref):
@@ -545,19 +603,27 @@
     return totals
 
 
-def scatter_rows(first, second, devices):
+def scatter_rows(parts, owns, split, devices):
     sizes = levels_of(devices)
-    count = len(first)
-    both = [g.reshape(sizes + (g.shape[0] // devices, g.shape[1])) for g in first + second]
-    both = scatter_level(both, devices, sizes, 3, 3)
-    first, second = both[:count], both[count:]
+    got = lax.ppermute(parts, "dp", cyclic(devices, sizes, 3, 1))
+    width = owns[0].shape[1]
+    shape = sizes[:3] + (owns[0].shape[0] * 2 // devices, width)
+    both = [
+        (own + got[:, n * width : (n + 1) * width].astype(F32)).reshape(shape) for n, own in enumerate(owns)
+    ]
+    first, second = both[:split], both[split:]
     first = scatter_level(first, devices, sizes, 2, 2)
-    if second:
-        second = scatter_level(second, devices, sizes, 1, 1)
+    second = scatter_level(second, devices, sizes, 1, 1)
     first = scatter_level(first, devices, sizes, 1, 1)
-    if second:
-        second = scatter_level(second, devices, sizes, 2, 1)
+    second = scatter_level(second, devices, sizes, 2, 1)
     return scatter_level(first + second, devices, sizes, 0, 0)
+
+
+def other_first(rows, devices):
+    place = coordinate(levels_of(devices), 3)
+    split = rows.reshape(devices // 2, 2, rows.shape[0] // devices, rows.shape[1])
+    pick = lambda index: lax.dynamic_index_in_dim(split, index, 1, keepdims=False)
+    return jnp.concatenate([pick(1 - place), pick(place)], axis=0).reshape(rows.shape)
 
 
 def exchange(slots, experts):
@@ -627,10 +693,23 @@
         preferred_element_type=F32,
     )
     slot = jnp.sum(jnp.where(onehot, earlier, 0.0), axis=1).astype(jnp.int32)
-    target = (slot // per_chunk) * chunk_rows + route * per_chunk + slot % per_chunk
-    target_row, target_col = target[None, :], target[:, None]
-
-    dys = [exchange(pack(dy, target_row, c, chunk_rows), experts) for c in range(CHUNKS)]
+
+    def places_of(route, slot):
+        chunk = sum(jnp.where(slot >= n * per_chunk, 1, 0) for n in range(1, CHUNKS))
+        return chunk * (chunk_rows - per_chunk) + route * per_chunk + slot, route * capacity + slot
+
+    target_row, entire_row = places_of(route[None, :], slot[None, :])
+    route_col = route[:, None]
+    target_col, entire_col = places_of(route_col, slot[:, None])
+
+    slots = CHUNKS * chunk_rows
+    dy_slots = ()
+    for c in range(CHUNKS):
+        dy_slots = (
+            pack(dy, entire_row, c * chunk_rows, chunk_rows, slots, dy_slots),
+        )
+    dy_slots = exchange(dy_slots[0], experts).reshape(experts, CHUNKS, per_chunk, width)
+    dys = [dy_slots[:, c].reshape(chunk_rows, width) for c in range(CHUNKS)]
     w_in = expert_in[0].astype(BF16)
     w_out = expert_out[0].astype(BF16)
 
@@ -649,7 +728,15 @@
     expert_vecs = jnp.concatenate([expert_out_bias, router_row, jnp.zeros((6, width), F32)], axis=0)
     returned, dmoes, kept = [], [], ()
     dbias_in = dsums = 0.0
-    received = [exchange(pack(moe_in, target_row, c, chunk_rows), experts) for c in range(CHUNKS)]
+    received = [
+        exchange(pack(moe_in, target_row, c * chunk_rows, chunk_rows, chunk_rows), experts)
+        for c in range(CHUNKS)
+    ]
+    mix_t = other_first(jnp.concatenate(mixes, axis=1).T, devices)
+    normed_t = other_first(normed.T, devices)
+    received[0], target_col, entire_col, route_col, mix_t, normed_t = lax.optimization_barrier(
+        (received[0], target_col, entire_col, route_col, mix_t, normed_t)
+    )
     for c in range(CHUNKS):
         ret, dmoe, *kept, dbias, sums = expert_chunk(
             c, CHUNKS * chunk_rows, received[c], dys[c], w_in, expert_in_bias, w_out, expert_vecs, kept
@@ -661,20 +748,23 @@
     act, dpre, arrived, rows_in = kept
     grad_expert_out = dot_tn(act, arrived)
     grad_expert_in = dot_tn(rows_in, dpre)
-    returned = [exchange(r, experts) for r in returned]
+    returned = jnp.stack([r.reshape(experts, per_chunk, width) for r in returned], axis=1)
+    returned = exchange(returned.reshape(slots, width), experts)
 
     dhid, dattn, mid_sums = middle(dmoes, target_col, hidden, dy, vecs)
-    part_out = dot_tn(jnp.concatenate(mixes, axis=1), dattn)
-    dqkvs, qkv_sums, parts = [None] * GROUPS, [None] * GROUPS, [None] * GROUPS
-    for g in reversed(range(GROUPS)):
-        dqkvs[g], col_sums = attend_back(g, qkvs[g], mixes[g], dattn, full_late, out_place, lses[g], seg_col, seg_row)
-        qkv_sums[g] = col_sums[0:1]
-        parts[g] = dot_tn(normed, dqkvs[g])
-    grad_out, *upper = scatter_rows([part_out], parts[1:], devices)
-    grad_qkv = scatter_rows(parts[:1], [], devices) + upper
+    parts, own_out = outer(mix_t, dattn, GROUPS + 1)
+    dqkvs, qkv_sums, owns = [], [], []
+    for g in range(GROUPS):
+        dqkv, col_sums, parts, own = attend_back(
+            g, qkvs[g], mixes[g], dattn, full_late, out_place, lses[g], seg_col, seg_row, normed_t, parts
+        )
+        dqkvs.append(dqkv)
+        qkv_sums.append(col_sums[0:1])
+        owns.append(own)
+    *grad_qkv, grad_out = scatter_rows(parts, owns + [own_out], 2, devices)
     grad_inputs, last_sums = last(dqkvs, weights, places, x, dhid, early_rows)
     output = finish_output(
-        returned, target_col, route.reshape(tokens, 1), hidden, moe_in, full_late, router_at, router_wide
+        returned, entire_col, route_col, hidden, moe_in, full_late, router_at, router_wide
     )
 
     grad_query = jnp.concatenate([s[:, :wide] for s in qkv_sums], axis=1)

time: 565 us -> 626 us (1.11)
  waiting for transfers between devices: 140 us -> 203 us
  starting transfers between devices: 76.9 us -> 51.7 us
  Pallas kernels: 185 us -> 197 us
  local copies, waits for them, and re-layouts: 28.4 us -> 36.1 us
  matrix products: 39.4 us -> 31.9 us
  other arithmetic: 42.5 us -> 49.8 us
    all_to_all x7 -> x5, waiting for transfers between devices: 61.9 us -> 130 us  [exchange(): lax.all_to_all(slots.reshape(experts, rows // experts, width), 'dp', spli...]
    ppermute x16, waiting for transfers between devices: 57 us -> 23.6 us  [shifted(): parts.append(lax.ppermute(block, 'dp', cyclic(devices, sizes, axis, shift)))]
    ppermute x14 -> x7, waiting for transfers between devices: 21.5 us -> 43.6 us  [scatter_level(): got = lax.ppermute(part, 'dp', cyclic(devices, sizes, axis, shift))]
    all_to_all x7 -> x5, starting transfers between devices: 31.6 us -> 17.2 us  [exchange(): lax.all_to_all(slots.reshape(experts, rows // experts, width), 'dp', spli...]
    ppermute x14 -> x7, starting transfers between devices: 19.1 us -> 11.1 us  [scatter_level(): got = lax.ppermute(part, 'dp', cyclic(devices, sizes, axis, shift))]
    pallas_call x3, Pallas kernels: 38.9 us -> 46.8 us  [attend_back(): pl.pallas_call(attend_back_kernel, grid=(1,), in_specs=[whole(qkv.shape),...]
    dot_general x6 -> x2, matrix products: 38.8 us -> 31.4 us  [dot_tn(): lax.dot_general(a, b, (((0,), (0,)), ((), ())), preferred_element_type=F32)]
    pallas_call x4 -> x5, Pallas kernels: 17.2 us -> 21.6 us  [the longest x4 17.2 us: pack(): pl.pallas_call(functools.partial(pack_kernel, base), grid=(count // block...]
  transfers between devices with their start and end apart: 38 -> 30, of which waited for: 13 -> 14; matrix products, arithmetic and copies ran while one was open for 17% -> 16% of each run, Pallas kernels for 27% -> 12%
where the time goes in v3:
time: 626 us; the launch traced here: 615 us
  waiting for transfers between devices  203 us (32%)
  Pallas kernels  197 us (31%)
  starting transfers between devices  51.7 us (8%)
  other arithmetic  49.8 us (8%)
  blocking collectives  44 us (7%)
  local copies, waits for them, and re-layouts  36.1 us (6%)
  matrix products  31.9 us (5%)
    all_to_all x5, waiting for transfers between devices, exchange(): lax.all_to_all(slots.reshape(experts, rows // experts, width), 'dp', spli...  130 us
    pallas_call x2, Pallas kernels, expert_chunk(): pl.pallas_call(functools.partial(expert_kernel, aliased), grid=(hidden //...  62.4 us
    pallas_call x3, Pallas kernels, attend_back(): pl.pallas_call(attend_back_kernel, grid=(1,), in_specs=[whole(qkv.shape),...  46.8 us
    all_to_all x1, blocking collectives, exchange(): lax.all_to_all(slots.reshape(experts, rows // experts, width), 'dp', spli...  44 us
    ppermute x7, waiting for transfers between devices, scatter_level(): got = lax.ppermute(part, 'dp', cyclic(devices, sizes, axis, shift))  43.6 us
    pallas_call x3, Pallas kernels, attend(): pl.pallas_call(attend_kernel, grid=(1,), in_specs=[whole(normed.shape), p...  31.7 us
    dot_general x2, matrix products, dot_tn(): lax.dot_general(a, b, (((0,), (0,)), ((), ())), preferred_element_type=F32)  31.4 us
    ppermute x16, waiting for transfers between devices, shifted(): parts.append(lax.ppermute(block, 'dp', cyclic(devices, sizes, axis, shift)))  23.6 us
  transfers between devices with their start and end apart: 30, of which 14 were waited for; matrix products, arithmetic and copies ran while one was open for 16% of the time, Pallas kernels for 12%

profile of v3, /device:TPU:0, one launch (start us, length us, event | category | flops | bytes accessed | tf_op | source)
XLA Modules:
  0.0 614.9 jit_solution(17797703512238644404)
XLA Ops:
  30.1 6.2 %collective-permute-done.4 = bf16[4,2,24,384]{3,2,0,1:T(8,128)(2,1)S(1)} collective-permute-done((bf16[4,2,24,384]{3,2,0,1:T(8,128)(2,1)S(1)}, bf16[4,2,24,384]{3,2,0,1:T(8,128)(2,1)S(1)}, u32[]{:S(2)}, u32[]{:S(2)}) %collective-permute-start.4) | collective-permute-done | bytes 147488 | tf_op jit(solution)/shard_map/ppermute | solution.py:552
  39.9 5.4 collective-permute-done.12
  45.4 7.5 %collective-permute-done.14 = bf16[4,2,24,1280]{3,2,0,1:T(8,128)(2,1)S(1)} collective-permute-done((bf16[4,2,24,1280]{3,2,0,1:T(8,128)(2,1)S(1)}, bf16[4,2,24,1280]{3,2,0,1:T(8,128)(2,1)S(1)}, u32[]{:S(2)}, u32[]{:S(2)}) %collective-permute-start.14) | collective-permute-done | bytes 491552 | tf_op jit(solution)/shard_map/ppermute | solution.py:552
  62.8 10.6 %attend.3 = (bf16[1024,768]{1,0:T(8,128)(2,1)}, bf16[1024,256]{1,0:T(8,128)(2,1)}, f32[8,1024]{1,0:T(8,128)}) custom-call(bf16[1024,768]{1,0:T(8,128)(2,1)} %fusion.6.x_ref, bf16[768,896]{1,0:T(8,128)(2,1)} %bitcast.263, f32[8,768]{1,0:T(8,128)} %copy-done.25, s32[1024,1]{1,0:T(8,128)} %copy.153.sc_ref, s32[1,1024]{1,0:T(1,128)} %sr_ref.11), custom_call_target="tpu_custom_call" | custom-call | tf_op jit(solution)/shard_map/attend/pallas_call | solution.py:111
  78.4 10.5 %attend.5 = (bf16[1024,768]{1,0:T(8,128)(2,1)}, bf16[1024,256]{1,0:T(8,128)(2,1)}, f32[8,1024]{1,0:T(8,128)}) custom-call(bf16[1024,768]{1,0:T(8,128)(2,1)} %fusion.6.x_ref, bf16[768,2432]{1,0:T(8,128)(2,1)} %bitcast.243, f32[8,768]{1,0:T(8,128)} %copy-done.25, s32[1024,1]{1,0:T(8,128)} %copy.153.sc_ref, s32[1,1024]{1,0:T(1,128)} %sr_ref.11), custom_call_target="tpu_custom_call" | custom-call | tf_op jit(solution)/shard_map/attend/pallas_call | solution.py:111
  88.9 10.7 %attend.4 = (bf16[1024,768]{1,0:T(8,128)(2,1)}, bf16[1024,256]{1,0:T(8,128)(2,1)}, f32[8,1024]{1,0:T(8,128)}) custom-call(bf16[1024,768]{1,0:T(8,128)(2,1)} %fusion.6.x_ref, bf16[768,2432]{1,0:T(8,128)(2,1)} %bitcast.244, f32[8,768]{1,0:T(8,128)} %copy-done.25, s32[1024,1]{1,0:T(8,128)} %copy.153.sc_ref, s32[1,1024]{1,0:T(1,128)} %sr_ref.11), custom_call_target="tpu_custom_call" | custom-call | tf_op jit(solution)/shard_map/attend/pallas_call | solution.py:111
  101.4 5.9 project.1
  107.4 4.3 pack.4
  115.1 4.3 pack.5.refs_0_
  119.5 4.3 pack.6
  123.8 29.0 %all-to-all-done = bf16[32,32,768]{2,1,0:T(8,128)(2,1)S(1)} async-done(((bf16[32,32,768]{2,1,0:T(8,128)(2,1)}), bf16[32,32,768]{2,1,0:T(8,128)(2,1)S(1)}, u32[]{:S(2)}, u32[]{:S(2)}) %all-to-all-start) | async-done | bytes 1572896 | tf_op jit(solution)/shard_map/all_to_all | solution.py:631
  157.8 4.3 pack.7
  162.1 67.0 %all-to-all-done.1 = bf16[32,64,768]{2,1,0:T(8,128)(2,1)S(1)} async-done(((bf16[32,64,768]{2,1,0:T(8,128)(2,1)}), bf16[32,64,768]{2,1,0:T(8,128)(2,1)S(1)}, u32[]{:S(2)}, u32[]{:S(2)}) %all-to-all-start.1) | async-done | bytes 3145760 | tf_op jit(solution)/shard_map/all_to_all | solution.py:631
  233.3 6.3 %convert_bitcast_fusion.refs_4_ = bf16[3072,768]{1,0:T(8,128)(2,1)} fusion(f32[1,3072,768]{2,1,0:T(8,128)} %param.34), kind=kLoop, calls=%fused_computation.2 | loop fusion | flops 2359296 | bytes 14155776 | tf_op jit(solution)/shard_map/convert_element_type | solution.py:714
  245.9 6.7 %convert_bitcast_fusion.1.refs_2_ = bf16[768,3072]{1,0:T(8,128)(2,1)} fusion(f32[1,768,3072]{2,1,0:T(8,128)} %param.32), kind=kLoop, calls=%fused_computation.3 | loop fusion | flops 2359296 | bytes 14155776 | tf_op jit(solution)/shard_map/convert_element_type | solution.py:713
  270.0 31.0 %expert.2 = (bf16[1024,768]{1,0:T(8,128)(2,1)}, bf16[1024,768]{1,0:T(8,128)(2,1)}, bf16[2048,3072]{1,0:T(8,128)(2,1)}, bf16[2048,3072]{1,0:T(8,128)(2,1)}, bf16[...) custom-call(bf16[1024,768]{1,0:T(8,128)(2,1)} %bitcast.276, ...), custom_call_target="tpu_custom_call" | custom-call | tf_op jit(solution)/shard_map/expert/pallas_call | solution.py:487
  301.0 31.4 %expert.3 = (bf16[1024,768]{1,0:T(8,128)(2,1)}, bf16[1024,768]{1,0:T(8,128)(2,1)}, bf16[2048,3072]{1,0:T(8,128)(2,1)}, bf16[2048,3072]{1,0:T(8,128)(2,1)}, bf16[...) custom-call(bf16[1024,768]{1,0:T(8,128)(2,1)} %bitcast.73.refs_0_, ...), custom_call_target="tpu_custom_call", output_to_operand_aliasing={{2}: (6, {}), {3}: (7, {}), {4}: (8, {}), {5}: (9, {})} | custom-call | tf_op jit(solution)/shard_map/expert/pallas_call | solution.py:487
  332.4 44.0 %all_to_all.42 = bf16[32,32,768]{2,1,0:T(8,128)(2,1)} all-to-all(bf16[32,32,768]{2,1,0:T(8,128)(2,1)} %bitcast.287), channel_id=1, replica_groups=mesh['dp'=32] {'dp'}, dimensions={0} | all-to-all | bytes 3145728 | tf_op jit(solution)/shard_map/all_to_all | solution.py:631
  380.5 16.1 %convolution_bitcast_fusion.1 = f32[1,768,3072]{2,1,0:T(8,128)} fusion(bf16[2048,768]{1,0:T(8,128)(2,1)} %get-tuple-element.114, bf16[2048,3072]{1,0:T(8,128)(2,1)} %get-tuple-element.115), kind=kOutput, calls=%fused_computation.1 | convolution fusion | flops 9663676416 | bytes 25165824 | tf_op jit(solution)/shard_map/dot_general | solution.py:35
  396.7 20.4 %all-to-all-done.4 = bf16[32,32,768]{2,1,0:T(8,128)(2,1)S(1)} async-done(((bf16[32,32,768]{2,1,0:T(8,128)(2,1)}), bf16[32,32,768]{2,1,0:T(8,128)(2,1)S(1)}, u32[]{:S(2)}, u32[]{:S(2)}) %all-to-all-start.4) | async-done | bytes 1572896 | tf_op jit(solution)/shard_map/all_to_all | solution.py:631
  418.2 9.8 %middle.1 = (f32[1024,768]{1,0:T(8,128)}, bf16[1024,768]{1,0:T(8,128)(2,1)}, f32[8,768]{1,0:T(8,128)}) custom-call(bf16[1024,768]{1,0:T(8,128)(2,1)} %bitcast.272, bf16[1024,768]{1,0:T(8,128)(2,1)} %bitcast.271, s32[1024,1]{1,0:T(8,128)} %get-tuple-element.85.refs_2_, f32[1024,768]{1,0:T(8,128)} %get-tuple-element.81.hid_ref.refs_3_, ...), custom_call_target="tpu_custom_call" | custom-call | tf_op jit(solution)/shard_map/middle/pallas_call | solution.py:361
  428.0 4.4 outer.1
  432.4 15.3 %attend_back.3 = (bf16[1024,768]{1,0:T(8,128)(2,1)}, f32[8,768]{1,0:T(8,128)}, bf16[384,3072]{1,0:T(8,128)(2,1)}, f32[384,768]{1,0:T(8,128)}) custom-call(bf16[1024,768]{1,0:T(8,128)(2,1)} %get-tuple-element.82.qkv_ref, bf16[1024,256]{1,0:T(8,128)(2,1)} %get-tuple-element.68.m0_ref.mix_ref, ...), custom_call_target="tpu_custom_call", output_to_operand_aliasing={{2}: (8, {})} | custom-call | tf_op jit(solution)/shard_map/attend_back/pallas_call | solution.py:236
  447.7 15.6 %attend_back.4 = (bf16[1024,768]{1,0:T(8,128)(2,1)}, f32[8,768]{1,0:T(8,128)}, bf16[384,3072]{1,0:T(8,128)(2,1)}, f32[384,768]{1,0:T(8,128)}) custom-call(bf16[1024,768]{1,0:T(8,128)(2,1)} %get-tuple-element.92.qkv_ref, bf16[1024,256]{1,0:T(8,128)(2,1)} %get-tuple-element.69.m1_ref.mix_ref, ...), custom_call_target="tpu_custom_call", output_to_operand_aliasing={{2}: (8, {})} | custom-call | tf_op jit(solution)/shard_map/attend_back/pallas_call | solution.py:236
  463.3 15.9 %attend_back.5 = (bf16[1024,768]{1,0:T(8,128)(2,1)}, f32[8,768]{1,0:T(8,128)}, bf16[384,3072]{1,0:T(8,128)(2,1)}, f32[384,768]{1,0:T(8,128)}) custom-call(bf16[1024,768]{1,0:T(8,128)(2,1)} %get-tuple-element.96.qkv_ref, bf16[1024,256]{1,0:T(8,128)(2,1)} %get-tuple-element.70.m2_ref.mix_ref, ...), custom_call_target="tpu_custom_call", output_to_operand_aliasing={{2}: (8, {})} | custom-call | tf_op jit(solution)/shard_map/attend_back/pallas_call | solution.py:236
  479.3 15.3 %convolution_bitcast_fusion = f32[1,3072,768]{2,1,0:T(8,128)} fusion(bf16[2048,3072]{1,0:T(8,128)(2,1)} %get-tuple-element.118, bf16[2048,768]{1,0:T(8,128)(2,1)S(1)} %copy-done.15), kind=kOutput, calls=%fused_computation | convolution fusion | flops 9663676416 | bytes 25165824 | tf_op jit(solution)/shard_map/dot_general | solution.py:35
  495.1 10.4 %last.1 = (f32[1024,768]{1,0:T(8,128)}, f32[8,768]{1,0:T(8,128)}) custom-call(bf16[1024,768]{1,0:T(8,128)(2,1)} %get-tuple-element.91.d0_ref, bf16[1024,768]{1,0:T(8,128)(2,1)} %get-tuple-element.95.d1_ref, bf16[1024,768]{1,0:T(8,128)(2,1)} %get-tuple-element.99.d2_ref, bf16[768,896]{1,0:T(8,128)(2,1)} %bitcast.264, bf16[768,2432]{1,0:T(8,128)(2,1)} %bitcast.250, ...), custom_call_target="tpu_custom_call" | custom-call | tf_op jit(solution)/shard_map/last/pallas_call | solution.py:418
  515.6 5.0 all-to-all-done.6
  532.8 35.5 %collective-permute-done.17 = bf16[4,2,24,1536]{3,2,0,1:T(8,128)(2,1)S(1)} collective-permute-done((bf16[4,2,24,1536]{3,2,0,1:T(8,128)(2,1)S(1)}, bf16[4,2,24,1536]{3,2,0,1:T(8,128)(2,1)S(1)}, u32[]{:S(2)}, u32[]{:S(2)}) %collective-permute-start.17) | collective-permute-done | bytes 589856 | tf_op jit(solution)/shard_map/ppermute | solution.py:597
  570.9 8.1 %collective-permute-done.18 = bf16[4,24,1536]{2,1,0:T(8,128)(2,1)S(1)} collective-permute-done((bf16[4,24,1536]{2,1,0:T(8,128)(2,1)S(1)}, bf16[4,24,1536]{2,1,0:T(8,128)(2,1)S(1)}, u32[]{:S(2)}, u32[]{:S(2)}) %collective-permute-start.18) | collective-permute-done | bytes 294944 | tf_op jit(solution)/shard_map/ppermute | solution.py:597
  587.8 14.1 %all-to-all-done.3 = bf16[32,64,768]{2,1,0:T(8,128)(2,1)S(1)} async-done(((bf16[32,64,768]{2,1,0:T(8,128)(2,1)}), bf16[32,64,768]{2,1,0:T(8,128)(2,1)S(1)}, u32[]{:S(2)}, u32[]{:S(2)}) %all-to-all-start.3) | async-done | bytes 3145760 | tf_op jit(solution)/shard_map/all_to_all | solution.py:631
  603.5 8.1 %finish_output.1 = bf16[1024,768]{1,0:T(8,128)(2,1)} custom-call(bf16[2048,768]{1,0:T(8,128)(2,1)} %bitcast.265, s32[1024,1]{1,0:T(8,128)} %get-tuple-element.79.tgt_ref, s32[1024,1]{1,0:T(8,128)} %copy.170.route_ref, f32[1024,768]{1,0:T(8,128)} %get-tuple-element.81.hid_ref.refs_3_, bf16[1024,768]{1,0:T(8,128)(2,1)} %get-tuple-element.71.rows_ref.moe_ref, ...), custom_call_target="tpu_custom_call" | custom-call | tf_op jit(solution)/shard_map/finish_output/pallas_call | solution.py:388
  (257 shorter events, 129.5 us)
Async XLA Ops:
  6.0 17.8 %collective-permute-start.10 = (bf16[24,2432]{1,0:T(8,128)(2,1)S(1)}, bf16[24,2432]{1,0:T(8,128)(2,1)S(1)}, u32[]{:S(2)}, u32[]{:S(2)}) collective-permute-start(bf16[24,2432]{1,0:T(8,128)(2,1)S(1)} %pad_maximum_fusion.21), channel_id=1, source_target_pairs={{0,8},{1,9},{2,10},{3,11},{4,12},{5,13},{6,14},{7,15},{8,16},{9,17... | collective-permute-start | bytes 350216 | tf_op jit(solution)/shard_map/ppermute | solution.py:552
  9.1 14.7 %collective-permute-start.8 = (bf16[24,2432]{1,0:T(8,128)(2,1)S(1)}, bf16[24,2432]{1,0:T(8,128)(2,1)S(1)}, u32[]{:S(2)}, u32[]{:S(2)}) collective-permute-start(bf16[24,2432]{1,0:T(8,128)(2,1)S(1)} %pad_maximum_fusion.21), channel_id=1, source_target_pairs={{0,24},{1,25},{2,26},{3,27},{4,28},{5,29},{6,30},{7,31},{8,0},{9,1... | collective-permute-start | bytes 350216 | tf_op jit(solution)/shard_map/ppermute | solution.py:552
  12.7 4.5 collective-permute-start
  14.7 5.4 collective-permute-start.1
  14.7 5.9 collective-permute-start.2
  17.2 8.3 %collective-permute-start.9 = (bf16[24,2432]{1,0:T(8,128)(2,1)S(1)}, bf16[24,2432]{1,0:T(8,128)(2,1)S(1)}, u32[]{:S(2)}, u32[]{:S(2)}) collective-permute-start(bf16[24,2432]{1,0:T(8,128)(2,1)S(1)} %pad_maximum_fusion.21), channel_id=1, source_target_pairs={{0,16},{1,17},{2,18},{3,19},{4,20},{5,21},{6,22},{7,23},{8,24},{9,... | collective-permute-start | bytes 350216 | tf_op jit(solution)/shard_map/ppermute | solution.py:552
  20.6 8.2 %collective-permute-start.3 = (bf16[4,24,384]{2,1,0:T(8,128)(2,1)S(1)}, bf16[4,24,384]{2,1,0:T(8,128)(2,1)S(1)}, u32[]{:S(2)}, u32[]{:S(2)}) collective-permute-start(bf16[4,24,384]{2,1,0:T(8,128)(2,1)S(1)} %pad_maximum_fusion.25), channel_id=1, source_target_pairs={{0,4},{1,5},{2,6},{3,7},{4,0},{5,1},{6,2},{7,3},{8,12},{9,13},{10,... | collective-permute-start | bytes 221192 | tf_op jit(solution)/shard_map/ppermute | solution.py:552
  22.2 7.3 %collective-permute-start.5 = (bf16[4,24,512]{2,1,0:T(8,128)(2,1)S(1)}, bf16[4,24,512]{2,1,0:T(8,128)(2,1)S(1)}, u32[]{:S(2)}, u32[]{:S(2)}) collective-permute-start(bf16[4,24,512]{2,1,0:T(8,128)(2,1)S(1)} %pad_maximum_fusion.22), channel_id=1, source_target_pairs={{0,2},{1,3},{2,0},{3,1},{4,6},{5,7},{6,4},{7,5},{8,10},{9,11},{10,... | collective-permute-start | bytes 294920 | tf_op jit(solution)/shard_map/ppermute | solution.py:552
  25.7 10.6 %collective-permute-start.11 = (bf16[4,24,1152]{2,1,0:T(8,128)(2,1)S(1)}, bf16[4,24,1152]{2,1,0:T(8,128)(2,1)S(1)}, u32[]{:S(2)}, u32[]{:S(2)}) collective-permute-start(bf16[4,24,1152]{2,1,0:T(8,128)(2,1)S(1)} %pad_maximum_fusion.15), channel_id=1, source_target_pairs={{0,4},{1,5},{2,6},{3,7},{4,0},{5,1},{6,2},{7,3},{8,12},{9,13},{10,... | collective-permute-start | bytes 663560 | tf_op jit(solution)/shard_map/ppermute | solution.py:552
  27.3 11.8 %collective-permute-start.13 = (bf16[4,24,1280]{2,1,0:T(8,128)(2,1)S(1)}, bf16[4,24,1280]{2,1,0:T(8,128)(2,1)S(1)}, u32[]{:S(2)}, u32[]{:S(2)}) collective-permute-start(bf16[4,24,1280]{2,1,0:T(8,128)(2,1)S(1)} %pad_maximum_fusion.12), channel_id=1, source_target_pairs={{0,2},{1,3},{2,0},{3,1},{4,6},{5,7},{6,4},{7,5},{8,10},{9,11},{10,... | collective-permute-start | bytes 737288 | tf_op jit(solution)/shard_map/ppermute | solution.py:552
  28.9 7.4 %collective-permute-start.4 = (bf16[4,2,24,384]{3,2,0,1:T(8,128)(2,1)S(1)}, bf16[4,2,24,384]{3,2,0,1:T(8,128)(2,1)S(1)}, u32[]{:S(2)}, u32[]{:S(2)}) collective-permute-start(bf16[4,2,24,384]{3,2,0,1:T(8,128)(2,1)S(1)} %pad_maximum_fusion.17), channel_id=1, source_target_pairs={{0,2},{1,3},{2,0},{3,1},{4,6},{5,7},{6,4},{7,5},{8,10},{9,11},{10,... | collective-permute-start | bytes 442376 | tf_op jit(solution)/shard_map/ppermute | solution.py:552
  29.6 8.5 %collective-permute-start.6 = (bf16[4,2,24,512]{3,2,0,1:T(8,128)(2,1)S(1)}, bf16[4,2,24,512]{3,2,0,1:T(8,128)(2,1)S(1)}, u32[]{:S(2)}, u32[]{:S(2)}) collective-permute-start(bf16[4,2,24,512]{3,2,0,1:T(8,128)(2,1)S(1)} %pad_maximum_fusion.16), channel_id=1, source_target_pairs={{0,4},{1,5},{2,6},{3,7},{4,0},{5,1},{6,2},{7,3},{8,12},{9,13},{10,... | collective-permute-start | bytes 589832 | tf_op jit(solution)/shard_map/ppermute | solution.py:552
  36.5 8.7 %collective-permute-start.12 = (bf16[4,2,24,1152]{3,2,0,1:T(8,128)(2,1)S(1)}, bf16[4,2,24,1152]{3,2,0,1:T(8,128)(2,1)S(1)}, u32[]{:S(2)}, u32[]{:S(2)}) collective-permute-start(bf16[4,2,24,1152]{3,2,0,1:T(8,128)(2,1)S(1)} %pad_maximum_fusion.8), channel_id=1, source_target_pairs={{0,2},{1,3},{2,0},{3,1},{4,6},{5,7},{6,4},{7,5},{8,10},{9,11},{10,... | collective-permute-start | bytes 1327112 | tf_op jit(solution)/shard_map/ppermute | solution.py:552
  39.1 18.3 %collective-permute-start.7 = (bf16[4,2,2,24,896]{4,3,0,2,1:T(8,128)(2,1)}, bf16[4,2,2,24,896]{4,3,0,2,1:T(8,128)(2,1)}, u32[]{:S(2)}, u32[]{:S(2)}) collective-permute-start(bf16[4,2,2,24,896]{4,3,0,2,1:T(8,128)(2,1)} %maximum_maximum_fusion.1), channel_id=1, source_target_pairs={{0,1},{1,0},{2,3},{3,2},{4,5},{5,4},{6,7},{7,6},{8,9},{9,8},{10,11... | collective-permute-start | bytes 2064392 | tf_op jit(solution)/shard_map/ppermute | solution.py:552
  39.3 13.7 %collective-permute-start.14 = (bf16[4,2,24,1280]{3,2,0,1:T(8,128)(2,1)S(1)}, bf16[4,2,24,1280]{3,2,0,1:T(8,128)(2,1)S(1)}, u32[]{:S(2)}, u32[]{:S(2)}) collective-permute-start(bf16[4,2,24,1280]{3,2,0,1:T(8,128)(2,1)S(1)} %pad_maximum_fusion.7), channel_id=1, source_target_pairs={{0,4},{1,5},{2,6},{3,7},{4,0},{5,1},{6,2},{7,3},{8,12},{9,13},{10,... | collective-permute-start | bytes 1474568 | tf_op jit(solution)/shard_map/ppermute | solution.py:552
  54.5 18.9 %collective-permute-start.15 = (bf16[4,2,2,24,2432]{4,3,0,2,1:T(8,128)(2,1)}, bf16[4,2,2,24,2432]{4,3,0,2,1:T(8,128)(2,1)}, u32[]{:S(2)}, u32[]{:S(2)}) collective-permute-start(bf16[4,2,2,24,2432]{4,3,0,2,1:T(8,128)(2,1)} %maximum_maximum_fusion), channel_id=1, source_target_pairs={{0,1},{1,0},{2,3},{3,2},{4,5},{5,4},{6,7},{7,6},{8,9},{9,8},{10,11... | collective-permute-start | bytes 5603336 | tf_op jit(solution)/shard_map/ppermute | solution.py:552
  111.7 41.1 %all-to-all-start = ((bf16[32,32,768]{2,1,0:T(8,128)(2,1)}), bf16[32,32,768]{2,1,0:T(8,128)(2,1)S(1)}, u32[]{:S(2)}, u32[]{:S(2)}) async-start(bf16[32,32,768]{2,1,0:T(8,128)(2,1)} %bitcast.274), calls=%async_computation | async-start | bytes 3145728 | tf_op jit(solution)/shard_map/all_to_all | solution.py:631
  154.0 75.1 %all-to-all-start.1 = ((bf16[32,64,768]{2,1,0:T(8,128)(2,1)}), bf16[32,64,768]{2,1,0:T(8,128)(2,1)S(1)}, u32[]{:S(2)}, u32[]{:S(2)}) async-start(bf16[32,64,768]{2,1,0:T(8,128)(2,1)} %bitcast.255), calls=%async_computation.1 | async-start | bytes 6291456 | tf_op jit(solution)/shard_map/all_to_all | solution.py:631
  229.1 71.9 %all-to-all-start.2 = ((bf16[32,32,768]{2,1,0:T(8,128)(2,1)}), bf16[32,32,768]{2,1,0:T(8,128)(2,1)}, u32[]{:S(2)}, u32[]{:S(2)}) async-start(bf16[32,32,768]{2,1,0:T(8,128)(2,1)} %bitcast.270), calls=%async_computation.2 | async-start | bytes 3145728 | tf_op jit(solution)/shard_map/all_to_all | solution.py:631
  376.4 40.6 %all-to-all-start.4 = ((bf16[32,32,768]{2,1,0:T(8,128)(2,1)}), bf16[32,32,768]{2,1,0:T(8,128)(2,1)S(1)}, u32[]{:S(2)}, u32[]{:S(2)}) async-start(bf16[32,32,768]{2,1,0:T(8,128)(2,1)} %bitcast.79), calls=%async_computation.4 | async-start | bytes 3145728 | tf_op jit(solution)/shard_map/all_to_all | solution.py:631
  479.2 46.5 %collective-permute-start.16 = (bf16[384,3072]{1,0:T(8,128)(2,1)}, bf16[384,3072]{1,0:T(8,128)(2,1)}, u32[]{:S(2)}, u32[]{:S(2)}) collective-permute-start(bf16[384,3072]{1,0:T(8,128)(2,1)} %get-tuple-element.103), channel_id=1, source_target_pairs={{0,1},{1,0},{2,3},{3,2},{4,5},{5,4},{6,7},{7,6},{8,9},{9,8},{10,11... | collective-permute-start | bytes 7077896 | tf_op jit(solution)/shard_map/ppermute | solution.py:608
  495.1 18.2 %copy-start.18 = (bf16[1024,768]{1,0:T(8,128)(2,1)S(1)}, bf16[1024,768]{1,0:T(8,128)(2,1)}, u32[]{:S(2)}) copy-start(bf16[1024,768]{1,0:T(8,128)(2,1)} %get-tuple-element.73) | copy-start | bytes 4718596
  495.1 18.2 %copy-start.19 = (bf16[1024,768]{1,0:T(8,128)(2,1)S(1)}, bf16[1024,768]{1,0:T(8,128)(2,1)}, u32[]{:S(2)}) copy-start(bf16[1024,768]{1,0:T(8,128)(2,1)} %get-tuple-element.78) | copy-start | bytes 4718596
  509.4 11.2 %all-to-all-start.6 = ((f32[32,1,256]{2,1,0:T(1,128)}), f32[32,1,256]{2,1,0:T(1,128)S(1)}, u32[]{:S(2)}, u32[]{:S(2)}) async-start(f32[32,1,256]{2,1,0:T(1,128)} %copy.185), calls=%async_computation.6 | async-start | bytes 65536 | tf_op jit(solution)/shard_map/all_to_all | solution.py:777
  520.6 81.2 %all-to-all-start.3 = ((bf16[32,64,768]{2,1,0:T(8,128)(2,1)}), bf16[32,64,768]{2,1,0:T(8,128)(2,1)S(1)}, u32[]{:S(2)}, u32[]{:S(2)}) async-start(bf16[32,64,768]{2,1,0:T(8,128)(2,1)} %bitcast.266), calls=%async_computation.3 | async-start | bytes 6291456 | tf_op jit(solution)/shard_map/all_to_all | solution.py:631
  529.4 38.9 %collective-permute-start.17 = (bf16[4,2,24,1536]{3,2,0,1:T(8,128)(2,1)S(1)}, bf16[4,2,24,1536]{3,2,0,1:T(8,128)(2,1)S(1)}, u32[]{:S(2)}, u32[]{:S(2)}) collective-permute-start(bf16[4,2,24,1536]{3,2,0,1:T(8,128)(2,1)S(1)} %pad_maximum_fusion.5), channel_id=1, source_target_pairs={{0,2},{1,3},{2,0},{3,1},{4,6},{5,7},{6,4},{7,5},{8,10},{9,11},{10,... | collective-permute-start | bytes 1769480 | tf_op jit(solution)/shard_map/ppermute | solution.py:597
  531.3 37.7 %collective-permute-start.19 = (bf16[4,2,24,1536]{3,2,0,1:T(8,128)(2,1)S(1)}, bf16[4,2,24,1536]{3,2,0,1:T(8,128)(2,1)S(1)}, u32[]{:S(2)}, u32[]{:S(2)}) collective-permute-start(bf16[4,2,24,1536]{3,2,0,1:T(8,128)(2,1)S(1)} %pad_maximum_fusion.6), channel_id=1, source_target_pairs={{0,4},{1,5},{2,6},{3,7},{4,0},{5,1},{6,2},{7,3},{8,12},{9,13},{10,... | collective-permute-start | bytes 1769480 | tf_op jit(solution)/shard_map/ppermute | solution.py:597
  568.5 10.5 %collective-permute-start.18 = (bf16[4,24,1536]{2,1,0:T(8,128)(2,1)S(1)}, bf16[4,24,1536]{2,1,0:T(8,128)(2,1)S(1)}, u32[]{:S(2)}, u32[]{:S(2)}) collective-permute-start(bf16[4,24,1536]{2,1,0:T(8,128)(2,1)S(1)} %pad_maximum_fusion.9), channel_id=1, source_target_pairs={{0,4},{1,5},{2,6},{3,7},{4,0},{5,1},{6,2},{7,3},{8,12},{9,13},{10,... | collective-permute-start | bytes 884744 | tf_op jit(solution)/shard_map/ppermute | solution.py:597
  569.2 9.9 %collective-permute-start.20 = (bf16[4,24,1536]{2,1,0:T(8,128)(2,1)S(1)}, bf16[4,24,1536]{2,1,0:T(8,128)(2,1)S(1)}, u32[]{:S(2)}, u32[]{:S(2)}) collective-permute-start(bf16[4,24,1536]{2,1,0:T(8,128)(2,1)S(1)} %pad_maximum_fusion.10), channel_id=1, source_target_pairs={{0,2},{1,3},{2,0},{3,1},{4,6},{5,7},{6,4},{7,5},{8,10},{9,11},{10,... | collective-permute-start | bytes 884744 | tf_op jit(solution)/shard_map/ppermute | solution.py:597
  580.1 31.5 %collective-permute-start.21 = (bf16[24,3072]{1,0:T(8,128)(2,1)}, bf16[24,3072]{1,0:T(8,128)(2,1)}, u32[]{:S(2)}, u32[]{:S(2)}) collective-permute-start(bf16[24,3072]{1,0:T(8,128)(2,1)} %pad_maximum_fusion.18), channel_id=1, source_target_pairs={{0,8},{1,9},{2,10},{3,11},{4,12},{5,13},{6,14},{7,15},{8,16},{9,17... | collective-permute-start | bytes 442376 | tf_op jit(solution)/shard_map/ppermute | solution.py:597
  584.1 27.5 %collective-permute-start.22 = (bf16[24,3072]{1,0:T(8,128)(2,1)}, bf16[24,3072]{1,0:T(8,128)(2,1)}, u32[]{:S(2)}, u32[]{:S(2)}) collective-permute-start(bf16[24,3072]{1,0:T(8,128)(2,1)} %pad_maximum_fusion.19), channel_id=1, source_target_pairs={{0,16},{1,17},{2,18},{3,19},{4,20},{5,21},{6,22},{7,23},{8,24},{9,... | collective-permute-start | bytes 442376 | tf_op jit(solution)/shard_map/ppermute | solution.py:597
  585.3 26.3 %collective-permute-start.23 = (bf16[24,3072]{1,0:T(8,128)(2,1)}, bf16[24,3072]{1,0:T(8,128)(2,1)}, u32[]{:S(2)}, u32[]{:S(2)}) collective-permute-start(bf16[24,3072]{1,0:T(8,128)(2,1)} %pad_maximum_fusion.20), channel_id=1, source_target_pairs={{0,24},{1,25},{2,26},{3,27},{4,28},{5,29},{6,30},{7,31},{8,0},{9,1... | collective-permute-start | bytes 442376 | tf_op jit(solution)/shard_map/ppermute | solution.py:597
  (33 other events, 200.8 us)

commit v4 on v3

--- a/solution.py
+++ b/solution.py
@@ -105,28 +105,33 @@
         lse_ref[:, rows] = jnp.transpose(total)[: lse_ref.shape[0], :]
 
 
-def attend(group, normed, weight, block, early_rows, seg_col, seg_row):
+def attend(normed, weights, early_rows, seg_col, seg_row):
     tokens, width = normed.shape
     wide = width // GROUPS
+    column = lambda rows, n: pl.BlockSpec((rows, n), lambda g: (0, g))
     return pl.pallas_call(
         attend_kernel,
-        grid=(1,),
+        grid=(GROUPS,),
         in_specs=[
             whole(normed.shape),
-            pl.BlockSpec((width, 3 * wide), lambda i: (0, block)),
-            pl.BlockSpec((8, wide), lambda i: (0, group)),
+            column(width, 3 * wide),
+            column(8, wide),
             whole(seg_col.shape),
             whole(seg_row.shape),
         ],
-        out_specs=(whole((tokens, 3 * wide)), whole((tokens, wide)), whole((8, tokens))),
+        out_specs=(
+            column(tokens, 3 * wide),
+            column(tokens, wide),
+            pl.BlockSpec((8, tokens), lambda g: (g, 0)),
+        ),
         out_shape=(
-            jax.ShapeDtypeStruct((tokens, 3 * wide), BF16),
-            jax.ShapeDtypeStruct((tokens, wide), BF16),
-            jax.ShapeDtypeStruct((8, tokens), F32),
+            jax.ShapeDtypeStruct((tokens, 3 * width), BF16),
+            jax.ShapeDtypeStruct((tokens, width), BF16),
+            jax.ShapeDtypeStruct((8 * GROUPS, tokens), F32),
         ),
         compiler_params=params(),
         name="attend",
-    )(normed, weight, early_rows, seg_col, seg_row)
+    )(normed, weights, early_rows, seg_col, seg_row)
 
 
 def halves(grad, part_ref, own_ref):
@@ -135,31 +140,7 @@
     own_ref[...] = grad[half:]
 
 
-def outer_kernel(turned_ref, grad_ref, part_ref, own_ref):
-    halves(dot(turned_ref[...], grad_ref[...]), part_ref, own_ref)
-
-
-def outer(turned, grad, blocks):
-    rows, _ = turned.shape
-    width = grad.shape[1]
-    return pl.pallas_call(
-        outer_kernel,
-        grid=(1,),
-        in_specs=[whole(turned.shape), whole(grad.shape)],
-        out_specs=(
-            pl.BlockSpec((rows // 2, width), lambda i: (0, blocks - 1)),
-            whole((rows // 2, width)),
-        ),
-        out_shape=(
-            jax.ShapeDtypeStruct((rows // 2, blocks * width), BF16),
-            jax.ShapeDtypeStruct((rows // 2, width), F32),
-        ),
-        compiler_params=params(),
-        name="outer",
-    )(turned, grad)
-
-
-def attend_back_kernel(
+def behind_kernel(
     qkv_ref,
     mix_ref,
     da_ref,
@@ -168,14 +149,62 @@
     sc_ref,
     sr_ref,
     turned_ref,
-    _,
-    out_ref,
+    mix_t_ref,
+    w_ref,
+    vec_ref,
+    x_hbm,
+    dhid_hbm,
     sum_ref,
     part_ref,
     own_ref,
+    grad_ref,
+    last_ref,
+    out_ref,
     do_ref,
     dk_ref,
     dv_ref,
+    acc_ref,
+    x_ref,
+    dhid_ref,
+    sems,
+):
+    step = pl.program_id(0)
+    copies = (
+        pltpu.make_async_copy(x_hbm, x_ref, sems.at[0]),
+        pltpu.make_async_copy(dhid_hbm, dhid_ref, sems.at[1]),
+    )
+
+    @pl.when(step == 0)
+    def _():
+        for copy in copies:
+            copy.start()
+        halves(dot(mix_t_ref[...], da_ref[...]), part_ref, own_ref)
+        acc_ref[...] = jnp.zeros_like(acc_ref)
+
+    @pl.when(step > 0)
+    def _():
+        attend_back(
+            qkv_ref, mix_ref, da_ref, wo_ref, lse_ref, sc_ref, sr_ref, out_ref, sum_ref, do_ref, dk_ref, dv_ref
+        )
+        halves(dot(turned_ref[...], out_ref[...]), part_ref, own_ref)
+        acc_ref[...] += dot_nt(out_ref[...], w_ref[...])
+
+    @pl.when(step == pl.num_programs(0) - 1)
+    def _():
+        for copy in copies:
+            copy.wait()
+        last_ref[...] = jnp.zeros_like(last_ref)
+        for r in range(0, x_ref.shape[0], QBLOCK):
+            rows = slice(r, r + QBLOCK)
+            grad = acc_ref[rows, :]
+            scaled, inverse = norm_stats(x_ref[rows, :].astype(F32))
+            grad_ref[rows, :] = dhid_ref[rows, :] + norm_back(grad, scaled, inverse, vec_ref[0:1, :])
+            last_ref[0:1, :] += jnp.sum(grad * scaled, axis=0, keepdims=True)
+            last_ref[1:2, :] += jnp.sum(grad, axis=0, keepdims=True)
+
+
+def attend_back(
+    qkv_ref, mix_ref, da_ref, wo_ref, lse_ref, sc_ref, sr_ref, out_ref, sum_ref, do_ref, dk_ref, dv_ref
 ):
     tokens = qkv_ref.shape[0]
     wide = mix_ref.shape[1]
@@ -227,68 +256,77 @@
     sum_ref[...] = jnp.broadcast_to(
         jnp.sum(out_ref[...].astype(F32), axis=0, keepdims=True), sum_ref.shape
     )
-    halves(dot(turned_ref[...], out_ref[...]), part_ref, own_ref)
-
-
-def attend_back(group, qkv, mix, dattn, weight, block, lse, seg_col, seg_row, turned, parts):
-    tokens, wide = mix.shape
-    width = dattn.shape[1]
+
+
+def behind(qkv, mix, dattn, weights, lse, seg_col, seg_row, turned, mix_t, vecs, x, dhid):
+    tokens, width = mix.shape
+    wide = width // GROUPS
+    steps = GROUPS + 1
+    group = lambda i: jnp.maximum(i - 1, 0)
+    column = lambda rows, n: pl.BlockSpec((rows, n), lambda i: (0, group(i)))
+    piece = pl.BlockSpec((width // 2, width), lambda i: (0, lax.rem(i + GROUPS, steps)))
+    hbm = pl.BlockSpec(memory_space=pl.ANY)
     return pl.pallas_call(
-        attend_back_kernel,
-        grid=(1,),
+        behind_kernel,
+        grid=(steps,),
         in_specs=[
-            whole(qkv.shape),
-            whole(mix.shape),
+            column(tokens, 3 * wide),
+            column(tokens, wide),
             whole(dattn.shape),
-            pl.BlockSpec((wide, width), lambda i: (group, block)),
-            whole(lse.shape),
+            pl.BlockSpec((wide, width), lambda i: (group(i), GROUPS)),
+            pl.BlockSpec((8, tokens), lambda i: (group(i), 0)),
             whole(seg_col.shape),
             whole(seg_row.shape),
             whole(turned.shape),
-            pl.BlockSpec(memory_space=pl.ANY),
+            whole(mix_t.shape),
+            column(width, 3 * wide),
+            whole(vecs.shape),
+            hbm,
+            hbm,
         ],
-        out_specs=(
-            whole((tokens, 3 * wide)),
-            whole((8, 3 * wide)),
-            pl.BlockSpec((width // 2, 3 * wide), lambda i: (0, group)),
-            whole((width // 2, 3 * wide)),
-        ),
-        input_output_aliases={8: 2},
+        out_specs=(column(8, 3 * wide), piece, piece, whole((tokens, width)), whole((8, width))),
         out_shape=(
-            jax.ShapeDtypeStruct((tokens, 3 * wide), BF16),
-            jax.ShapeDtypeStruct((8, 3 * wide), F32),
-            jax.ShapeDtypeStruct(parts.shape, BF16),
-            jax.ShapeDtypeStruct((width // 2, 3 * wide), F32),
+            jax.ShapeDtypeStruct((8, 3 * width), F32),
+            jax.ShapeDtypeStruct((width // 2, steps * width), BF16),
+            jax.ShapeDtypeStruct((width // 2, steps * width), F32),
+            jax.ShapeDtypeStruct((tokens, width), F32),
+            jax.ShapeDtypeStruct((8, width), F32),
         ),
         scratch_shapes=[
+            pltpu.VMEM((tokens, 3 * wide), BF16),
             pltpu.VMEM((tokens, wide), BF16),
             pltpu.VMEM((tokens, PAIR), F32),
             pltpu.VMEM((tokens, PAIR), F32),
+            pltpu.VMEM((tokens, width), F32),
+            pltpu.VMEM((tokens, width), x.dtype),
+            pltpu.VMEM((tokens, width), F32),
+            pltpu.SemaphoreType.DMA((2,)),
         ],
         compiler_params=params(),
-        name="attend_back",
-    )(qkv, mix, dattn, weight, lse, seg_col, seg_row, turned, parts)
-
-
-def project_kernel(x_ref, m0_ref, m1_ref, m2_ref, wo_ref, vec_ref, hid_ref, moe_ref):
-    wide = m0_ref.shape[1]
+        name="behind",
+    )(qkv, mix, dattn, weights, lse, seg_col, seg_row, turned, mix_t, weights, vecs, x, dhid)
+
+
+def project_kernel(x_ref, mix_ref, wo_ref, vec_ref, hid_ref, moe_ref):
     hidden = x_ref[...].astype(F32) + vec_ref[0:1, :]
-    for g, ref in enumerate((m0_ref, m1_ref, m2_ref)):
-        hidden = hidden + dot(ref[...], wo_ref[g * wide : (g + 1) * wide, :])
+    hidden = hidden + dot(mix_ref[...], wo_ref[...])
     hid_ref[...] = hidden
     scaled, _ = norm_stats(hidden)
     moe_ref[...] = (scaled * vec_ref[1:2, :] + vec_ref[2:3, :]).astype(BF16)
 
 
-def project(x, mixes, weight, block, vecs):
+def project(x, mix, weights, vecs):
     tokens, width = x.shape
-    wide = mixes[0].shape[1]
     row = lambda n: pl.BlockSpec((QBLOCK, n), lambda i: (i, 0))
     return pl.pallas_call(
         project_kernel,
         grid=(tokens // QBLOCK,),
-        in_specs=[row(width), row(wide), row(wide), row(wide)]
-        + [pl.BlockSpec((width, width), lambda i: (0, block)), whole(vecs.shape)],
+        in_specs=[
+            row(width),
+            row(width),
+            pl.BlockSpec((width, width), lambda i: (0, GROUPS)),
+            whole(vecs.shape),
+        ],
         out_specs=(row(width), row(width)),
         out_shape=(
             jax.ShapeDtypeStruct((tokens, width), F32),
@@ -296,7 +334,7 @@
         ),
         compiler_params=params(),
         name="project",
-    )(x, *mixes, weight, vecs)
+    )(x, mix, weights, vecs)
 
 
 def pack_kernel(base, target_ref, rows_ref, *refs):
@@ -373,62 +411,34 @@
     )(*slots, target_col, hidden, dy, vecs)
 
 
-def output_kernel(slots_ref, tgt_ref, route_ref, hid_ref, moe_ref, router_ref, out_ref):
+def output_kernel(capacity, slots_ref, tgt_ref, hid_ref, moe_ref, router_ref, out_ref):
     logits = dot(moe_ref[...], router_ref[...])
+    past = tgt_ref[...] - iota(logits.shape, 1) * capacity
     chosen = jnp.sum(
-        jnp.where(iota(logits.shape, 1) == route_ref[...], logits, 0.0), axis=1, keepdims=True
+        jnp.where((past >= 0) & (past < capacity), logits, 0.0), axis=1, keepdims=True
     )
     gate = jax.nn.sigmoid(chosen)
     out_ref[...] = (hid_ref[...] + gate * unpack_rows(tgt_ref[...], [slots_ref])).astype(BF16)
 
 
-def finish_output(slots, target_col, route_col, hidden, moe_in, weight, at, count):
+def finish_output(slots, capacity, target_col, hidden, moe_in, weights, at, count):
     tokens, width = hidden.shape
     row = lambda n: pl.BlockSpec((QBLOCK, n), lambda i: (i, 0))
     return pl.pallas_call(
-        output_kernel,
+        functools.partial(output_kernel, capacity),
         grid=(tokens // QBLOCK,),
-        in_specs=[whole(slots.shape), row(1), row(1), row(width), row(width)]
-        + [pl.BlockSpec((width, count), lambda i: (0, at // count))],
+        in_specs=[
+            whole(slots.shape),
+            row(1),
+            row(width),
+            row(width),
+            pl.BlockSpec((width, count), lambda i: (0, at // count)),
+        ],
         out_specs=row(width),
         out_shape=jax.ShapeDtypeStruct((tokens, width), BF16),
         compiler_params=params(),
-        name="finish_output",
-    )(slots, target_col, route_col, hidden, moe_in, weight)
-
-
-def last_kernel(d0_ref, d1_ref, d2_ref, w0_ref, w1_ref, w2_ref, x_ref, dhid_ref, vec_ref, out_ref, sum_ref):
-    grad = dot_nt(d0_ref[...], w0_ref[...])
-    grad = grad + dot_nt(d1_ref[...], w1_ref[...])
-    grad = grad + dot_nt(d2_ref[...], w2_ref[...])
-    scaled, inverse = norm_stats(x_ref[...].astype(F32))
-    out_ref[...] = dhid_ref[...] + norm_back(grad, scaled, inverse, vec_ref[0:1, :])
-
-    @pl.when(pl.program_id(0) == 0)
-    def _():
-        sum_ref[...] = jnp.zeros_like(sum_ref)
-
-    sum_ref[0:1, :] += jnp.sum(grad * scaled, axis=0, keepdims=True)
-    sum_ref[1:2, :] += jnp.sum(grad, axis=0, keepdims=True)
-
-
-def last(dqkvs, weights, blocks, x, dhid, vecs):
-    tokens, width = x.shape
-    row = lambda n: pl.BlockSpec((QBLOCK, n), lambda i: (i, 0))
-    return pl.pallas_call(
-        last_kernel,
-        grid=(tokens // QBLOCK,),
-        in_specs=[row(d.shape[1]) for d in dqkvs]
-        + [pl.BlockSpec((width, width), functools.partial(lambda b, i: (0, b), b)) for b in blocks]
-        + [row(width), row(width), whole(vecs.shape)],
-        out_specs=(row(width), whole((8, width))),
-        out_shape=(
-            jax.ShapeDtypeStruct((tokens, width), F32),
-            jax.ShapeDtypeStruct((8, width), F32),
-        ),
-        compiler_params=params(),
-        name="last",
-    )(*dqkvs, *weights, x, dhid, vecs)
+        name="finish",
+    )(slots, target_col, hidden, moe_in, weights)
 
 
 def expert_kernel(aliased, *refs):
@@ -603,15 +613,15 @@
     return totals
 
 
-def scatter_rows(parts, owns, split, devices):
+def scatter_rows(parts, own, devices):
     sizes = levels_of(devices)
     got = lax.ppermute(parts, "dp", cyclic(devices, sizes, 3, 1))
-    width = owns[0].shape[1]
-    shape = sizes[:3] + (owns[0].shape[0] * 2 // devices, width)
-    both = [
-        (own + got[:, n * width : (n + 1) * width].astype(F32)).reshape(shape) for n, own in enumerate(owns)
-    ]
-    first, second = both[:split], both[split:]
+    shape = sizes[:3] + (parts.shape[0] * 2 // devices,)
+    half = parts.shape[1] // 2
+    first, second = (
+        [(own[:, cut] + got[:, cut].astype(F32)).reshape(shape + (half,))]
+        for cut in (slice(0, half), slice(half, 2 * half))
+    )
     first = scatter_level(first, devices, sizes, 2, 2)
     second = scatter_level(second, devices, sizes, 1, 1)
     first = scatter_level(first, devices, sizes, 1, 1)
@@ -671,16 +681,12 @@
         [router_weight, out_bias[:, None], moe_gain[:, None], moe_shift[:, None]], axis=1
     ).astype(BF16)
     late = jnp.pad(late, ((0, 0), (0, -late.shape[1] % 128)))
-    full_early = gather_rows(jnp.concatenate([blocks[:, 0], early], axis=1), devices)
-    full_late = gather_rows(
-        jnp.concatenate([blocks[:, 1], blocks[:, 2], out_weight.astype(BF16), late], axis=1), devices
-    )
-    weights = (full_early, full_late, full_late)
-    places = (0, 0, 1)
-    out_place = 2
-    router_at, router_wide = 6 * wide + width, late.shape[1]
-    early_rows = full_early[:, 3 * wide : 3 * wide + 8].astype(F32).T
-    late_rows = full_late[:, router_at:].astype(F32).T
+    full = gather_rows(
+        jnp.concatenate([blocks.reshape(rows, 3 * width), out_weight.astype(BF16), late, early], axis=1), devices
+    )
+    router_at, router_wide = 4 * width, late.shape[1]
+    early_rows = full[:, router_at + router_wide :][:, :8].astype(F32).T
+    late_rows = full[:, router_at : router_at + router_wide].astype(F32).T
     vecs = jnp.pad(late_rows[experts : experts + 3], ((0, 5), (0, 0)))
     router_row = lax.dynamic_index_in_dim(late_rows, lax.axis_index("dp"), 0, keepdims=True)
 
@@ -699,8 +705,7 @@
         return chunk * (chunk_rows - per_chunk) + route * per_chunk + slot, route * capacity + slot
 
     target_row, entire_row = places_of(route[None, :], slot[None, :])
-    route_col = route[:, None]
-    target_col, entire_col = places_of(route_col, slot[:, None])
+    target_col, entire_col = places_of(route[:, None], slot[:, None])
 
     slots = CHUNKS * chunk_rows
     dy_slots = ()
@@ -717,13 +722,8 @@
     seg_col = segments.reshape(tokens, 1)
     scaled, _ = norm_stats(x.astype(F32))
     normed = (scaled * early_rows[0:1] + early_rows[1:2]).astype(BF16)
-    qkvs, mixes, lses = [], [], []
-    for g in range(GROUPS):
-        qkv, mix, lse = attend(g, normed, weights[g], places[g], early_rows, seg_col, seg_row)
-        qkvs.append(qkv)
-        mixes.append(mix)
-        lses.append(lse)
-    hidden, moe_in = project(x, mixes, full_late, out_place, vecs)
+    qkv, mix, lse = attend(normed, full, early_rows, seg_col, seg_row)
+    hidden, moe_in = project(x, mix, full, vecs)
 
     expert_vecs = jnp.concatenate([expert_out_bias, router_row, jnp.zeros((6, width), F32)], axis=0)
     returned, dmoes, kept = [], [], ()
@@ -732,10 +732,10 @@
         exchange(pack(moe_in, target_row, c * chunk_rows, chunk_rows, chunk_rows), experts)
         for c in range(CHUNKS)
     ]
-    mix_t = other_first(jnp.concatenate(mixes, axis=1).T, devices)
+    mix_t = other_first(mix.T, devices)
     normed_t = other_first(normed.T, devices)
-    received[0], target_col, entire_col, route_col, mix_t, normed_t = lax.optimization_barrier(
-        (received[0], target_col, entire_col, route_col, mix_t, normed_t)
+    received[0], target_col, entire_col, mix_t, normed_t = lax.optimization_barrier(
+        (received[0], target_col, entire_col, mix_t, normed_t)
     )
     for c in range(CHUNKS):
         ret, dmoe, *kept, dbias, sums = expert_chunk(
@@ -743,7 +743,7 @@
         )
         dmoes.append(exchange(dmoe, experts))
         returned.append(ret)
-        dbias_in = dbias_in + dbias
+        dbias_in = dbias_in + dbias[0:1]
         dsums = dsums + sums
     act, dpre, arrived, rows_in = kept
     grad_expert_out = dot_tn(act, arrived)
@@ -752,32 +752,24 @@
     returned = exchange(returned.reshape(slots, width), experts)
 
     dhid, dattn, mid_sums = middle(dmoes, target_col, hidden, dy, vecs)
-    parts, own_out = outer(mix_t, dattn, GROUPS + 1)
-    dqkvs, qkv_sums, owns = [], [], []
-    for g in range(GROUPS):
-        dqkv, col_sums, parts, own = attend_back(
-            g, qkvs[g], mixes[g], dattn, full_late, out_place, lses[g], seg_col, seg_row, normed_t, parts
-        )
-        dqkvs.append(dqkv)
-        qkv_sums.append(col_sums[0:1])
-        owns.append(own)
-    *grad_qkv, grad_out = scatter_rows(parts, owns + [own_out], 2, devices)
-    grad_inputs, last_sums = last(dqkvs, weights, places, x, dhid, early_rows)
+    qkv_sums, parts, own, grad_inputs, last_sums = behind(
+        qkv, mix, dattn, full, lse, seg_col, seg_row, normed_t, mix_t, early_rows, x, dhid
+    )
+    grads = jnp.concatenate(scatter_rows(parts, own, devices), axis=1)
+    grad_qkv, grad_out = grads[:, : 3 * width], grads[:, 3 * width :]
     output = finish_output(
-        returned, entire_col, route_col, hidden, moe_in, full_late, router_at, router_wide
-    )
-
-    grad_query = jnp.concatenate([s[:, :wide] for s in qkv_sums], axis=1)
-    grad_value = jnp.concatenate([s[:, 2 * wide :] for s in qkv_sums], axis=1)
-    small = jnp.concatenate(
-        [grad_query, grad_value, mid_sums[0:3], last_sums[0:2], dsums[0:1]], axis=0
-    )
+        returned, capacity, entire_col, hidden, moe_in, full, router_at, router_wide
+    )
+
+    qkv_sums = qkv_sums[0].reshape(GROUPS, 3, wide)
+    grad_query, grad_value = qkv_sums[:, 0].reshape(1, width), qkv_sums[:, 2].reshape(1, width)
+    small = jnp.concatenate([grad_query, grad_value, mid_sums[0:3], last_sums[0:2], dsums[0:1]], axis=0)
     small = small.reshape(8, devices, rows).transpose(1, 0, 2).reshape(devices, 8 * rows)
     small = jnp.pad(small, ((0, 0), (0, -small.shape[1] % 128)))
     small = lax.all_to_all(small, "dp", split_axis=0, concat_axis=0, tiled=True)
     vectors = jnp.sum(small[:, : 7 * rows], axis=0).reshape(7, rows)
     grad_router = small[:, 7 * rows : 8 * rows].T
-    grad_qkv = jnp.stack([g.reshape(rows, 3, wide) for g in grad_qkv], axis=2).reshape(rows, 3 * width)
+    grad_qkv = grad_qkv.reshape(rows, GROUPS, 3, wide).transpose(0, 2, 1, 3).reshape(rows, 3 * width)
     return (
         output.reshape(seq_count, tokens, width),
         grad_inputs.reshape(seq_count, tokens, width),
@@ -792,7 +784,7 @@
         vectors[4],
         grad_router,
         grad_expert_in[None],
-        dbias_in[0:1],
+        dbias_in,
         grad_expert_out[None],
         dsums[1:2],
     )

time: 626 us -> 503 us (0.80); the launches traced: 615 us -> 498 us
  waiting for transfers between devices: 203 us -> 149 us
  blocking collectives: 44 us -> 0 us
  Pallas kernels: 197 us -> 175 us
    all_to_all x5 -> x6, waiting for transfers between devices: 130 us -> 85.7 us  [exchange(): lax.all_to_all(slots.reshape(experts, rows // experts, width), 'dp', spli...]
    all_to_all x1 -> x0, blocking collectives: 44 us -> none  [exchange(): lax.all_to_all(slots.reshape(experts, rows // experts, width), 'dp', spli...]
    pallas_call x9 -> x3, Pallas kernels: 102 us -> 80.5 us  [the longest x1 46.1 us: behind(): pl.pallas_call(behind_kernel, grid=(steps,), in_specs=[column(tokens, 3 *...]
    all_to_all x5 -> x6, starting transfers between devices: 17.2 us -> 26.7 us  [exchange(): lax.all_to_all(slots.reshape(experts, rows // experts, width), 'dp', spli...]
    ppermute x16 -> x8, starting transfers between devices: 19.5 us -> 12.6 us  [shifted(): parts.append(lax.ppermute(block, 'dp', cyclic(devices, sizes, axis, shift)))]
    ppermute x16 -> x8, waiting for transfers between devices: 23.6 us -> 19.6 us  [shifted(): parts.append(lax.ppermute(block, 'dp', cyclic(devices, sizes, axis, shift)))]
  transfers between devices with their start and end apart: 30 -> 23, of which waited for: 14 -> 13; matrix products, arithmetic and copies ran while one was open for 16% -> 20% of each run, Pallas kernels for 12% -> 24%
where the time goes in v4:
time: 503 us; the launch traced here: 498 us
  Pallas kernels  175 us (35%)
  waiting for transfers between devices  149 us (30%)
  starting transfers between devices  53.5 us (11%)
  other arithmetic  50.2 us (10%)
  local copies, waits for them, and re-layouts  36.4 us (7%)
  matrix products  32 us (6%)
    all_to_all x6, waiting for transfers between devices, exchange(): lax.all_to_all(slots.reshape(experts, rows // experts, width), 'dp', spli...  85.7 us
    pallas_call x2, Pallas kernels, expert_chunk(): pl.pallas_call(functools.partial(expert_kernel, aliased), grid=(hidden //...  62.1 us
    pallas_call x1, Pallas kernels, behind(): pl.pallas_call(behind_kernel, grid=(steps,), in_specs=[column(tokens, 3 *...  46.1 us
    ppermute x7, waiting for transfers between devices, scatter_level(): got = lax.ppermute(part, 'dp', cyclic(devices, sizes, axis, shift))  38.9 us
    dot_general x2, matrix products, dot_tn(): lax.dot_general(a, b, (((0,), (0,)), ((), ())), preferred_element_type=F32)  31.5 us
    all_to_all x6, starting transfers between devices, exchange(): lax.all_to_all(slots.reshape(experts, rows // experts, width), 'dp', spli...  26.7 us
    pallas_call x1, Pallas kernels, attend(): pl.pallas_call(attend_kernel, grid=(GROUPS,), in_specs=[whole(normed.shap...  26.1 us
    ppermute x8, waiting for transfers between devices, shifted(): parts.append(lax.ppermute(block, 'dp', cyclic(devices, sizes, axis, shift)))  19.6 us
  transfers between devices with their start and end apart: 23, of which 13 were waited for; matrix products, arithmetic and copies ran while one was open for 20% of the time, Pallas kernels for 24%

profile of v4, /device:TPU:0, one launch (start us, length us, event | category | flops | bytes accessed | tf_op | source)
XLA Modules:
  0.0 498.4 jit_solution(7124208624955423059)
XLA Ops:
  17.5 6.0 %collective-permute-done.1 = bf16[24,3328]{1,0:T(8,128)(2,1)S(1)} collective-permute-done((bf16[24,3328]{1,0:T(8,128)(2,1)S(1)}, bf16[24,3328]{1,0:T(8,128)(2,1)S(1)}, u32[]{:S(2)}, u32[]{:S(2)}) %collective-permute-start.1) | collective-permute-done | bytes 159776 | tf_op jit(solution)/shard_map/ppermute | solution.py:562
  27.0 6.4 %collective-permute-done.3 = bf16[4,24,1664]{2,1,0:T(8,128)(2,1)S(1)} collective-permute-done((bf16[4,24,1664]{2,1,0:T(8,128)(2,1)S(1)}, bf16[4,24,1664]{2,1,0:T(8,128)(2,1)S(1)}, u32[]{:S(2)}, u32[]{:S(2)}) %collective-permute-start.3) | collective-permute-done | bytes 319520 | tf_op jit(solution)/shard_map/ppermute | solution.py:562
  38.9 4.3 pack.5.refs_0_
  43.2 4.3 pack.6
  47.5 5.9 %all-to-all-start.1 = ((bf16[32,64,768]{2,1,0:T(8,128)(2,1)}), bf16[32,64,768]{2,1,0:T(8,128)(2,1)}, u32[]{:S(2)}, u32[]{:S(2)}) async-start(bf16[32,64,768]{2,1,0:T(8,128)(2,1)} %bitcast.180), calls=%async_computation.1 | async-start | bytes 6291456 | tf_op jit(solution)/shard_map/all_to_all | solution.py:641
  69.9 26.1 %attend.1 = (bf16[1024,2304]{1,0:T(8,128)(2,1)}, bf16[1024,768]{1,0:T(8,128)(2,1)}, f32[24,1024]{1,0:T(8,128)}) custom-call(bf16[1024,768]{1,0:T(8,128)(2,1)} %fusion.6.x_ref, bf16[768,3328]{1,0:T(8,128)(2,1)} %bitcast.173, f32[8,768]{1,0:T(8,128)} %copy-done.19, s32[1024,1]{1,0:T(8,128)} %copy.136.sc_ref, s32[1,1024]{1,0:T(1,128)} %sr_ref.3), custom_call_target="tpu_custom_call" | custom-call | tf_op jit(solution)/shard_map/attend/pallas_call | solution.py:112
  96.1 5.9 %project.1 = (f32[1024,768]{1,0:T(8,128)}, bf16[1024,768]{1,0:T(8,128)(2,1)}) custom-call(bf16[1024,768]{1,0:T(8,128)(2,1)} %bitcast.178, bf16[1024,768]{1,0:T(8,128)(2,1)} %get-tuple-element.50.mix_ref, bf16[768,3328]{1,0:T(8,128)(2,1)} %bitcast.174, f32[8,768]{1,0:T(8,128)} %pad.18.vec_ref.refs_5_), custom_call_target="tpu_custom_call" | custom-call | tf_op jit(solution)/shard_map/project/pallas_call | solution.py:321
  102.0 4.3 pack.4
  106.3 18.4 %all-to-all-done.1 = bf16[32,64,768]{2,1,0:T(8,128)(2,1)} async-done(((bf16[32,64,768]{2,1,0:T(8,128)(2,1)}), bf16[32,64,768]{2,1,0:T(8,128)(2,1)}, u32[]{:S(2)}, u32[]{:S(2)}) %all-to-all-start.1) | async-done | bytes 3145760 | tf_op jit(solution)/shard_map/all_to_all | solution.py:641
  124.7 4.2 all-to-all-start
  129.0 6.6 %convert_bitcast_fusion.1.refs_2_ = bf16[768,3072]{1,0:T(8,128)(2,1)} fusion(f32[1,768,3072]{2,1,0:T(8,128)} %param.32), kind=kLoop, calls=%fused_computation.4 | loop fusion | flops 2359296 | bytes 14155776 | tf_op jit(solution)/shard_map/convert_element_type | solution.py:718
  135.6 4.3 pack.7
  139.8 26.7 %all-to-all-done = bf16[32,32,768]{2,1,0:T(8,128)(2,1)S(1)} async-done(((bf16[32,32,768]{2,1,0:T(8,128)(2,1)}), bf16[32,32,768]{2,1,0:T(8,128)(2,1)S(1)}, u32[]{:S(2)}, u32[]{:S(2)}) %all-to-all-start) | async-done | bytes 1572896 | tf_op jit(solution)/shard_map/all_to_all | solution.py:641
  166.6 3.8 all-to-all-start.2
  179.8 6.3 %convert_bitcast_fusion.refs_4_ = bf16[3072,768]{1,0:T(8,128)(2,1)} fusion(f32[1,3072,768]{2,1,0:T(8,128)} %param.34), kind=kLoop, calls=%fused_computation.3 | loop fusion | flops 2359296 | bytes 14155776 | tf_op jit(solution)/shard_map/convert_element_type | solution.py:719
  201.3 31.0 %expert.2 = (bf16[1024,768]{1,0:T(8,128)(2,1)}, bf16[1024,768]{1,0:T(8,128)(2,1)}, bf16[2048,3072]{1,0:T(8,128)(2,1)}, bf16[2048,3072]{1,0:T(8,128)(2,1)}, bf16[...) custom-call(bf16[1024,768]{1,0:T(8,128)(2,1)} %bitcast.201, ...), custom_call_target="tpu_custom_call" | custom-call | tf_op jit(solution)/shard_map/expert/pallas_call | solution.py:497
  232.3 6.2 %all-to-all-start.4 = ((bf16[32,32,768]{2,1,0:T(8,128)(2,1)}), bf16[32,32,768]{2,1,0:T(8,128)(2,1)S(1)}, u32[]{:S(2)}, u32[]{:S(2)}) async-start(bf16[32,32,768]{2,1,0:T(8,128)(2,1)} %bitcast.205), calls=%async_computation.4 | async-start | bytes 3145728 | tf_op jit(solution)/shard_map/all_to_all | solution.py:641
  238.6 31.1 %expert.3 = (bf16[1024,768]{1,0:T(8,128)(2,1)}, bf16[1024,768]{1,0:T(8,128)(2,1)}, bf16[2048,3072]{1,0:T(8,128)(2,1)}, bf16[2048,3072]{1,0:T(8,128)(2,1)}, bf16[...) custom-call(bf16[1024,768]{1,0:T(8,128)(2,1)} %bitcast.191, ...), custom_call_target="tpu_custom_call", output_to_operand_aliasing={{2}: (6, {}), {3}: (7, {}), {4}: (8, {}), {5}: (9, {})} | custom-call | tf_op jit(solution)/shard_map/expert/pallas_call | solution.py:497
  269.7 6.5 %all-to-all-done.4 = bf16[32,32,768]{2,1,0:T(8,128)(2,1)S(1)} async-done(((bf16[32,32,768]{2,1,0:T(8,128)(2,1)}), bf16[32,32,768]{2,1,0:T(8,128)(2,1)S(1)}, u32[]{:S(2)}, u32[]{:S(2)}) %all-to-all-start.4) | async-done | bytes 1572896 | tf_op jit(solution)/shard_map/all_to_all | solution.py:641
  280.8 16.1 %convolution_bitcast_fusion.1 = f32[1,768,3072]{2,1,0:T(8,128)} fusion(bf16[2048,768]{1,0:T(8,128)(2,1)} %get-tuple-element.78, bf16[2048,3072]{1,0:T(8,128)(2,1)} %get-tuple-element.79), kind=kOutput, calls=%fused_computation.1 | convolution fusion | flops 9663676416 | bytes 25165824 | tf_op jit(solution)/shard_map/dot_general | solution.py:35
  296.9 20.8 %all-to-all-done.5 = bf16[32,32,768]{2,1,0:T(8,128)(2,1)S(1)} async-done(((bf16[32,32,768]{2,1,0:T(8,128)(2,1)}), bf16[32,32,768]{2,1,0:T(8,128)(2,1)S(1)}, u32[]{:S(2)}, u32[]{:S(2)}) %all-to-all-start.5) | async-done | bytes 1572896 | tf_op jit(solution)/shard_map/all_to_all | solution.py:641
  318.8 9.6 %middle.1 = (f32[1024,768]{1,0:T(8,128)}, bf16[1024,768]{1,0:T(8,128)(2,1)}, f32[8,768]{1,0:T(8,128)}) custom-call(bf16[1024,768]{1,0:T(8,128)(2,1)} %bitcast.195, bf16[1024,768]{1,0:T(8,128)(2,1)} %bitcast.197, s32[1024,1]{1,0:T(8,128)} %get-tuple-element.64.refs_2_, f32[1024,768]{1,0:T(8,128)} %get-tuple-element.60.hid_ref.refs_3_, ...), custom_call_target="tpu_custom_call" | custom-call | tf_op jit(solution)/shard_map/middle/pallas_call | solution.py:399
  328.4 46.1 %behind.1 = (f32[8,2304]{1,0:T(8,128)}, bf16[384,3072]{1,0:T(8,128)(2,1)}, f32[384,3072]{1,0:T(8,128)}, f32[1024,768]{1,0:T(8,128)}, f32[8,768]{1,0:T(8,128)}) custom-call(bf16[1024,2304]{1,0:T(8,128)(2,1)} %get-tuple-element.61.qkv_ref, bf16[1024,768]{1,0:T(8,128)(2,1)} %get-tuple-element.50.mix_ref, bf16[1024,768]{1,0:T(8,128)(2,1)} %get-tuple-element.65.da_ref, ...), custom_call_target="tpu_custom_call" | custom-call | tf_op jit(solution)/shard_map/behind/pallas_call | solution.py:269
  374.7 15.4 %convolution_bitcast_fusion = f32[1,3072,768]{2,1,0:T(8,128)} fusion(bf16[2048,3072]{1,0:T(8,128)(2,1)} %get-tuple-element.82, bf16[2048,768]{1,0:T(8,128)(2,1)S(1)} %copy-done.14), kind=kOutput, calls=%fused_computation | convolution fusion | flops 9663676416 | bytes 25165824 | tf_op jit(solution)/shard_map/dot_general | solution.py:35
  393.1 3.9 all-to-all-start.6
  399.3 5.0 %all-to-all-done.6 = f32[32,1,256]{2,1,0:T(1,128)S(1)} async-done(((f32[32,1,256]{2,1,0:T(1,128)}), f32[32,1,256]{2,1,0:T(1,128)S(1)}, u32[]{:S(2)}, u32[]{:S(2)}) %all-to-all-start.6) | async-done | bytes 32800 | tf_op jit(solution)/shard_map/all_to_all | solution.py:769
  407.1 5.1 %convert_add_fusion.1 = (f32[384,1536]{1,0:T(8,128)S(1)}, f32[384,1536]{1,0:T(8,128)}) fusion(f32[384,3072]{1,0:T(8,128)} %get-tuple-element.71, bf16[384,3072]{1,0:T(8,128)(2,1)} %collective-permute-done.8), kind=kLoop, calls=%fused_computation.20 | loop fusion | flops 2359296 | bytes 11796480 | tf_op jit(solution)/shard_map/add | solution.py:622
  421.4 30.6 %collective-permute-done.9 = bf16[4,2,24,1536]{3,2,0,1:T(8,128)(2,1)} collective-permute-done((bf16[4,2,24,1536]{3,2,0,1:T(8,128)(2,1)}, bf16[4,2,24,1536]{3,2,0,1:T(8,128)(2,1)}, u32[]{:S(2)}, u32[]{:S(2)}) %collective-permute-start.9) | collective-permute-done | bytes 589856 | tf_op jit(solution)/shard_map/ppermute | solution.py:607
  456.1 8.3 %collective-permute-done.10 = bf16[4,24,1536]{2,1,0:T(8,128)(2,1)S(1)} collective-permute-done((bf16[4,24,1536]{2,1,0:T(8,128)(2,1)S(1)}, bf16[4,24,1536]{2,1,0:T(8,128)(2,1)S(1)}, u32[]{:S(2)}, u32[]{:S(2)}) %collective-permute-start.10) | collective-permute-done | bytes 294944 | tf_op jit(solution)/shard_map/ppermute | solution.py:607
  466.4 4.5 collective-permute-start.15
  472.2 13.3 %all-to-all-done.3 = bf16[32,64,768]{2,1,0:T(8,128)(2,1)S(1)} async-done(((bf16[32,64,768]{2,1,0:T(8,128)(2,1)}), bf16[32,64,768]{2,1,0:T(8,128)(2,1)S(1)}, u32[]{:S(2)}, u32[]{:S(2)}) %all-to-all-start.3) | async-done | bytes 3145760 | tf_op jit(solution)/shard_map/all_to_all | solution.py:641
  487.1 8.2 %finish.1 = bf16[1024,768]{1,0:T(8,128)(2,1)} custom-call(bf16[2048,768]{1,0:T(8,128)(2,1)} %bitcast.185, s32[1024,1]{1,0:T(8,128)} %get-tuple-element.59.tgt_ref, f32[1024,768]{1,0:T(8,128)} %get-tuple-element.60.hid_ref.refs_3_, bf16[1024,768]{1,0:T(8,128)(2,1)} %get-tuple-element.51.rows_ref.moe_ref, bf16[768,3328]{1,0:T(8,128)(2,1)} %bitcast.177), custom_call_target="tpu_custom_call" | custom-call | tf_op jit(solution)/shard_map/finish/pallas_call | solution.py:427
  (202 shorter events, 101.4 us)
Async XLA Ops:
  7.3 10.2 %collective-permute-start.2 = (bf16[24,3328]{1,0:T(8,128)(2,1)S(1)}, bf16[24,3328]{1,0:T(8,128)(2,1)S(1)}, u32[]{:S(2)}, u32[]{:S(2)}) collective-permute-start(bf16[24,3328]{1,0:T(8,128)(2,1)S(1)} %fusion.14), channel_id=1, source_target_pairs={{0,8},{1,9},{2,10},{3,11},{4,12},{5,13},{6,14},{7,15},{8,16},{9,17... | collective-permute-start | bytes 479240 | tf_op jit(solution)/shard_map/ppermute | solution.py:562
  10.4 13.1 %collective-permute-start.1 = (bf16[24,3328]{1,0:T(8,128)(2,1)S(1)}, bf16[24,3328]{1,0:T(8,128)(2,1)S(1)}, u32[]{:S(2)}, u32[]{:S(2)}) collective-permute-start(bf16[24,3328]{1,0:T(8,128)(2,1)S(1)} %fusion.14), channel_id=1, source_target_pairs={{0,16},{1,17},{2,18},{3,19},{4,20},{5,21},{6,22},{7,23},{8,24},{9,... | collective-permute-start | bytes 479240 | tf_op jit(solution)/shard_map/ppermute | solution.py:562
  13.0 10.5 %collective-permute-start = (bf16[24,3328]{1,0:T(8,128)(2,1)S(1)}, bf16[24,3328]{1,0:T(8,128)(2,1)S(1)}, u32[]{:S(2)}, u32[]{:S(2)}) collective-permute-start(bf16[24,3328]{1,0:T(8,128)(2,1)S(1)} %fusion.14), channel_id=1, source_target_pairs={{0,24},{1,25},{2,26},{3,27},{4,28},{5,29},{6,30},{7,31},{8,0},{9,1... | collective-permute-start | bytes 479240 | tf_op jit(solution)/shard_map/ppermute | solution.py:562
  23.8 11.5 %copy-start.24 = (s32[1,1024,1]{1,2,0:T(1,128)S(1)}, s32[1,1024,1]{1,2,0:T(1,128)}, u32[]{:S(2)}) copy-start(s32[1,1024,1]{1,2,0:T(1,128)} %param.20) | copy-start | bytes 12292
  23.9 9.4 %collective-permute-start.3 = (bf16[4,24,1664]{2,1,0:T(8,128)(2,1)S(1)}, bf16[4,24,1664]{2,1,0:T(8,128)(2,1)S(1)}, u32[]{:S(2)}, u32[]{:S(2)}) collective-permute-start(bf16[4,24,1664]{2,1,0:T(8,128)(2,1)S(1)} %get-tuple-element.138), channel_id=1, source_target_pairs={{0,4},{1,5},{2,6},{3,7},{4,0},{5,1},{6,2},{7,3},{8,12},{9,13},{10,... | collective-permute-start | bytes 958472 | tf_op jit(solution)/shard_map/ppermute | solution.py:562
  25.5 9.1 %collective-permute-start.5 = (bf16[4,24,1664]{2,1,0:T(8,128)(2,1)S(1)}, bf16[4,24,1664]{2,1,0:T(8,128)(2,1)S(1)}, u32[]{:S(2)}, u32[]{:S(2)}) collective-permute-start(bf16[4,24,1664]{2,1,0:T(8,128)(2,1)S(1)} %get-tuple-element.139), channel_id=1, source_target_pairs={{0,2},{1,3},{2,0},{3,1},{4,6},{5,7},{6,4},{7,5},{8,10},{9,11},{10,... | collective-permute-start | bytes 958472 | tf_op jit(solution)/shard_map/ppermute | solution.py:562
  34.8 18.6 %collective-permute-start.6 = (bf16[4,2,24,1664]{3,2,0,1:T(8,128)(2,1)S(1)}, bf16[4,2,24,1664]{3,2,0,1:T(8,128)(2,1)}, u32[]{:S(2)}, u32[]{:S(2)}) collective-permute-start(bf16[4,2,24,1664]{3,2,0,1:T(8,128)(2,1)S(1)} %pad_maximum_fusion.6), channel_id=1, source_target_pairs={{0,4},{1,5},{2,6},{3,7},{4,0},{5,1},{6,2},{7,3},{8,12},{9,13},{10,... | collective-permute-start | bytes 1916936 | tf_op jit(solution)/shard_map/ppermute | solution.py:562
  36.8 17.8 %collective-permute-start.4 = (bf16[4,2,24,1664]{3,2,0,1:T(8,128)(2,1)}, bf16[4,2,24,1664]{3,2,0,1:T(8,128)(2,1)S(1)}, u32[]{:S(2)}, u32[]{:S(2)}) collective-permute-start(bf16[4,2,24,1664]{3,2,0,1:T(8,128)(2,1)} %pad_maximum_fusion.5), channel_id=1, source_target_pairs={{0,2},{1,3},{2,0},{3,1},{4,6},{5,7},{6,4},{7,5},{8,10},{9,11},{10,... | collective-permute-start | bytes 1916936 | tf_op jit(solution)/shard_map/ppermute | solution.py:562
  47.5 77.2 %all-to-all-start.1 = ((bf16[32,64,768]{2,1,0:T(8,128)(2,1)}), bf16[32,64,768]{2,1,0:T(8,128)(2,1)}, u32[]{:S(2)}, u32[]{:S(2)}) async-start(bf16[32,64,768]{2,1,0:T(8,128)(2,1)} %bitcast.180), calls=%async_computation.1 | async-start | bytes 6291456 | tf_op jit(solution)/shard_map/all_to_all | solution.py:641
  56.5 5.2 %collective-permute-start.7 = (bf16[4,2,2,24,3328]{4,3,0,2,1:T(8,128)(2,1)}, bf16[4,2,2,24,3328]{4,3,0,2,1:T(8,128)(2,1)}, u32[]{:S(2)}, u32[]{:S(2)}) collective-permute-start(bf16[4,2,2,24,3328]{4,3,0,2,1:T(8,128)(2,1)} %maximum_maximum_fusion), channel_id=1, source_target_pairs={{0,1},{1,0},{2,3},{3,2},{4,5},{5,4},{6,7},{7,6},{8,9},{9,8},{10,11... | collective-permute-start | bytes 7667720 | tf_op jit(solution)/shard_map/ppermute | solution.py:562
  124.7 41.8 %all-to-all-start = ((bf16[32,32,768]{2,1,0:T(8,128)(2,1)}), bf16[32,32,768]{2,1,0:T(8,128)(2,1)S(1)}, u32[]{:S(2)}, u32[]{:S(2)}) async-start(bf16[32,32,768]{2,1,0:T(8,128)(2,1)} %bitcast.198), calls=%async_computation | async-start | bytes 3145728 | tf_op jit(solution)/shard_map/all_to_all | solution.py:641
  166.6 13.3 %copy-start.11 = (bf16[32,32,768]{2,1,0:T(8,128)(2,1)}, bf16[32,32,768]{2,1,0:T(8,128)(2,1)S(1)}, u32[]{:S(2)}) copy-start(bf16[32,32,768]{2,1,0:T(8,128)(2,1)S(1)} %all-to-all-done) | copy-start | bytes 4718596
  166.6 65.7 %all-to-all-start.2 = ((bf16[32,32,768]{2,1,0:T(8,128)(2,1)}), bf16[32,32,768]{2,1,0:T(8,128)(2,1)S(1)}, u32[]{:S(2)}, u32[]{:S(2)}) async-start(bf16[32,32,768]{2,1,0:T(8,128)(2,1)} %bitcast.196), calls=%async_computation.2 | async-start | bytes 3145728 | tf_op jit(solution)/shard_map/all_to_all | solution.py:641
  232.3 43.9 %all-to-all-start.4 = ((bf16[32,32,768]{2,1,0:T(8,128)(2,1)}), bf16[32,32,768]{2,1,0:T(8,128)(2,1)S(1)}, u32[]{:S(2)}, u32[]{:S(2)}) async-start(bf16[32,32,768]{2,1,0:T(8,128)(2,1)} %bitcast.205), calls=%async_computation.4 | async-start | bytes 3145728 | tf_op jit(solution)/shard_map/all_to_all | solution.py:641
  269.7 10.4 %copy-start.22 = (f32[8,768]{1,0:T(8,128)S(1)}, f32[8,768]{1,0:T(8,128)}, u32[]{:S(2)}) copy-start(f32[8,768]{1,0:T(8,128)} %get-tuple-element.76) | copy-start | bytes 73732
  276.2 20.7 %copy-start.8 = (bf16[32,32,768]{2,1,0:T(8,128)(2,1)}, bf16[32,32,768]{2,1,0:T(8,128)(2,1)S(1)}, u32[]{:S(2)}) copy-start(bf16[32,32,768]{2,1,0:T(8,128)(2,1)S(1)} %all-to-all-done.4) | copy-start | bytes 4718596
  276.2 41.5 %all-to-all-start.5 = ((bf16[32,32,768]{2,1,0:T(8,128)(2,1)}), bf16[32,32,768]{2,1,0:T(8,128)(2,1)S(1)}, u32[]{:S(2)}, u32[]{:S(2)}) async-start(bf16[32,32,768]{2,1,0:T(8,128)(2,1)} %bitcast.204), calls=%async_computation.5 | async-start | bytes 3145728 | tf_op jit(solution)/shard_map/all_to_all | solution.py:641
  328.4 46.2 %copy-start.14 = (bf16[2048,768]{1,0:T(8,128)(2,1)S(1)}, bf16[2048,768]{1,0:T(8,128)(2,1)}, u32[]{:S(2)}) copy-start(bf16[2048,768]{1,0:T(8,128)(2,1)} %get-tuple-element.83) | copy-start | bytes 9437188
  374.6 32.5 %collective-permute-start.8 = (bf16[384,3072]{1,0:T(8,128)(2,1)}, bf16[384,3072]{1,0:T(8,128)(2,1)}, u32[]{:S(2)}, u32[]{:S(2)}) collective-permute-start(bf16[384,3072]{1,0:T(8,128)(2,1)} %get-tuple-element.72), channel_id=1, source_target_pairs={{0,1},{1,0},{2,3},{3,2},{4,5},{5,4},{6,7},{7,6},{8,9},{9,8},{10,11... | collective-permute-start | bytes 7077896 | tf_op jit(solution)/shard_map/ppermute | solution.py:618
  374.7 17.3 %copy-start.25 = (f32[8,768]{1,0:T(8,128)S(1)}, f32[8,768]{1,0:T(8,128)}, u32[]{:S(2)}) copy-start(f32[8,768]{1,0:T(8,128)} %get-tuple-element.74) | copy-start | bytes 73732
  374.7 22.3 %copy-start.15 = (bf16[1024,768]{1,0:T(8,128)(2,1)S(1)}, bf16[1024,768]{1,0:T(8,128)(2,1)}, u32[]{:S(2)}) copy-start(bf16[1024,768]{1,0:T(8,128)(2,1)} %get-tuple-element.53) | copy-start | bytes 4718596
  374.7 22.3 %copy-start.16 = (bf16[1024,768]{1,0:T(8,128)(2,1)S(1)}, bf16[1024,768]{1,0:T(8,128)(2,1)}, u32[]{:S(2)}) copy-start(bf16[1024,768]{1,0:T(8,128)(2,1)} %get-tuple-element.58) | copy-start | bytes 4718596
  393.1 11.1 %all-to-all-start.6 = ((f32[32,1,256]{2,1,0:T(1,128)}), f32[32,1,256]{2,1,0:T(1,128)S(1)}, u32[]{:S(2)}, u32[]{:S(2)}) async-start(f32[32,1,256]{2,1,0:T(1,128)} %copy.155), calls=%async_computation.6 | async-start | bytes 65536 | tf_op jit(solution)/shard_map/all_to_all | solution.py:769
  404.3 81.2 %all-to-all-start.3 = ((bf16[32,64,768]{2,1,0:T(8,128)(2,1)}), bf16[32,64,768]{2,1,0:T(8,128)(2,1)S(1)}, u32[]{:S(2)}, u32[]{:S(2)}) async-start(bf16[32,64,768]{2,1,0:T(8,128)(2,1)} %bitcast.186), calls=%async_computation.3 | async-start | bytes 6291456 | tf_op jit(solution)/shard_map/all_to_all | solution.py:641
  414.4 37.6 %collective-permute-start.9 = (bf16[4,2,24,1536]{3,2,0,1:T(8,128)(2,1)}, bf16[4,2,24,1536]{3,2,0,1:T(8,128)(2,1)}, u32[]{:S(2)}, u32[]{:S(2)}) collective-permute-start(bf16[4,2,24,1536]{3,2,0,1:T(8,128)(2,1)} %fusion.9), channel_id=1, source_target_pairs={{0,2},{1,3},{2,0},{3,1},{4,6},{5,7},{6,4},{7,5},{8,10},{9,11},{10,... | collective-permute-start | bytes 1769480 | tf_op jit(solution)/shard_map/ppermute | solution.py:607
  418.4 35.8 %copy-start.5 = (f32[384,1536]{1,0:T(8,128)S(1)}, f32[384,1536]{1,0:T(8,128)}, u32[]{:S(2)}) copy-start(f32[384,1536]{1,0:T(8,128)} %get-tuple-element.119) | copy-start | bytes 7077892
  419.9 34.3 %collective-permute-start.11 = (bf16[4,2,24,1536]{3,2,0,1:T(8,128)(2,1)S(1)}, bf16[4,2,24,1536]{3,2,0,1:T(8,128)(2,1)S(1)}, u32[]{:S(2)}, u32[]{:S(2)}) collective-permute-start(bf16[4,2,24,1536]{3,2,0,1:T(8,128)(2,1)S(1)} %fusion.10), channel_id=1, source_target_pairs={{0,4},{1,5},{2,6},{3,7},{4,0},{5,1},{6,2},{7,3},{8,12},{9,13},{10,... | collective-permute-start | bytes 1769480 | tf_op jit(solution)/shard_map/ppermute | solution.py:607
  453.7 10.6 %collective-permute-start.10 = (bf16[4,24,1536]{2,1,0:T(8,128)(2,1)S(1)}, bf16[4,24,1536]{2,1,0:T(8,128)(2,1)S(1)}, u32[]{:S(2)}, u32[]{:S(2)}) collective-permute-start(bf16[4,24,1536]{2,1,0:T(8,128)(2,1)S(1)} %fusion.12), channel_id=1, source_target_pairs={{0,4},{1,5},{2,6},{3,7},{4,0},{5,1},{6,2},{7,3},{8,12},{9,13},{10,... | collective-permute-start | bytes 884744 | tf_op jit(solution)/shard_map/ppermute | solution.py:607
  454.3 10.1 %collective-permute-start.12 = (bf16[4,24,1536]{2,1,0:T(8,128)(2,1)S(1)}, bf16[4,24,1536]{2,1,0:T(8,128)(2,1)S(1)}, u32[]{:S(2)}, u32[]{:S(2)}) collective-permute-start(bf16[4,24,1536]{2,1,0:T(8,128)(2,1)S(1)} %fusion.13), channel_id=1, source_target_pairs={{0,2},{1,3},{2,0},{3,1},{4,6},{5,7},{6,4},{7,5},{8,10},{9,11},{10,... | collective-permute-start | bytes 884744 | tf_op jit(solution)/shard_map/ppermute | solution.py:607
  465.4 30.0 %collective-permute-start.14 = (bf16[24,3072]{1,0:T(8,128)(2,1)}, bf16[24,3072]{1,0:T(8,128)(2,1)S(1)}, u32[]{:S(2)}, u32[]{:S(2)}) collective-permute-start(bf16[24,3072]{1,0:T(8,128)(2,1)} %pad_maximum_fusion.9), channel_id=1, source_target_pairs={{0,16},{1,17},{2,18},{3,19},{4,20},{5,21},{6,22},{7,23},{8,24},{9,... | collective-permute-start | bytes 442376 | tf_op jit(solution)/shard_map/ppermute | solution.py:607
  466.4 28.9 %collective-permute-start.15 = (bf16[24,3072]{1,0:T(8,128)(2,1)}, bf16[24,3072]{1,0:T(8,128)(2,1)S(1)}, u32[]{:S(2)}, u32[]{:S(2)}) collective-permute-start(bf16[24,3072]{1,0:T(8,128)(2,1)} %pad_maximum_fusion.10), channel_id=1, source_target_pairs={{0,24},{1,25},{2,26},{3,27},{4,28},{5,29},{6,30},{7,31},{8,0},{9,1... | collective-permute-start | bytes 442376 | tf_op jit(solution)/shard_map/ppermute | solution.py:607
  471.6 23.7 %collective-permute-start.13 = (bf16[24,3072]{1,0:T(8,128)(2,1)}, bf16[24,3072]{1,0:T(8,128)(2,1)}, u32[]{:S(2)}, u32[]{:S(2)}) collective-permute-start(bf16[24,3072]{1,0:T(8,128)(2,1)} %pad_maximum_fusion.8), channel_id=1, source_target_pairs={{0,8},{1,9},{2,10},{3,11},{4,12},{5,13},{6,14},{7,15},{8,16},{9,17... | collective-permute-start | bytes 442376 | tf_op jit(solution)/shard_map/ppermute | solution.py:607
  (19 other events, 75.1 us)
